TPU v7x, 32 devices: a whole 2x2x4 slice. The times are simulated.
32 devices in a mesh: utt: 4 (over x, core), seq: 8 (over z, y).
Axes of the slice: x: 2, y: 2, z: 4, core: 2. Of those that a mesh axis runs over, the one named last changes fastest.
Arguments:
- frames_in: bfloat16 [4, 1024, 1024], P('utt', 'seq'), may hold values from -6 to 6
- skip_in: bfloat16 [4, 1024, 1024], P('utt', 'seq'), may hold values from -6 to 6
- flow_times: float32 [4, 3], P('utt'), may hold values from 0 to 1
- frame_lengths: int32 [4, 3], P('utt'), may hold values from 1 to 512, 1024 in all within a row
- char_lengths: int32 [4, 3], P('utt'), may hold values from 64 to 255
- drop_mask: int32 [4, 1024], P('utt', 'seq'), may hold values from 0 to 1, as said below
- out_grad: bfloat16 [4, 1024, 1024], P('utt', 'seq'), may hold values from -6 to 6
- w_skip: bfloat16 [2048, 1024], replicated, may hold values from -0.125 to 0.125
- b_skip: float32 [1024], replicated, may hold values from -2 to 2
- w_mod: bfloat16 [1024, 6144], replicated, as said below
- b_mod: float32 [6144], replicated, may hold values from -1.6 to 1.6
- w_qkv: bfloat16 [1024, 3072], replicated, as said below
- b_qkv: float32 [3072], replicated, may hold values from -2 to 2
- w_out: bfloat16 [1024, 1024], replicated, may hold values from -3.5 to 3.5
- b_out: float32 [1024], replicated, may hold values from -2 to 2
- w_up: bfloat16 [1024, 4096], replicated, may hold values from -0.1875 to 0.1875
- b_up: float32 [4096], replicated, may hold values from -2 to 2
- w_down: bfloat16 [4096, 1024], replicated, may hold values from -0.09375 to 0.09375
- b_down: float32 [1024], replicated, may hold values from -2 to 2
Outputs:
- mixed_out: bfloat16 [4, 1024, 1024], P('utt', 'seq')
- grad_frames: bfloat16 [4, 1024, 1024], P('utt', 'seq')
- grad_skip: bfloat16 [4, 1024, 1024], P('utt', 'seq')
- grad_w_skip: float32 [2048, 1024], P('seq')
- grad_b_skip: float32 [1024], P('seq')
- grad_w_mod: float32 [1024, 6144], P('seq')
- grad_b_mod: float32 [6144], P('seq')
- grad_w_qkv: float32 [1024, 3072], P('seq')
- grad_b_qkv: float32 [3072], P('seq')
- grad_w_out: float32 [1024, 1024], P('seq')
- grad_b_out: float32 [1024], P('seq')
- grad_w_up: float32 [1024, 4096], P('seq')
- grad_b_up: float32 [4096], P('seq')
- grad_w_down: float32 [4096, 1024], P('seq')
- grad_b_down: float32 [1024], P('seq')
Inputs may be any that keep to these rules, and one draw needn't show every extreme that they name: `frame_lengths`: frames of each utterance of a group in frame order; they sum to 1024 and the longest has exactly 512. `drop_mask`: 1 where a frame's text condition is dropped. `w_qkv`: entries of magnitude at most 4 / sqrt(1024). `w_mod`: entries of magnitude at most 4 / sqrt(1024).
All inputs are finite; a program needn't handle non-finite values.
Results may differ from a plain program's by a relative error of at most 0.02.
Values may be sent and summed in bfloat16 or wider, within the bound.
A program may use at most 256 MiB of HBM per device.

v0:
```python
from functools import partial
import math

import jax
import jax.numpy as jnp
from jax import lax
from jax.experimental import pallas as pl
from jax.experimental.pallas import tpu as pltpu
from jax.sharding import PartitionSpec as P

HEADS = 16
HEAD_DIM = 64


HIGHEST_PRECISION = lax.Precision.HIGHEST
EPSILON = 1e-06


def layer_norm(values):
    average = jnp.mean(values, axis=-1, keepdims=True)
    centred = values - average
    spread = jnp.mean(centred * centred, axis=-1, keepdims=True)
    return centred * lax.rsqrt(spread + EPSILON)


def modulate(values, scale_part, shift_part):
    return layer_norm(values) * (1.0 + scale_part) + shift_part


def time_embed(flow_vals, model_width):
    half_dim = model_width // 2
    inverse = jnp.exp(-math.log(10000.0) * jnp.arange(half_dim, dtype=jnp.float32) / half_dim)
    angles = 1000.0 * flow_vals[:, None] * inverse[None, :]
    return jnp.concatenate([jnp.sin(angles), jnp.cos(angles)], axis=1)


def rotary_tables(position, head_size):
    half_dim = head_size // 2
    inverse = jnp.exp(
        -math.log(10000.0) * 2.0 * jnp.arange(half_dim, dtype=jnp.float32) / head_size
    )
    angles = position.astype(jnp.float32)[:, None] * inverse[None, :]
    return (jnp.cos(angles)[:, None, :], jnp.sin(angles)[:, None, :])


def rotate(tensor, angle_cos, angle_sin):
    half_dim = tensor.shape[-1] // 2
    leading = tensor[..., :half_dim]
    trailing = tensor[..., half_dim:]
    return jnp.concatenate(
        [leading * angle_cos - trailing * angle_sin, trailing * angle_cos + leading * angle_sin],
        axis=-1,
    )


def unrotate(gradient, angle_cos, angle_sin):
    half_dim = gradient.shape[-1] // 2
    leading = gradient[..., :half_dim]
    trailing = gradient[..., half_dim:]
    return jnp.concatenate(
        [leading * angle_cos + trailing * angle_sin, trailing * angle_cos - leading * angle_sin],
        axis=-1,
    )


def frame_tables(lengths, char_counts, first_frame, frame_count):
    utt_ends = jnp.cumsum(lengths)
    utt_starts = utt_ends - lengths
    frame_index = first_frame + jnp.arange(frame_count, dtype=jnp.int32)
    segment = jnp.sum((frame_index[:, None] >= utt_ends[None, :]).astype(jnp.int32), axis=1)
    member = segment[:, None] == jnp.arange(lengths.shape[0], dtype=jnp.int32)[None, :]
    position = frame_index - jnp.sum(jnp.where(member, utt_starts[None, :], 0), axis=1)
    prompt = jnp.sum(jnp.where(member, char_counts[None, :], 0), axis=1)
    return (segment, position, position >= prompt, member)


def key_segments(key_start, key_count, utt_ends):
    frame_index = key_start + jnp.arange(key_count, dtype=jnp.int32)
    return jnp.sum((frame_index[:, None] >= utt_ends[None, :]).astype(jnp.int32), axis=1)


def block_scores(queries, key_piece, query_segment, key_segment, usable):
    key_rows = key_piece.reshape(key_piece.shape[0], queries.shape[1], queries.shape[2])
    scores = (
        jnp.einsum("qhd,khd->hqk", queries, key_rows, preferred_element_type=jnp.float32) * 0.125
    )
    allowed = jnp.logical_and(query_segment[:, None] == key_segment[None, :], usable)
    return (jnp.where(allowed[None], jnp.exp(scores), 0.0), key_rows)


def over_blocks(block_fn, running, piece, key_start, shard_rows):
    key_count = piece.shape[1]
    shard_total = key_count // shard_rows
    group_size = max(1, min(shard_total, 1024 // shard_rows))
    while shard_total % group_size != 0:
        group_size = group_size - 1
    block_rows = group_size * shard_rows
    if block_rows == key_count:
        return block_fn(running, piece, key_start)

    def one_block(block_index, inner_state):
        portion = lax.dynamic_slice_in_dim(piece, block_index * block_rows, block_rows, 1)
        return block_fn(inner_state, portion, key_start + block_index * block_rows)

    return lax.fori_loop(0, key_count // block_rows, one_block, running)


def forward_piece(running, piece, key_start, usable, queries, query_segment, utt_ends):
    weighted, totals = running
    key_segment = key_segments(key_start, piece.shape[1], utt_ends)
    weights, key_rows = block_scores(queries, piece[0], query_segment, key_segment, usable)
    value_rows = piece[1].reshape(key_rows.shape)
    totals = totals + jnp.sum(weights, axis=2)
    weighted = weighted + jnp.einsum(
        "hqk,khd->qhd", weights.astype(jnp.bfloat16), value_rows, preferred_element_type=jnp.float32
    )
    return (weighted, totals)


def backward_piece(piece, key_start, usable, queries, query_segment, utt_ends, grad_acc, delta):
    key_count = piece.shape[1]
    key_segment = key_segments(key_start, key_count, utt_ends)
    weights, key_rows = block_scores(queries, piece[0], query_segment, key_segment, usable)
    value_rows = piece[1].reshape(key_rows.shape)
    value_dots = jnp.einsum(
        "qhd,khd->hqk", grad_acc, value_rows, preferred_element_type=jnp.float32
    )
    d_scores = (weights * (value_dots - delta[:, :, None])).astype(jnp.bfloat16)
    d_query = (
        jnp.einsum("hqk,khd->qhd", d_scores, key_rows, preferred_element_type=jnp.float32) * 0.125
    )
    d_key = (
        jnp.einsum("hqk,qhd->khd", d_scores, queries, preferred_element_type=jnp.float32) * 0.125
    )
    d_value = jnp.einsum(
        "hqk,qhd->khd", weights.astype(jnp.bfloat16), grad_acc, preferred_element_type=jnp.float32
    )
    return (
        d_query,
        jnp.stack([d_key.reshape(key_count, -1), d_value.reshape(key_count, -1)], axis=0),
    )


def back_product(gradient_rows, matrix):
    return jnp.einsum("fo,io->fi", gradient_rows, matrix, preferred_element_type=jnp.float32)


def xor_permute(value, axis_name, bit):
    size = lax.axis_size(axis_name)
    return lax.ppermute(value, axis_name, [(i, i ^ bit) for i in range(size)])


def bits_of(axis_name):
    size, bits, bit = lax.axis_size(axis_name), [], 1
    while bit < size:
        bits.append(bit)
        bit *= 2
    return bits


def xor_sum(value, axis_name):
    for bit in bits_of(axis_name):
        value = value + xor_permute(value, axis_name, bit)
    return value


def gather_left(rows):
    for bit in reversed(bits_of("utt")):
        rows = jnp.concatenate([rows, xor_permute(rows, "utt", bit)], axis=0)
    return rows


def gather_right(rows):
    place = lax.axis_index("utt")
    for bit in reversed(bits_of("utt")):
        mine = (place & bit) // bit
        width = rows.shape[1] // 2
        kept = lax.dynamic_slice_in_dim(rows, mine * width, width, 1)
        given = lax.dynamic_slice_in_dim(rows, (1 - mine) * width, width, 1)
        rows = jnp.concatenate([kept, xor_permute(given, "utt", bit)], axis=0)
    return rows


def gather_ordered(value, axis):
    place = lax.axis_index("utt")
    for bit in bits_of("utt"):
        other = xor_permute(value, "utt", bit)
        low = (place & bit) == 0
        value = jnp.concatenate(
            [jnp.where(low, value, other), jnp.where(low, other, value)], axis=axis
        )
    return value


def scatter_rows(tile):
    place = lax.axis_index("seq")
    for bit in bits_of("seq"):
        mine = (place & bit) // bit
        rest = lax.axis_size("seq") // (2 * bit)
        pieces = tile.reshape(rest, 2, -1, tile.shape[-1])
        kept = lax.dynamic_index_in_dim(pieces, mine, 1, keepdims=False)
        given = lax.dynamic_index_in_dim(pieces, 1 - mine, 1, keepdims=False)
        given = xor_permute(given, "seq", bit)
        tile = (kept.astype(jnp.float32) + given.astype(jnp.float32)).astype(jnp.bfloat16)
    return tile.reshape(-1, tile.shape[-1])


def weight_grad(left_all, right_rows):
    right_all = gather_right(right_rows)
    tile = jnp.einsum(
        "fi,fo->io", left_all, right_all, preferred_element_type=jnp.float32
    ).astype(jnp.bfloat16)
    tile = tile.reshape(-1, tile.shape[-1])
    piece = scatter_rows(tile)
    return gather_ordered(piece, 1).astype(jnp.float32)


def swap_halves(values, lower):
    return jnp.where(lower, pltpu.roll(values, 96, 1), pltpu.roll(values, 32, 1))


def lower_half(shape):
    return lax.broadcasted_iota(jnp.int32, shape, 1) % HEAD_DIM < HEAD_DIM // 2


def rotate_pack_kernel(q_ref, k_ref, v_ref, cos_ref, sin_ref, out_ref):
    lower = lower_half(q_ref.shape)
    cos, sin = cos_ref[...], sin_ref[...]
    q, k = q_ref[...], k_ref[...]
    out_ref[0, :, 0:128] = (q * cos + swap_halves(q, lower) * sin).astype(jnp.bfloat16)
    out_ref[0, :, 128:256] = (k * cos + swap_halves(k, lower) * sin).astype(jnp.bfloat16)
    out_ref[0, :, 256:384] = v_ref[...].astype(jnp.bfloat16)


def rotate_pack(qkv_full, cos, sin):
    rows = qkv_full.shape[0]
    blocks = qkv_full.shape[1] // 384
    table = pl.BlockSpec((rows, 128), lambda i: (0, 0))
    return pl.pallas_call(
        rotate_pack_kernel,
        grid=(blocks,),
        in_specs=[
            pl.BlockSpec((rows, 128), lambda i: (0, i)),
            pl.BlockSpec((rows, 128), lambda i: (0, blocks + i)),
            pl.BlockSpec((rows, 128), lambda i: (0, 2 * blocks + i)),
            table,
            table,
        ],
        out_specs=pl.BlockSpec((1, rows, 384), lambda i: (i, 0, 0)),
        out_shape=jax.ShapeDtypeStruct((blocks, rows, 384), jnp.bfloat16),
    )(qkv_full, qkv_full, qkv_full, cos, sin)


def head_scores(q, k, seg_q, seg_k):
    scores = lax.dot_general(q, k, (((1,), (1,)), ((), ())), preferred_element_type=jnp.float32)
    return jnp.where(seg_q == seg_k, jnp.exp(scores * 0.125), 0.0)


MESH = pl.DeviceIdType.MESH
VMEM_LIMIT = 60 * 1024 * 1024


def flip(index, bit):
    return index + bit - 2 * bit * ((index // bit) % 2)


def everywhere(memory):
    return pl.BlockSpec(memory_space=memory)


class Links:
    def __init__(self, send_sems, recv_sems, local_sems):
        self.send_sems, self.recv_sems, self.local_sems = send_sems, recv_sems, local_sems
        self.sent, self.held = [], 0
        self.utt, self.seq = lax.axis_index("utt"), lax.axis_index("seq")

    def enter(self, utt_peers, seq_peers):
        barrier = pltpu.get_barrier_semaphore()
        targets = [self.mate(r) for r in utt_peers] + [self.peer(r) for r in seq_peers]
        for target in targets:
            pl.semaphore_signal(barrier, inc=1, device_id=target, device_id_type=MESH)
        pl.semaphore_wait(barrier, len(targets))

    def mate(self, offset):
        return (self.utt_of(offset), self.seq)

    def utt_of(self, offset):
        place = self.utt
        for bit in (1, 2):
            if offset & bit:
                place = flip(place, bit)
        return place

    def seq_of(self, offset):
        place = self.seq
        for bit in (1, 2, 4):
            if offset & bit:
                place = flip(place, bit)
        return place

    def peer(self, offset):
        return (self.utt, self.seq_of(offset))

    def send(self, source, target, device):
        index = len(self.sent)
        copy = pltpu.make_async_remote_copy(
            src_ref=source,
            dst_ref=target,
            send_sem=self.send_sems.at[index],
            recv_sem=self.recv_sems.at[index],
            device_id=device,
            device_id_type=MESH,
        )
        copy.start()
        self.sent.append(copy)
        return copy

    def keep(self, source, target):
        copy = pltpu.make_async_copy(source, target, self.local_sems.at[self.held])
        self.held += 1
        copy.start()
        return copy

    def leave(self):
        for copy in self.sent:
            copy.wait_send()


class Gathered:
    def __init__(self, links, source, target, columns=None):
        self.links, self.target = links, target
        self.rows = source.shape[0]
        self.columns = columns
        self.own = links.keep(source, self.slot(0))
        self.across = links.send(source, self.slot(2), links.mate(2))
        self.beside = links.send(source, self.slot(1), links.mate(1))

    def slot(self, offset):
        rows = pl.ds(offset * self.rows, self.rows)
        if self.columns is None:
            return self.target.at[rows, :]
        return self.target.at[rows, self.columns]

    def relay(self):
        self.across.wait_recv()
        self.relayed = self.links.send(self.slot(2), self.slot(3), self.links.mate(1))

    def wait(self):
        self.own.wait()
        self.beside.wait_recv()
        self.relayed.wait_recv()


class Quarter:
    def __init__(self, links, piece_of, target):
        rows = target.shape[0] // 4
        slot = lambda r: target.at[pl.ds(r * rows, rows), :]
        self.own = links.keep(piece_of(links.utt), slot(0))
        self.copies = [
            links.send(piece_of(links.utt_of(r)), slot(r), links.mate(r)) for r in (2, 3, 1)
        ]

    def wait(self):
        self.own.wait()
        for copy in self.copies:
            copy.wait_recv()


class Share:
    def __init__(self, links, left, right, columns, tile, got_y, got_z1, got_z2, result):
        self.links = links
        self.left, self.right, self.columns = left, right, columns
        self.tile, self.got_y, self.got_z1, self.got_z2 = tile, got_y, got_z1, got_z2
        self.result = result
        seq = links.seq
        self.y, self.zl, self.zh = seq % 2, (seq // 2) % 2, seq // 4

    def product(self, y):
        rows = self.tile.shape[3]

        def block(z, _):
            base = pl.multiple_of((2 * z + y) * rows, rows)
            self.tile[z // 2, z % 2, y] = lax.dot_general(
                self.left[:, pl.ds(base, rows)],
                self.right[:, self.columns],
                (((0,), (0,)), ((), ())),
                preferred_element_type=jnp.float32,
            ).astype(jnp.bfloat16)
            return 0

        lax.fori_loop(0, 4, block, 0)

    def start(self):
        self.product(1 - self.y)
        self.sent_y = self.links.send(
            self.tile.at[:, :, 1 - self.y], self.got_y, self.links.peer(1)
        )
        self.product(self.y)

    def add(self, index, got):
        tile = self.tile
        tile[index] = (tile[index].astype(jnp.float32) + got.astype(jnp.float32)).astype(
            jnp.bfloat16
        )

    def after_y(self):
        self.sent_y.wait_recv()

        def block(zh, _):
            self.add((zh, 1 - self.zl, self.y), self.got_y[zh, 1 - self.zl])
            return 0

        lax.fori_loop(0, 2, block, 0)
        self.sent_z1 = self.links.send(
            self.tile.at[:, 1 - self.zl, self.y], self.got_z1, self.links.peer(2)
        )

        def rest(zh, _):
            self.add((zh, self.zl, self.y), self.got_y[zh, self.zl])
            return 0

        lax.fori_loop(0, 2, rest, 0)

    def after_z1(self):
        self.sent_z1.wait_recv()
        self.add((1 - self.zh, self.zl, self.y), self.got_z1[1 - self.zh])
        self.sent_z2 = self.links.send(
            self.tile.at[1 - self.zh, self.zl, self.y], self.got_z2, self.links.peer(4)
        )
        self.add((self.zh, self.zl, self.y), self.got_z1[self.zh])

    def after_z2(self):
        self.sent_z2.wait_recv()
        links = self.links
        mine = self.result(links.utt)
        mine[...] = (
            self.tile[self.zh, self.zl, self.y].astype(jnp.float32)
            + self.got_z2[...].astype(jnp.float32)
        ).astype(jnp.bfloat16)
        self.across = links.send(mine, mine, links.mate(2))
        self.beside = links.send(mine, mine, links.mate(1))

    def relay(self):
        self.across.wait_recv()
        links = self.links
        theirs = self.result(links.utt_of(2))
        self.relayed = links.send(theirs, theirs, links.mate(1))

    def wait(self):
        self.beside.wait_recv()
        self.relayed.wait_recv()


def share_scratch(rows, columns):
    return [
        pltpu.VMEM((2, 2, 2, rows, columns), jnp.bfloat16),
        pltpu.VMEM((2, 2, rows, columns), jnp.bfloat16),
        pltpu.VMEM((2, rows, columns), jnp.bfloat16),
        pltpu.VMEM((rows, columns), jnp.bfloat16),
    ]


def run_shares(shares):
    stages = ("after_y", "after_z1", "after_z2", "relay", "wait")
    for turn in range(len(shares) + len(stages) - 1):
        for place, stage in enumerate(stages):
            if 0 <= turn - place < len(shares):
                getattr(shares[turn - place], stage)()


def semaphores(count):
    return [pltpu.SemaphoreType.DMA((count,))] * 2 + [pltpu.SemaphoreType.DMA((16,))]


def comm_params(collective_id):
    return pltpu.CompilerParams(
        collective_id=collective_id, has_side_effects=True, vmem_limit_bytes=VMEM_LIMIT
    )


def attend_kernel(
    packed_ref, segq_ref, segk_ref, counts_ref, flow_ref, norm_ref, frames_ref, skip_ref,
    attn_ref, heads_ref, exact_ref, total_ref, sums_ref, flows_ref, norm_all, joined_all,
    attn_heads, counts_got, send_sems, recv_sems, local_sems,
):
    links = Links(send_sems, recv_sems, local_sems)
    links.enter((1, 2, 3), range(1, 8))
    rows = packed_ref.shape[1]
    width = frames_ref.shape[1]
    own_rows = pl.ds(pl.multiple_of(links.seq * rows, rows), rows)
    own = links.keep(packed_ref.at[links.seq], heads_ref.at[own_rows, :])
    incoming = [
        links.send(packed_ref.at[links.seq_of(r)], heads_ref.at[own_rows, :], links.peer(r))
        for r in (6, 7, 4, 5, 2, 3, 1)
    ]
    flows_ref[links.utt] = flow_ref[...]
    flow_copies = [
        links.send(flow_ref, flows_ref.at[links.utt], links.mate(r)) for r in (1, 2, 3)
    ]
    gathers = [
        Gathered(links, norm_ref, norm_all),
        Gathered(links, frames_ref, joined_all, pl.ds(0, width)),
        Gathered(links, skip_ref, joined_all, pl.ds(width, width)),
    ]
    sums_ref[...] = counts_ref[...]
    for place, (target, source) in enumerate(
        ((links.mate(1), 0), (links.mate(2), 1), (links.peer(1), 2), (links.peer(2), 3),
         (links.peer(4), 4))
    ):
        counts_got[5 + place] = sums_ref[...]
        copy = links.send(counts_got.at[5 + place], counts_got.at[source], target)
        copy.wait_recv()
        sums_ref[...] = sums_ref[...] + counts_got[source]
    gathers[0].relay()
    own.wait()
    for copy in incoming:
        copy.wait_recv()
    first = lax.broadcasted_iota(jnp.int32, (256, 128), 1) < HEAD_DIM
    zero = jnp.zeros((256, 128), jnp.bfloat16)
    k, v = heads_ref[:, 128:256], heads_ref[:, 256:384]
    seg_k = segk_ref[...]

    def block(step, _):
        here = pl.ds(pl.multiple_of(step * 256, 256), 256)
        q, seg_q = heads_ref[here, 0:128], segq_ref[here, :]
        results = []
        for mine in (first, jnp.logical_not(first)):
            weights = head_scores(jnp.where(mine, q, zero), k, seg_q, seg_k)
            total = jnp.sum(weights, axis=1, keepdims=True)
            summed = jnp.dot(weights.astype(jnp.bfloat16), v, preferred_element_type=jnp.float32)
            results.append((summed, total))
        total = jnp.where(first, results[0][1], results[1][1])
        attended = jnp.where(first, results[0][0], results[1][0]) / total
        attn_heads[here, :] = attended.astype(jnp.bfloat16)
        exact_ref[here, :] = attended
        total_ref[here, :] = total
        return 0

    lax.fori_loop(0, heads_ref.shape[0] // 256, block, 0)
    column = attn_ref.at[:, pl.ds(pl.multiple_of(links.seq * 128, 128), 128)]
    part = lambda place: attn_heads.at[pl.ds(pl.multiple_of(place * rows, rows), rows), :]
    own = links.keep(part(links.seq), column)
    incoming = [
        links.send(part(links.seq_of(r)), column, links.peer(r)) for r in (6, 7, 4, 5, 2, 3, 1)
    ]
    for gather in gathers[1:]:
        gather.relay()
    for copy in flow_copies:
        copy.wait_recv()
    own.wait()
    for copy in incoming:
        copy.wait_recv()
    for gather in gathers:
        gather.wait()
    links.leave()


def attend(packed, seg_col, seg_row, counts, flow, norm_a, frames, skip):
    shards, rows, _ = packed.shape
    total_rows, width = shards * rows, norm_a.shape[1]
    vmem, there = everywhere(pltpu.VMEM), everywhere(pl.ANY)
    shape = jax.ShapeDtypeStruct
    return pl.pallas_call(
        attend_kernel,
        in_specs=[there, vmem, vmem, vmem, vmem, there, there, there],
        out_specs=[vmem] * 8,
        out_shape=[
            shape((rows, width), jnp.bfloat16),
            shape((total_rows, 384), jnp.bfloat16),
            shape((total_rows, 128), jnp.float32),
            shape((total_rows, 128), jnp.float32),
            shape(counts.shape, jnp.float32),
            shape((4,) + flow.shape, jnp.float32),
            shape((4 * rows, width), jnp.bfloat16),
            shape((4 * rows, 2 * width), jnp.bfloat16),
        ],
        scratch_shapes=[
            pltpu.VMEM((total_rows, 128), jnp.bfloat16),
            pltpu.VMEM((10,) + counts.shape, jnp.float32),
        ]
        + semaphores(40),
        compiler_params=comm_params(1),
    )(packed, seg_col, seg_row, counts, flow, norm_a, frames, skip)


def attend_back_kernel(
    d_attn_ref, heads_ref, segq_ref, segk_ref, exact_ref, total_ref, cos_ref, sin_ref,
    d_ff_ref, act_ref, norm_ref, d_inner_ref, attn_ref, d_branch_ref,
    d_qkv_ref, g_down, g_up, g_out,
    grad_heads, d_heads, dk_ref, dv_ref,
    d_ff_all, act_all, norm_all, d_inner_all, attn_all, d_branch_all,
    *rest,
):
    tiles, (send_sems, recv_sems, local_sems) = rest[:-3], rest[-3:]
    links = Links(send_sems, recv_sems, local_sems)
    links.enter((1, 2, 3), range(1, 8))
    rows = d_attn_ref.shape[0]
    far_first = (6, 7, 4, 5, 2, 3, 1)
    own_rows = pl.ds(pl.multiple_of(links.seq * rows, rows), rows)
    strip = lambda ref, place, size: ref.at[
        :, pl.ds(pl.multiple_of(place * size, size), size)
    ]
    own = links.keep(strip(d_attn_ref, links.seq, 128), grad_heads.at[own_rows, :])
    incoming = [
        links.send(
            strip(d_attn_ref, links.seq_of(r), 128), grad_heads.at[own_rows, :], links.peer(r)
        )
        for r in far_first
    ]
    gather_d = Gathered(links, d_ff_ref, d_ff_all)
    quarter_a = Quarter(links, lambda u: act_ref.at[u], act_all)
    gather_n = Gathered(links, norm_ref, norm_all)
    width = d_inner_all.shape[1]
    quarter_i = Quarter(links, lambda u: strip(d_inner_ref, u, width), d_inner_all)
    gather_b = Gathered(links, attn_ref, attn_all)
    narrow = d_branch_all.shape[1]
    quarter_b = Quarter(links, lambda u: strip(d_branch_ref, u, narrow), d_branch_all)
    own.wait()
    for copy in incoming:
        copy.wait_recv()
    dk_ref[...] = jnp.zeros_like(dk_ref)
    dv_ref[...] = jnp.zeros_like(dv_ref)
    first = lax.broadcasted_iota(jnp.int32, (256, 128), 1) < HEAD_DIM
    zero = jnp.zeros((256, 128), jnp.bfloat16)
    lower = lower_half((256, 128))
    k, v = heads_ref[:, 128:256], heads_ref[:, 256:384]
    seg_k = segk_ref[...]
    along = (((1,), (1,)), ((), ()))
    down = (((0,), (0,)), ((), ()))

    def turned(values, here):
        return (
            values * cos_ref[here, :] - swap_halves(values, lower) * sin_ref[here, :]
        ).astype(jnp.bfloat16)

    def block(step, _):
        here = pl.ds(pl.multiple_of(step * 256, 256), 256)
        q, seg_q = heads_ref[here, 0:128], segq_ref[here, :]
        scaled = grad_heads[here, :].astype(jnp.float32) / total_ref[here, :]
        grad_acc = scaled.astype(jnp.bfloat16)
        product = scaled * exact_ref[here, :]
        d_query = []
        for mine in (first, jnp.logical_not(first)):
            q_own = jnp.where(mine, q, zero)
            g_own = jnp.where(mine, grad_acc, zero)
            delta = jnp.sum(jnp.where(mine, product, 0.0), axis=1, keepdims=True)
            weights = head_scores(q_own, k, seg_q, seg_k)
            dots = lax.dot_general(g_own, v, along, preferred_element_type=jnp.float32)
            d_scores = (weights * (dots - delta)).astype(jnp.bfloat16)
            d_query.append(jnp.dot(d_scores, k, preferred_element_type=jnp.float32))
            dk_ref[...] += lax.dot_general(
                d_scores, q_own, down, preferred_element_type=jnp.float32
            )
            dv_ref[...] += lax.dot_general(
                weights.astype(jnp.bfloat16), g_own, down, preferred_element_type=jnp.float32
            )
        d_heads[here, 0:128] = turned(jnp.where(first, d_query[0], d_query[1]) * 0.125, here)
        return 0

    blocks = heads_ref.shape[0] // 256
    lax.fori_loop(0, blocks, block, 0)

    def finish(step, _):
        here = pl.ds(pl.multiple_of(step * 256, 256), 256)
        d_heads[here, 128:256] = turned(dk_ref[here, :] * 0.125, here)
        d_heads[here, 256:384] = dv_ref[here, :].astype(jnp.bfloat16)
        return 0

    lax.fori_loop(0, blocks, finish, 0)
    model = d_attn_ref.shape[1]
    part = lambda place, c: d_heads.at[
        pl.ds(pl.multiple_of(place * rows, rows), rows), pl.ds(c * 128, 128)
    ]
    home = lambda c: d_qkv_ref.at[
        :, pl.ds(pl.multiple_of(c * model + links.seq * 128, 128), 128)
    ]
    owns = [links.keep(part(links.seq, c), home(c)) for c in range(3)]
    incoming = [
        links.send(part(links.seq_of(r), c), home(c), links.peer(r))
        for r in far_first
        for c in range(3)
    ]
    half = width // 2
    shares = []
    for index, (left, right, columns, result) in enumerate(
        (
            (act_all, d_ff_all, 0, lambda u: g_down.at[
                pl.ds(pl.multiple_of(u * 128, 128), 128), pl.ds(0, half)]),
            (act_all, d_ff_all, 1, lambda u: g_down.at[
                pl.ds(pl.multiple_of(u * 128, 128), 128), pl.ds(half, half)]),
            (norm_all, d_inner_all, 0, lambda u: g_up.at[
                :, pl.ds(pl.multiple_of(u * width, width), half)]),
            (norm_all, d_inner_all, 1, lambda u: g_up.at[
                :, pl.ds(pl.multiple_of(u * width + half, half), half)]),
        )
    ):
        shares.append(
            Share(links, left, right, pl.ds(columns * half, half),
                  *tiles[4 * index : 4 * index + 4], result)
        )
    shares.append(
        Share(links, attn_all, d_branch_all, pl.ds(0, narrow), *tiles[16:20],
              lambda u: g_out.at[:, pl.ds(pl.multiple_of(u * narrow, narrow), narrow)])
    )
    gather_d.relay()
    gather_n.relay()
    gather_d.wait()
    quarter_a.wait()
    shares[0].start()
    shares[1].start()
    gather_b.relay()
    gather_n.wait()
    quarter_i.wait()
    shares[2].start()
    shares[3].start()
    gather_b.wait()
    quarter_b.wait()
    shares[4].start()
    run_shares(shares)
    for copy in owns:
        copy.wait()
    for copy in incoming:
        copy.wait_recv()
    links.leave()


def attend_back(
    d_attn, heads, seg_col, seg_row, exact, total, cos, sin,
    d_ff, act_quarters, norm_f, d_inner, attn_b, d_branch,
):
    rows, model = d_attn.shape
    frames = heads.shape[0]
    inner = d_inner.shape[1]
    vmem, there = everywhere(pltpu.VMEM), everywhere(pl.ANY)
    shape = jax.ShapeDtypeStruct
    bf16 = lambda *dims: pltpu.VMEM(dims, jnp.bfloat16)
    half = inner // 8
    return pl.pallas_call(
        attend_back_kernel,
        in_specs=[there] + [vmem] * 7 + [there] * 6,
        out_specs=[vmem] * 4,
        out_shape=[
            shape((rows, 3 * model), jnp.bfloat16),
            shape((inner // 8, model), jnp.bfloat16),
            shape((model // 8, inner), jnp.bfloat16),
            shape((model // 8, model), jnp.bfloat16),
        ],
        scratch_shapes=[
            bf16(frames, 128),
            bf16(frames, 384),
            pltpu.VMEM((frames, 128), jnp.float32),
            pltpu.VMEM((frames, 128), jnp.float32),
            bf16(4 * rows, model),
            bf16(4 * rows, inner // 4),
            bf16(4 * rows, model),
            bf16(4 * rows, inner // 4),
            bf16(4 * rows, model),
            bf16(4 * rows, model // 4),
        ]
        + share_scratch(128, half) * 4
        + share_scratch(model // 8, model // 4)
        + semaphores(80),
        compiler_params=comm_params(2),
    )(
        d_attn, heads, seg_col, seg_row, exact, total, cos, sin,
        d_ff, act_quarters, norm_f, d_inner, attn_b, d_branch,
    )


def last_kernel(
    norm_all, joined_all, d_qkv_ref, d_resid_ref, small_ref,
    g_qkv, g_skip, smalls,
    d_qkv_all, d_resid_all, small_got, small_sum, *rest,
):
    tiles, (send_sems, recv_sems, local_sems) = rest[:-3], rest[-3:]
    links = Links(send_sems, recv_sems, local_sems)
    links.enter((1, 2, 3), (1, 2, 4))
    strip = lambda ref, place, size: ref.at[
        :, pl.ds(pl.multiple_of(place * size, size), size)
    ]
    wide, narrow = d_qkv_all.shape[1], d_resid_all.shape[1]
    quarter_q = Quarter(links, lambda u: strip(d_qkv_ref, u, wide), d_qkv_all)
    quarter_r = Quarter(links, lambda u: strip(d_resid_ref, u, narrow), d_resid_all)
    exchange = [links.send(small_ref, small_got.at[0], links.peer(1))]
    half = wide // 2
    shares = [
        Share(links, norm_all, d_qkv_all, pl.ds(0, half), *tiles[0:4],
              lambda u: g_qkv.at[:, pl.ds(pl.multiple_of(u * wide, 128), half)]),
        Share(links, norm_all, d_qkv_all, pl.ds(half, half), *tiles[4:8],
              lambda u: g_qkv.at[:, pl.ds(pl.multiple_of(u * wide + half, 128), half)]),
        Share(links, joined_all, d_resid_all, pl.ds(0, narrow), *tiles[8:12],
              lambda u: g_skip.at[:, pl.ds(pl.multiple_of(u * narrow, narrow), narrow)]),
    ]
    quarter_q.wait()
    shares[0].start()
    shares[1].start()
    quarter_r.wait()
    shares[2].start()
    exchange[0].wait_recv()
    small_sum[0] = small_ref[...] + small_got[0]
    exchange.append(links.send(small_sum.at[0], small_got.at[1], links.peer(2)))
    shares[0].after_y()
    exchange[1].wait_recv()
    small_sum[1] = small_sum[0] + small_got[1]
    exchange.append(links.send(small_sum.at[1], small_got.at[2], links.peer(4)))
    shares[1].after_y()
    shares[0].after_z1()
    exchange[2].wait_recv()
    mine = smalls.at[links.utt]
    mine[...] = small_sum[1] + small_got[2]
    spread = [links.send(mine, mine, links.mate(r)) for r in (2, 3, 1)]
    shares[2].after_y()
    shares[1].after_z1()
    shares[0].after_z2()
    shares[2].after_z1()
    shares[1].after_z2()
    shares[0].relay()
    shares[2].after_z2()
    shares[1].relay()
    shares[0].wait()
    shares[2].relay()
    shares[1].wait()
    shares[2].wait()
    for copy in spread:
        copy.wait_recv()
    links.leave()


def last(norm_all, joined_all, d_qkv, d_resid, small):
    rows, model = d_resid.shape
    vmem, there = everywhere(pltpu.VMEM), everywhere(pl.ANY)
    shape = jax.ShapeDtypeStruct
    bf16 = lambda *dims: pltpu.VMEM(dims, jnp.bfloat16)
    wide = d_qkv.shape[1] // 4
    return pl.pallas_call(
        last_kernel,
        in_specs=[vmem, vmem, there, there, vmem],
        out_specs=[vmem] * 3,
        out_shape=[
            shape((model // 8, 4 * wide), jnp.bfloat16),
            shape((model // 4, model), jnp.bfloat16),
            shape((4,) + small.shape, jnp.float32),
        ],
        scratch_shapes=[
            bf16(4 * rows, wide),
            bf16(4 * rows, model // 4),
            pltpu.VMEM((3,) + small.shape, jnp.float32),
            pltpu.VMEM((2,) + small.shape, jnp.float32),
        ]
        + share_scratch(model // 8, wide // 2) * 2
        + share_scratch(model // 4, model // 4)
        + semaphores(48),
        compiler_params=comm_params(3),
    )(norm_all, joined_all, d_qkv, d_resid, small)


def wide_tables(position):
    half_dim = HEAD_DIM // 2
    lane = jnp.arange(128, dtype=jnp.int32) % HEAD_DIM
    inverse = jnp.exp(
        -math.log(10000.0) * 2.0 * (lane % half_dim).astype(jnp.float32) / HEAD_DIM
    )
    angles = position.astype(jnp.float32)[:, None] * inverse[None, :]
    sign = jnp.where(lane < half_dim, -1.0, 1.0)
    return jnp.cos(angles), jnp.sin(angles) * sign[None, :]


def local(
    frames_in,
    skip_in,
    flow_times,
    frame_lengths,
    char_lengths,
    drop_mask,
    out_grad,
    w_skip,
    b_skip,
    w_mod,
    b_mod,
    w_qkv,
    b_qkv,
    w_out,
    b_out,
    w_up,
    b_up,
    w_down,
    b_down,
):
    local_rows = frames_in.shape[1]
    model_width = frames_in.shape[2]
    shards = lax.axis_size("seq")
    seq_place = lax.axis_index("seq")
    lengths = frame_lengths[0]
    utt_ends = jnp.cumsum(lengths)
    segment, position, in_loss, member = frame_tables(
        lengths, char_lengths[0], seq_place * local_rows, local_rows
    )
    member_f = member.astype(jnp.float32)
    loss_mask = in_loss.astype(jnp.float32)
    dropped = drop_mask[0].astype(jnp.float32)
    counts = jnp.stack([jnp.sum(loss_mask * dropped), jnp.sum(loss_mask * (1.0 - dropped))])
    counts = jnp.pad(counts[None, :], ((0, 7), (0, 126)))
    whole = model_width * 4
    fused = (
        lax.axis_size("utt") == 4
        and shards == 8
        and HEADS * HEAD_DIM == 1024
        and w_up.shape[1] == whole
        and local_rows == 128
    )
    if not fused:
        counts = xor_sum(xor_sum(counts, "utt"), "seq")
    time_act = jax.nn.silu(time_embed(flow_times[0], model_width)).astype(jnp.bfloat16)
    mod_u = jnp.dot(time_act, w_mod, preferred_element_type=jnp.float32) + b_mod
    mod_f = jnp.dot(member_f, mod_u, precision=HIGHEST_PRECISION)
    shift_a, scale_a, gate_a, shift_f, scale_f, gate_f = jnp.split(mod_f, 6, axis=1)
    joined = jnp.concatenate([frames_in[0], skip_in[0]], axis=1)
    residual = jnp.dot(joined, w_skip, preferred_element_type=jnp.float32) + b_skip
    norm_a = modulate(residual, scale_a, shift_a).astype(jnp.bfloat16)
    qkv_full = jnp.dot(norm_a, w_qkv, preferred_element_type=jnp.float32) + b_qkv
    if fused:
        all_segment, all_position, _, _ = frame_tables(
            lengths, char_lengths[0], 0, local_rows * shards
        )
        cos_all, sin_all = wide_tables(all_position)
        cos_own, sin_own = wide_tables(position)
        seg_col, seg_row = all_segment[:, None], all_segment[None, :]
        flow = jnp.pad(flow_times, ((0, 7), (0, 128 - flow_times.shape[1])))
        attn_b, qkv_heads, exact, total, counts, flows, norm_all, joined_all = attend(
            rotate_pack(qkv_full, cos_own, sin_own),
            seg_col,
            seg_row,
            counts,
            flow,
            norm_a,
            frames_in[0],
            skip_in[0],
        )
    else:
        angle_cos, angle_sin = rotary_tables(position, HEAD_DIM)
        queries = rotate(
            qkv_full[:, :model_width].reshape(local_rows, HEADS, HEAD_DIM), angle_cos, angle_sin
        ).astype(jnp.bfloat16)
        key_rot = rotate(
            qkv_full[:, model_width : 2 * model_width].reshape(local_rows, HEADS, HEAD_DIM),
            angle_cos,
            angle_sin,
        ).astype(jnp.bfloat16)
        key_value = jnp.stack(
            [
                key_rot.reshape(local_rows, model_width),
                qkv_full[:, 2 * model_width :].astype(jnp.bfloat16),
            ],
            axis=0,
        )
        start_state = (
            jnp.zeros((local_rows, HEADS, HEAD_DIM), jnp.float32),
            jnp.zeros((HEADS, local_rows), jnp.float32),
        )
        fwd_piece = partial(forward_piece, queries=queries, query_segment=segment, utt_ends=utt_ends)
        weighted, totals = over_blocks(
            partial(fwd_piece, usable=True),
            start_state,
            lax.all_gather(key_value, "seq", axis=1, tiled=True),
            jnp.int32(0),
            local_rows,
        )
        totals_rows = jnp.transpose(totals)
        attended = weighted / totals_rows[:, :, None]
        attn_b = attended.reshape(local_rows, model_width).astype(jnp.bfloat16)
    n_drop, n_keep = counts[0, 0], counts[0, 1]
    loss_weight = (
        loss_mask
        * (n_drop + n_keep)
        * 0.5
        * (dropped / (n_drop + 1.0) + (1.0 - dropped) / (n_keep + 1.0))
    )
    branch = jnp.dot(attn_b, w_out, preferred_element_type=jnp.float32) + b_out
    mid_state = residual + gate_a * branch
    norm_f = modulate(mid_state, scale_f, shift_f).astype(jnp.bfloat16)
    ff_inner = jnp.dot(norm_f, w_up, preferred_element_type=jnp.float32) + b_up
    ff_act, gelu_pull = jax.vjp(partial(jax.nn.gelu, approximate=True), ff_inner)
    act_b = ff_act.astype(jnp.bfloat16)
    ff_out = jnp.dot(act_b, w_down, preferred_element_type=jnp.float32) + b_down
    out_state = mid_state + gate_f * ff_out
    d_out = out_grad[0].astype(jnp.float32) * loss_weight[:, None]
    d_ff = (gate_f * d_out).astype(jnp.bfloat16)
    d_gate_f = d_out * ff_out
    g_b_down = jnp.sum(d_ff.astype(jnp.float32), axis=0)
    (d_inner,) = gelu_pull(back_product(d_ff, w_down))
    d_inner_b = d_inner.astype(jnp.bfloat16)
    g_b_up = jnp.sum(d_inner_b.astype(jnp.float32), axis=0)
    d_norm_f = back_product(d_inner_b, w_up)
    _, norm_f_pull = jax.vjp(modulate, mid_state, scale_f, shift_f)
    d_mid_norm, d_scale_f, d_shift_f = norm_f_pull(d_norm_f)
    d_mid = d_out + d_mid_norm
    d_branch = (gate_a * d_mid).astype(jnp.bfloat16)
    d_gate_a = d_mid * branch
    g_b_out = jnp.sum(d_branch.astype(jnp.float32), axis=0)
    d_attn = back_product(d_branch, w_out)
    if fused:
        act_quarters = jnp.transpose(act_b.reshape(local_rows, shards, 4, -1), (2, 0, 1, 3))
        d_qkv, g_w_down, g_w_up, g_w_out = attend_back(
            d_attn.astype(jnp.bfloat16),
            qkv_heads,
            seg_col,
            seg_row,
            exact,
            total,
            cos_all,
            sin_all,
            d_ff,
            act_quarters.reshape(4, local_rows, -1),
            norm_f,
            d_inner_b,
            attn_b,
            d_branch,
        )
    else:
        g_w_down = weight_grad(gather_left(act_b), d_ff)
        g_w_up = weight_grad(gather_left(norm_f), d_inner_b)
        g_w_out = weight_grad(gather_left(attn_b), d_branch)
        d_attn = d_attn.reshape(local_rows, HEADS, HEAD_DIM)
        grad_acc = (d_attn / totals_rows[:, :, None]).astype(jnp.bfloat16)
        delta = jnp.transpose(jnp.sum(d_attn * attended, axis=2) / totals_rows)
        bwd_piece = partial(
            backward_piece,
            queries=queries,
            query_segment=segment,
            utt_ends=utt_ends,
            grad_acc=grad_acc,
            delta=delta,
        )
        zero_query = jnp.zeros((local_rows, HEADS, HEAD_DIM), jnp.float32)
        zero_all = jnp.zeros((2, local_rows * shards, model_width), jnp.float32)

        def block_fn(inner_state, portion, block_start):
            d_query_sum, d_all = inner_state
            d_query_add, d_block = bwd_piece(portion, block_start, True)
            return (
                d_query_sum + d_query_add,
                lax.dynamic_update_slice_in_dim(d_all, d_block, block_start, 1),
            )

        d_query, d_all = over_blocks(
            block_fn,
            (zero_query, zero_all),
            lax.all_gather(key_value, "seq", axis=1, tiled=True),
            jnp.int32(0),
            local_rows,
        )
        d_key_value = lax.psum_scatter(d_all, "seq", scatter_dimension=1, tiled=True)
        d_query_pre = unrotate(d_query, angle_cos, angle_sin).reshape(local_rows, model_width)
        d_key_pre = unrotate(
            d_key_value[0].reshape(local_rows, HEADS, HEAD_DIM), angle_cos, angle_sin
        ).reshape(local_rows, model_width)
        d_qkv = jnp.concatenate([d_query_pre, d_key_pre, d_key_value[1]], axis=1).astype(jnp.bfloat16)
    g_b_qkv = jnp.sum(d_qkv.astype(jnp.float32), axis=0)
    d_norm_a = back_product(d_qkv, w_qkv)
    _, norm_a_pull = jax.vjp(modulate, residual, scale_a, shift_a)
    d_resid_norm, d_scale_a, d_shift_a = norm_a_pull(d_norm_a)
    d_resid = (d_mid + d_resid_norm).astype(jnp.bfloat16)
    g_b_skip = jnp.sum(d_resid.astype(jnp.float32), axis=0)
    d_joined = back_product(d_resid, w_skip)
    d_mod_f = jnp.concatenate(
        [d_shift_a, d_scale_a, d_gate_a, d_shift_f, d_scale_f, d_gate_f], axis=1
    )
    d_mod_u = jnp.dot(jnp.transpose(member_f), d_mod_f, precision=HIGHEST_PRECISION)
    small = jnp.concatenate(
        [g_b_skip, g_b_qkv, g_b_out, g_b_up, g_b_down, d_mod_u.reshape(-1)]
    )
    biases = small.shape[0] - d_mod_u.size
    if fused:
        g_w_qkv, g_w_skip, smalls = last(
            norm_all, joined_all, d_qkv, d_resid, small.reshape(-1, 128)
        )
        smalls = smalls.reshape(4, -1)
        bias_sum = jnp.sum(smalls[:, :biases], axis=0)
        d_mod_all = smalls[:, biases:].reshape(-1, d_mod_u.shape[1])
        flow_all = flows[:, 0, : flow_times.shape[1]].reshape(-1)
        act_all = jax.nn.silu(time_embed(flow_all, model_width)).astype(jnp.bfloat16)
        g_w_skip, g_w_qkv, g_w_out, g_w_up, g_w_down = (
            grad.astype(jnp.float32) for grad in (g_w_skip, g_w_qkv, g_w_out, g_w_up, g_w_down)
        )
    else:
        g_w_qkv = weight_grad(gather_left(norm_a), d_qkv)
        g_w_skip = weight_grad(gather_left(joined), d_resid)
        small = xor_sum(small.reshape(-1, 128), "seq").reshape(-1)
        bias_sum = xor_sum(small[:biases].reshape(-1, 128), "utt").reshape(-1)
        d_mod_all = gather_ordered(small[biases:].reshape(d_mod_u.shape), 0)
        act_all = gather_ordered(time_act, 0)
    act_all = act_all.astype(jnp.float32)
    own_width = model_width // shards
    act_own = lax.dynamic_slice_in_dim(act_all, seq_place * own_width, own_width, 1)
    g_w_mod = jnp.dot(jnp.transpose(act_own), d_mod_all, precision=HIGHEST_PRECISION)
    mod_width = d_mod_all.shape[1] // shards
    g_b_mod = jnp.sum(
        lax.dynamic_slice_in_dim(d_mod_all, seq_place * mod_width, mod_width, 1), axis=0
    )
    own_biases, offset = [], 0
    for vector in (g_b_skip, g_b_qkv, g_b_out, g_b_up, g_b_down):
        width = vector.shape[0] // shards
        own_biases.append(
            lax.dynamic_slice_in_dim(bias_sum, offset + seq_place * width, width, 0)
        )
        offset += vector.shape[0]
    return (
        out_state.astype(jnp.bfloat16)[None],
        d_joined[:, :model_width].astype(jnp.bfloat16)[None],
        d_joined[:, model_width:].astype(jnp.bfloat16)[None],
        g_w_skip,
        own_biases[0],
        g_w_mod,
        g_b_mod,
        g_w_qkv,
        own_biases[1],
        g_w_out,
        own_biases[2],
        g_w_up,
        own_biases[3],
        g_w_down,
        own_biases[4],
    )


def solution(mesh):
    return jax.shard_map(
        local,
        mesh=mesh,
        in_specs=(
            P("utt", "seq", None),
            P("utt", "seq", None),
            P("utt", None),
            P("utt", None),
            P("utt", None),
            P("utt", "seq"),
            P("utt", "seq", None),
            P(),
            P(),
            P(),
            P(),
            P(),
            P(),
            P(),
            P(),
            P(),
            P(),
            P(),
            P(),
        ),
        out_specs=(
            P("utt", "seq", None),
            P("utt", "seq", None),
            P("utt", "seq", None),
            P("seq", None),
            P("seq"),
            P("seq", None),
            P("seq"),
            P("seq", None),
            P("seq"),
            P("seq", None),
            P("seq"),
            P("seq", None),
            P("seq"),
            P("seq", None),
            P("seq"),
        ),
        check_vma=False,
    )
```

profile of v0, /device:TPU:0, one launch (start us, length us, event | category | flops | bytes accessed | tf_op | source)
XLA Modules:
  0.0 319.5 jit_solution(15329465017917810609)
XLA Ops:
  0.7 3.3 %fusion.56 = (f32[128]{0:T(128)S(1)}, f32[128,1024]{1,0:T(8,128)S(1)}) fusion(f32[1024]{0:T(1024)} %param.27, bf16[2048,1024]{1,0:T(8,128)(2,1)} %param.26, bf16[128,1024]{1,0:T(8,128)(2,1)} %bitcast.92, bf16[128,1024]{1,0:T(8,128)(2,1)} %bitcast.94), kind=kOutput, calls=%fused_computation.146 | convolution fusion | flops 538181504 | bytes 5247488 | tf_op jit(solution)/shard_map/dot_general | solution.py:918
  4.2 6.3 %convolution_add_fusion = f32[3,6144]{1,0:T(4,128)S(1)} fusion(bf16[1024,6144]{1,0:T(8,128)(2,1)} %param.28, f32[6144]{0:T(1024)S(1)} %copy-done.25, f32[3,512]{1,0:T(4,128)S(1)} %get-tuple-element.83, f32[3,512]{1,0:T(4,128)S(1)} %get-tuple-element.82), kind=kOutput, calls=%fused_computation | convolution fusion | flops 37785600 | bytes 12693504 | tf_op jit(solution)/shard_map/dot_general | solution.py:914
  10.8 1.5 fusion.29
  12.5 1.4 copy-done.1
  14.1 5.0 %convolution_add_fusion.2.q_ref.k_ref.v_ref = f32[128,3072]{1,0:T(8,128)} fusion(bf16[128,1024]{1,0:T(8,128)(2,1)S(1)} %fusion.9.norm_ref, bf16[1024,3072]{1,0:T(8,128)(2,1)} %param.30, f32[3072]{0:T(1024)S(1)} %copy-done.26), kind=kOutput, calls=%fused_computation.2 | convolution fusion | flops 805699584 | bytes 8138752 | tf_op jit(solution)/shard_map/dot_general | solution.py:920
  20.3 5.9 %shard_map.298.packed_ref = bf16[8,128,384]{2,1,0:T(8,128)(2,1)} custom-call(f32[128,3072]{1,0:T(8,128)} %convolution_add_fusion.2.q_ref.k_ref.v_ref, f32[128,3072]{1,0:T(8,128)} %convolution_add_fusion.2.q_ref.k_ref.v_ref, f32[128,3072]{1,0:T(8,128)} %convolution_add_fusion.2.q_ref.k_ref.v_ref, f32[128,128]{1,0:T(8,128)} %get-tuple-element.85.cos_ref, ...), custom_call_target="tpu_custom_call" | custom-call | tf_op jit(solution)/shard_map/pallas_call | solution.py:239
  26.3 1.0 copy.38.segq_ref
  27.9 1.4 maximum_bitcast_fusion
  30.5 47.5 %shard_map.299 = (bf16[128,1024]{1,0:T(8,128)(2,1)}, bf16[1024,384]{1,0:T(8,128)(2,1)}, f32[1024,128]{1,0:T(8,128)}, f32[1024,128]{1,0:T(8,128)}, f32[8,128]{1,0...) custom-call(bf16[8,128,384]{2,1,0:T(8,128)(2,1)} %shard_map.298.packed_ref, ...), custom_call_target="tpu_custom_call" | custom-call | tf_op jit(solution)/shard_map/pallas_call | solution.py:563
  78.0 2.5 fusion.53
  80.6 1.3 fusion.55
  85.1 6.4 %fusion.57 = f32[128,4096]{1,0:T(8,128)S(1)} fusion(bf16[128,1024]{1,0:T(8,128)(2,1)S(1)} %get-tuple-element.50.d_ff_ref, bf16[4096,1024]{1,0:T(8,128)(2,1)} %param.36), kind=kOutput, calls=%fused_computation.147 | convolution fusion | flops 1073741824 | bytes 10747904 | tf_op jit(solution)/shard_map/fo,io->fi/dot_general | solution.py:145
  91.6 6.6 %convert_reduce_fusion = (f32[4096]{0:T(1024)S(1)}, bf16[128,4096]{1,0:T(8,128)(2,1)S(1)}, bf16[128,4096]{1,0:T(8,128)(2,1)S(1)}) fusion(f32[128,4096]{1,0:T(8,128)S(1)} %fusion.57, f32[4096]{0:T(1024)S(1)} %copy-done.32, bf16[128,1024]{1,0:T(8,128)(2,1)S(1)} %get-tuple-element.65.norm_ref, bf16[1024,4096]{1,0:T(8,128)(2,1)} %param.34), kind=kOutput, calls=%fused_computation.13 | convolution fusion | flops 1086844928 | bytes 12877824 | tf_op jit(solution)/shard_map/dot_general | solution.py:981
  98.3 3.0 multiply_reduce_fusion.1
  101.3 1.3 convolution_add_fusion.5
  103.8 1.6 convolution_convert_fusion.1.d_attn_ref
  105.5 3.3 %fusion.7 = (f32[1024,128]{1,0:T(8,128)}, f32[1024,128]{1,0:T(8,128)}) fusion(f32[128]{0:T(128)S(1)} %get-tuple-element.92, f32[128]{0:T(128)S(1)} %get-tuple-element.93, f32[1024]{0:T(1024)S(1)} %subtract_convert_fusion), kind=kLoop, calls=%fused_computation.24 | loop fusion | flops 262144 | bytes 1053696 | tf_op jit(solution)/shard_map/mul | solution.py:865
  108.8 2.6 reshape.210
  111.4 2.3 copy.39
  113.7 2.3 reshape.211.act_ref
  116.0 103.5 %shard_map.300 = (bf16[128,3072]{1,0:T(8,128)(2,1)}, bf16[512,1024]{1,0:T(8,128)(2,1)}, bf16[128,4096]{1,0:T(8,128)(2,1)}, bf16[128,1024]{1,0:T(8,128)(2,1)}) custom-call(bf16[128,1024]{1,0:T(8,128)(2,1)} %convolution_convert_fusion.1.d_attn_ref, bf16[1024,384]{1,0:T(8,128)(2,1)} %get-tuple-element.32.heads_ref, s32[1024,1]{1,0:T(8,128)} %copy.38.segq_ref, ...), custom_call_target="tpu_custom_call" | custom-call | tf_op jit(solution)/shard_map/pallas_call | solution.py:738
  219.6 5.5 %constant_dynamic-update-slice_fusion.1 = (f32[128,6144]{1,0:T(8,128)S(1)}, f32[128]{0:T(128)S(1)}, f32[128,1024]{1,0:T(8,128)S(1)}) fusion(f32[128,6144]{1,0:T(8,128)} %copy-done.1, f32[128,1024]{1,0:T(8,128)S(1)} %get-tuple-element.87, f32[128]{0:T(128)S(1)} %broadcast_multiply_fusion.1, bf16[128,3072]{1,0:T(8,128)(2,1)} %get-tuple-element.35.d_qkv_ref, ...), kind=kOutput, calls=%fused_computation.72 | convolution fusion | flops 805961600 | bytes 9176064 | tf_op jit(solution)/shard_map/fo,io->fi/dot_general | solution.py:145
  225.1 1.5 fusion.51
  227.4 1.5 convolution_convert_fusion
  230.3 1.1 fusion.28
  232.2 69.2 %shard_map.301 = (bf16[128,3072]{1,0:T(8,128)(2,1)}, bf16[256,1024]{1,0:T(8,128)(2,1)}, f32[4,224,128]{2,1,0:T(8,128)}) custom-call(bf16[512,1024]{1,0:T(8,128)(2,1)} %get-tuple-element.36.norm_all, bf16[512,2048]{1,0:T(8,128)(2,1)} %get-tuple-element.37.joined_all, bf16[128,3072]{1,0:T(8,128)(2,1)} %get-tuple-element.35.d_qkv_ref, ...), custom_call_target="tpu_custom_call" | custom-call | tf_op jit(solution)/shard_map/pallas_call | solution.py:835
  301.4 2.1 convert_element_type.142
  303.5 1.3 copy.43
  306.8 3.1 fusion.26
  310.5 2.5 convert_element_type.144
  314.5 2.8 convert_element_type.146
  317.9 1.6 convert_element_type.147
  (133 shorter events, 13.1 us)
Async XLA Ops:
  0.6 77.3 %copy-start = (bf16[1024,1024]{1,0:T(8,128)(2,1)S(1)}, bf16[1024,1024]{1,0:T(8,128)(2,1)}, u32[]{:S(2)}) copy-start(bf16[1024,1024]{1,0:T(8,128)(2,1)} %param.32) | copy-start | bytes 6291460
  0.7 3.5 %copy-start.25 = (f32[6144]{0:T(1024)S(1)}, f32[6144]{0:T(1024)}, u32[]{:S(2)}) copy-start(f32[6144]{0:T(1024)} %param.29) | copy-start | bytes 73732
  0.7 3.3 %copy-start.31 = (f32[1,3]{1,0:T(1,128)S(1)}, f32[1,3]{1,0:T(1,128)}, u32[]{:S(2)}) copy-start(f32[1,3]{1,0:T(1,128)} %param.21) | copy-start | bytes 40
  4.2 6.3 %copy-start.33 = (s32[1,3]{1,0:T(1,128)S(1)}, s32[1,3]{1,0:T(1,128)}, u32[]{:S(2)}) copy-start(s32[1,3]{1,0:T(1,128)} %param.22) | copy-start | bytes 40
  10.5 3.6 %copy-start.26 = (f32[3072]{0:T(1024)S(1)}, f32[3072]{0:T(1024)}, u32[]{:S(2)}) copy-start(f32[3072]{0:T(1024)} %param.31) | copy-start | bytes 36868
  14.1 5.0 %copy-start.14 = (bf16[128,1024]{1,0:T(8,128)(2,1)}, bf16[128,1024]{1,0:T(8,128)(2,1)S(1)}, u32[]{:S(2)}) copy-start(bf16[128,1024]{1,0:T(8,128)(2,1)S(1)} %fusion.9.norm_ref) | copy-start | bytes 786436
  14.1 5.1 %copy-start.30 = (s32[1,3]{1,0:T(1,128)S(1)}, s32[1,3]{1,0:T(1,128)}, u32[]{:S(2)}) copy-start(s32[1,3]{1,0:T(1,128)} %param.23) | copy-start | bytes 40
  19.3 8.0 %copy-start.29 = (s32[1,128]{1,0:T(1,128)S(1)}, s32[1,128]{1,0:T(1,128)}, u32[]{:S(2)}) copy-start(s32[1,128]{1,0:T(1,128)} %param.24) | copy-start | bytes 1540
  20.3 57.8 %copy-start.28 = (f32[1024]{0:T(1024)S(1)}, f32[1024]{0:T(1024)}, u32[]{:S(2)}) copy-start(f32[1024]{0:T(1024)} %param.33) | copy-start | bytes 12292
  26.3 4.2 %copy-start.23 = (s32[1024]{0:T(1024)}, s32[1024]{0:T(1024)S(1)}, u32[]{:S(2)}) copy-start(s32[1024]{0:T(1024)S(1)} %convert_reduce_fusion.5) | copy-start | bytes 12292
  30.5 54.2 %copy-start.12 = (bf16[1,128,1024]{2,1,0:T(8,128)(2,1)S(1)}, bf16[1,128,1024]{2,1,0:T(8,128)(2,1)}, u32[]{:S(2)}) copy-start(bf16[1,128,1024]{2,1,0:T(8,128)(2,1)} %param.25) | copy-start | bytes 786436
  78.0 6.7 %copy-start.2 = (f32[128,6144]{1,0:T(8,128)S(1)}, f32[128,6144]{1,0:T(8,128)}, u32[]{:S(2)}) copy-start(f32[128,6144]{1,0:T(8,128)} %copy-done.1) | copy-start | bytes 9437188
  85.0 6.5 %copy-start.17 = (bf16[128,1024]{1,0:T(8,128)(2,1)}, bf16[128,1024]{1,0:T(8,128)(2,1)S(1)}, u32[]{:S(2)}) copy-start(bf16[128,1024]{1,0:T(8,128)(2,1)S(1)} %get-tuple-element.50.d_ff_ref) | copy-start | bytes 786436
  85.0 6.5 %copy-start.20 = (bf16[128,1024]{1,0:T(8,128)(2,1)}, bf16[128,1024]{1,0:T(8,128)(2,1)S(1)}, u32[]{:S(2)}) copy-start(bf16[128,1024]{1,0:T(8,128)(2,1)S(1)} %get-tuple-element.65.norm_ref) | copy-start | bytes 786436
  85.0 6.5 %copy-start.32 = (f32[4096]{0:T(1024)S(1)}, f32[4096]{0:T(1024)}, u32[]{:S(2)}) copy-start(f32[4096]{0:T(1024)} %param.35) | copy-start | bytes 49156
  85.1 13.2 %slice-start.2 = ((s8[8388608]{0:T(1024)(128)(4,1)}), s8[4194304]{0:T(1024)(128)(4,1)S(1)}, s32[]{:S(2)}) async-start(s8[8388608]{0:T(1024)(128)(4,1)} %bitcast.87), calls=%async_computation.2 | async-start | bytes 8388608
  85.1 16.2 %slice-start = ((s8[8388608]{0:T(1024)(128)(4,1)}), s8[4194304]{0:T(1024)(128)(4,1)S(1)}, s32[]{:S(2)}) async-start(s8[8388608]{0:T(1024)(128)(4,1)} %bitcast.85), calls=%async_computation | async-start | bytes 8388608
  91.6 6.7 %slice-start.3 = ((s8[8388608]{0:T(1024)(128)(4,1)}), s8[4194304]{0:T(1024)(128)(4,1)S(1)}, s32[]{:S(2)}) async-start(s8[8388608]{0:T(1024)(128)(4,1)} %bitcast.87), calls=%async_computation.3 | async-start | bytes 8388608
  91.6 9.7 %slice-start.1 = ((s8[8388608]{0:T(1024)(128)(4,1)}), s8[4194304]{0:T(1024)(128)(4,1)S(1)}, s32[]{:S(2)}) async-start(s8[8388608]{0:T(1024)(128)(4,1)} %bitcast.85), calls=%async_computation.1 | async-start | bytes 8388608
  98.2 3.1 copy-start.13
  98.2 3.1 copy-start.6
  98.3 3.1 copy-start.27
  102.6 2.7 copy-start.8
  102.6 2.7 copy-start.24
  219.5 7.1 %copy-start.11 = (f32[128,1024]{1,0:T(8,128)S(1)}, f32[128,1024]{1,0:T(8,128)}, u32[]{:S(2)}) copy-start(f32[128,1024]{1,0:T(8,128)} %copy-done.10) | copy-start | bytes 1572868
  219.6 7.1 %copy-start.18 = (f32[128,1024]{1,0:T(8,128)S(1)}, f32[128,1024]{1,0:T(8,128)}, u32[]{:S(2)}) copy-start(f32[128,1024]{1,0:T(8,128)} %get-tuple-element.88) | copy-start | bytes 1572868
  225.1 2.4 copy-start.3
  226.9 3.0 copy-start.16
  226.9 2.9 copy-start.7
  227.4 2.5 copy-start.5
  305.7 8.0 %copy-start.21 = (bf16[128,1024]{1,0:T(8,128)(2,1)S(1)}, bf16[128,1024]{1,0:T(8,128)(2,1)}, u32[]{:S(2)}) copy-start(bf16[128,1024]{1,0:T(8,128)(2,1)} %get-tuple-element.42) | copy-start | bytes 786436
  310.5 7.4 %copy-start.19 = (bf16[512,1024]{1,0:T(8,128)(2,1)S(1)}, bf16[512,1024]{1,0:T(8,128)(2,1)}, u32[]{:S(2)}) copy-start(bf16[512,1024]{1,0:T(8,128)(2,1)} %get-tuple-element.44) | copy-start | bytes 3145732
  (6 other events, 8.3 us)
where the time goes:
time: 320 us; the launch traced here: 319 us
  Pallas kernels  226 us (71%)
  matrix products  48.8 us (15%)
  other arithmetic  22.7 us (7%)
  local copies, waits for them, and re-layouts  18 us (6%)
  between operations  3.98 us (1%)
    pallas_call x1, Pallas kernels, attend_back(): pl.pallas_call(attend_back_kernel, in_specs=[there] + [vmem] * 7 + [there...  104 us
    pallas_call x1, Pallas kernels, last(): pl.pallas_call(last_kernel, in_specs=[vmem, vmem, there, there, vmem], ou...  69.2 us
    pallas_call x1, Pallas kernels, attend(): pl.pallas_call(attend_kernel, in_specs=[there, vmem, vmem, vmem, vmem, th...  47.5 us
    dot_general x5, matrix products, back_product(): jnp.einsum('fo,io->fi', gradient_rows, matrix, preferred_element_type=jnp...  18 us
    convert_element_type x5, other arithmetic, local(): grad.astype(jnp.float32)  9.81 us
    dot_general x1, matrix products, local(): ff_inner = jnp.dot(norm_f, w_up, preferred_element_type=jnp.float32) + b_up  6.6 us

commit v1 on v0

--- a/solution.py
+++ b/solution.py
@@ -460,9 +460,11 @@
     ]
 
 
-def run_shares(shares):
+def run_shares(shares, hooks):
     stages = ("after_y", "after_z1", "after_z2", "relay", "wait")
     for turn in range(len(shares) + len(stages) - 1):
+        for hook in hooks.get(turn, ()):
+            hook()
         for place, stage in enumerate(stages):
             if 0 <= turn - place < len(shares):
                 getattr(shares[turn - place], stage)()
@@ -583,18 +585,22 @@
     )(packed, seg_col, seg_row, counts, flow, norm_a, frames, skip)
 
 
-def attend_back_kernel(
+def backward_kernel(
     d_attn_ref, heads_ref, segq_ref, segk_ref, exact_ref, total_ref, cos_ref, sin_ref,
+    resid_ref, gain_ref, d_mid_ref, segment_ref, small_ref,
     d_ff_ref, act_ref, norm_ref, d_inner_ref, attn_ref, d_branch_ref,
-    d_qkv_ref, g_down, g_up, g_out,
+    norm_a_ref, joined_ref, w_qkv_ref, w_skip_ref,
+    g_down, g_up, g_out, g_qkv, g_skip, smalls, g_frames, g_skip_in,
     grad_heads, d_heads, dk_ref, dv_ref,
     d_ff_all, act_all, norm_all, d_inner_all, attn_all, d_branch_all,
+    norm_a_all, joined_all, d_qkv, d_qkv_all, d_resid, d_resid_all,
+    w_qkv, w_skip, small_own, small_got, small_sum,
     *rest,
 ):
     tiles, (send_sems, recv_sems, local_sems) = rest[:-3], rest[-3:]
     links = Links(send_sems, recv_sems, local_sems)
     links.enter((1, 2, 3), range(1, 8))
-    rows = d_attn_ref.shape[0]
+    rows, model = d_mid_ref.shape
     far_first = (6, 7, 4, 5, 2, 3, 1)
     own_rows = pl.ds(pl.multiple_of(links.seq * rows, rows), rows)
     strip = lambda ref, place, size: ref.at[
@@ -610,11 +616,18 @@
     gather_d = Gathered(links, d_ff_ref, d_ff_all)
     quarter_a = Quarter(links, lambda u: act_ref.at[u], act_all)
     gather_n = Gathered(links, norm_ref, norm_all)
-    width = d_inner_all.shape[1]
+    width, narrow = d_inner_all.shape[1], d_branch_all.shape[1]
     quarter_i = Quarter(links, lambda u: strip(d_inner_ref, u, width), d_inner_all)
     gather_b = Gathered(links, attn_ref, attn_all)
-    narrow = d_branch_all.shape[1]
     quarter_b = Quarter(links, lambda u: strip(d_branch_ref, u, narrow), d_branch_all)
+    loads = [
+        links.keep(w_qkv_ref, w_qkv),
+        links.keep(w_skip_ref, w_skip),
+        links.keep(norm_a_ref, norm_a_all),
+        links.keep(joined_ref, joined_all),
+    ]
+    small_own[...] = small_ref[...]
+    gather_d.relay()
     own.wait()
     for copy in incoming:
         copy.wait_recv()
@@ -667,11 +680,10 @@
         return 0
 
     lax.fori_loop(0, blocks, finish, 0)
-    model = d_attn_ref.shape[1]
     part = lambda place, c: d_heads.at[
         pl.ds(pl.multiple_of(place * rows, rows), rows), pl.ds(c * 128, 128)
     ]
-    home = lambda c: d_qkv_ref.at[
+    home = lambda c: d_qkv.at[
         :, pl.ds(pl.multiple_of(c * model + links.seq * 128, 128), 128)
     ]
     owns = [links.keep(part(links.seq, c), home(c)) for c in range(3)]
@@ -681,28 +693,28 @@
         for c in range(3)
     ]
     half = width // 2
-    shares = []
-    for index, (left, right, columns, result) in enumerate(
-        (
-            (act_all, d_ff_all, 0, lambda u: g_down.at[
-                pl.ds(pl.multiple_of(u * 128, 128), 128), pl.ds(0, half)]),
-            (act_all, d_ff_all, 1, lambda u: g_down.at[
-                pl.ds(pl.multiple_of(u * 128, 128), 128), pl.ds(half, half)]),
-            (norm_all, d_inner_all, 0, lambda u: g_up.at[
-                :, pl.ds(pl.multiple_of(u * width, width), half)]),
-            (norm_all, d_inner_all, 1, lambda u: g_up.at[
-                :, pl.ds(pl.multiple_of(u * width + half, half), half)]),
-        )
-    ):
-        shares.append(
-            Share(links, left, right, pl.ds(columns * half, half),
-                  *tiles[4 * index : 4 * index + 4], result)
-        )
-    shares.append(
-        Share(links, attn_all, d_branch_all, pl.ds(0, narrow), *tiles[16:20],
-              lambda u: g_out.at[:, pl.ds(pl.multiple_of(u * narrow, narrow), narrow)])
-    )
-    gather_d.relay()
+    down_at = lambda h: lambda u: g_down.at[
+        pl.ds(pl.multiple_of(u * 128, 128), 128), pl.ds(h * half, half)
+    ]
+    column_at = lambda ref, step, offset, size: lambda u: ref.at[
+        :, pl.ds(pl.multiple_of(u * step + offset, 128), size)
+    ]
+    wide, thin = d_qkv_all.shape[1], d_resid_all.shape[1]
+    third = wide // 2
+    plans = [
+        (act_all, d_ff_all, pl.ds(0, half), down_at(0)),
+        (act_all, d_ff_all, pl.ds(half, half), down_at(1)),
+        (norm_all, d_inner_all, pl.ds(0, half), column_at(g_up, width, 0, half)),
+        (norm_all, d_inner_all, pl.ds(half, half), column_at(g_up, width, half, half)),
+        (attn_all, d_branch_all, pl.ds(0, narrow), column_at(g_out, narrow, 0, narrow)),
+        (norm_a_all, d_qkv_all, pl.ds(0, third), column_at(g_qkv, wide, 0, third)),
+        (norm_a_all, d_qkv_all, pl.ds(third, third), column_at(g_qkv, wide, third, third)),
+        (joined_all, d_resid_all, pl.ds(0, thin), column_at(g_skip, thin, 0, thin)),
+    ]
+    shares = [
+        Share(links, left, right, columns, *tiles[4 * i : 4 * i + 4], result)
+        for i, (left, right, columns, result) in enumerate(plans)
+    ]
     gather_n.relay()
     gather_d.wait()
     quarter_a.wait()
@@ -716,17 +728,101 @@
     gather_b.wait()
     quarter_b.wait()
     shares[4].start()
-    run_shares(shares)
-    for copy in owns:
-        copy.wait()
-    for copy in incoming:
+    state = {}
+
+    def projections():
+        for copy in owns:
+            copy.wait()
+        for copy in incoming:
+            copy.wait_recv()
+        for copy in loads:
+            copy.wait()
+        state["qkv"] = Quarter(links, lambda u: strip(d_qkv, u, wide), d_qkv_all)
+        d_norm = lax.dot_general(
+            d_qkv[...], w_qkv[...], along, preferred_element_type=jnp.float32
+        )
+        resid = resid_ref[...]
+        centred = resid - jnp.mean(resid, axis=1, keepdims=True)
+        scale = lax.rsqrt(jnp.mean(centred * centred, axis=1, keepdims=True) + EPSILON)
+        unit = centred * scale
+        inward = d_norm * gain_ref[...]
+        d_resid_f = d_mid_ref[...] + scale * (
+            inward
+            - jnp.mean(inward, axis=1, keepdims=True)
+            - unit * jnp.mean(inward * unit, axis=1, keepdims=True)
+        )
+        rounded = d_resid_f.astype(jnp.bfloat16)
+        d_resid[...] = rounded
+        state["resid"] = Quarter(links, lambda u: strip(d_resid, u, thin), d_resid_all)
+        small_own[0:1, :] = jnp.sum(rounded.astype(jnp.float32), axis=0, keepdims=True)
+        for c in range(3):
+            small_own[1 + c : 2 + c, :] = jnp.sum(
+                d_qkv[:, c * model : (c + 1) * model].astype(jnp.float32), axis=0, keepdims=True
+            )
+        d_scale = d_norm * unit
+        for u in range((small_own.shape[0] - 10) // 6):
+            inside = segment_ref[...] == u
+            row = 10 + 6 * u
+            small_own[row : row + 1, :] = jnp.sum(
+                jnp.where(inside, d_norm, 0.0), axis=0, keepdims=True
+            )
+            small_own[row + 1 : row + 2, :] = jnp.sum(
+                jnp.where(inside, d_scale, 0.0), axis=0, keepdims=True
+            )
+        state["small"] = links.send(small_own, small_got.at[0], links.peer(1))
+
+    def last_shares():
+        state["qkv"].wait()
+        shares[5].start()
+        shares[6].start()
+        state["resid"].wait()
+        shares[7].start()
+
+    def inputs():
+        for index, out in enumerate((g_frames, g_skip_in)):
+            out[...] = lax.dot_general(
+                d_resid[...],
+                w_skip[pl.ds(index * model, model), :],
+                along,
+                preferred_element_type=jnp.float32,
+            ).astype(jnp.bfloat16)
+
+    def small_y():
+        state["small"].wait_recv()
+        small_sum[0] = small_own[...] + small_got[0]
+        state["small"] = links.send(small_sum.at[0], small_got.at[1], links.peer(2))
+
+    def small_z1():
+        state["small"].wait_recv()
+        small_sum[1] = small_sum[0] + small_got[1]
+        state["small"] = links.send(small_sum.at[1], small_got.at[2], links.peer(4))
+
+    def small_z2():
+        state["small"].wait_recv()
+        mine = smalls.at[links.utt]
+        mine[...] = small_sum[1] + small_got[2]
+        state["spread"] = [links.send(mine, mine, links.mate(r)) for r in (2, 3, 1)]
+
+    run_shares(
+        shares,
+        {
+            1: (projections,),
+            2: (last_shares,),
+            3: (inputs, small_y),
+            4: (small_z1,),
+            5: (small_z2,),
+        },
+    )
+    for copy in state["spread"]:
         copy.wait_recv()
     links.leave()
 
 
-def attend_back(
+def backward(
     d_attn, heads, seg_col, seg_row, exact, total, cos, sin,
+    resid, gain, d_mid, segment, small,
     d_ff, act_quarters, norm_f, d_inner, attn_b, d_branch,
+    norm_a_all, joined_all, w_qkv, w_skip,
 ):
     rows, model = d_attn.shape
     frames = heads.shape[0]
@@ -734,124 +830,57 @@
     vmem, there = everywhere(pltpu.VMEM), everywhere(pl.ANY)
     shape = jax.ShapeDtypeStruct
     bf16 = lambda *dims: pltpu.VMEM(dims, jnp.bfloat16)
-    half = inner // 8
+    f32 = lambda *dims: pltpu.VMEM(dims, jnp.float32)
+    part = model // 8
     return pl.pallas_call(
-        attend_back_kernel,
-        in_specs=[there] + [vmem] * 7 + [there] * 6,
-        out_specs=[vmem] * 4,
+        backward_kernel,
+        in_specs=[there] + [vmem] * 12 + [there] * 10,
+        out_specs=[vmem] * 8,
         out_shape=[
-            shape((rows, 3 * model), jnp.bfloat16),
             shape((inner // 8, model), jnp.bfloat16),
-            shape((model // 8, inner), jnp.bfloat16),
-            shape((model // 8, model), jnp.bfloat16),
+            shape((part, inner), jnp.bfloat16),
+            shape((part, model), jnp.bfloat16),
+            shape((part, 3 * model), jnp.bfloat16),
+            shape((2 * part, model), jnp.bfloat16),
+            shape((4,) + small.shape, jnp.float32),
+            shape((rows, model), jnp.bfloat16),
+            shape((rows, model), jnp.bfloat16),
         ],
         scratch_shapes=[
             bf16(frames, 128),
             bf16(frames, 384),
-            pltpu.VMEM((frames, 128), jnp.float32),
-            pltpu.VMEM((frames, 128), jnp.float32),
+            f32(frames, 128),
+            f32(frames, 128),
             bf16(4 * rows, model),
             bf16(4 * rows, inner // 4),
             bf16(4 * rows, model),
             bf16(4 * rows, inner // 4),
             bf16(4 * rows, model),
             bf16(4 * rows, model // 4),
+            bf16(4 * rows, model),
+            bf16(4 * rows, 2 * model),
+            bf16(rows, 3 * model),
+            bf16(4 * rows, 3 * model // 4),
+            bf16(rows, model),
+            bf16(4 * rows, model // 4),
+            bf16(*w_qkv.shape),
+            bf16(*w_skip.shape),
+            f32(*small.shape),
+            f32(3, *small.shape),
+            f32(2, *small.shape),
         ]
-        + share_scratch(128, half) * 4
-        + share_scratch(model // 8, model // 4)
-        + semaphores(80),
+        + share_scratch(part, inner // 8) * 4
+        + share_scratch(part, model // 4)
+        + share_scratch(part, 3 * model // 8) * 2
+        + share_scratch(2 * part, model // 4)
+        + semaphores(112),
         compiler_params=comm_params(2),
     )(
         d_attn, heads, seg_col, seg_row, exact, total, cos, sin,
+        resid, gain, d_mid, segment, small,
         d_ff, act_quarters, norm_f, d_inner, attn_b, d_branch,
-    )
-
-
-def last_kernel(
-    norm_all, joined_all, d_qkv_ref, d_resid_ref, small_ref,
-    g_qkv, g_skip, smalls,
-    d_qkv_all, d_resid_all, small_got, small_sum, *rest,
-):
-    tiles, (send_sems, recv_sems, local_sems) = rest[:-3], rest[-3:]
-    links = Links(send_sems, recv_sems, local_sems)
-    links.enter((1, 2, 3), (1, 2, 4))
-    strip = lambda ref, place, size: ref.at[
-        :, pl.ds(pl.multiple_of(place * size, size), size)
-    ]
-    wide, narrow = d_qkv_all.shape[1], d_resid_all.shape[1]
-    quarter_q = Quarter(links, lambda u: strip(d_qkv_ref, u, wide), d_qkv_all)
-    quarter_r = Quarter(links, lambda u: strip(d_resid_ref, u, narrow), d_resid_all)
-    exchange = [links.send(small_ref, small_got.at[0], links.peer(1))]
-    half = wide // 2
-    shares = [
-        Share(links, norm_all, d_qkv_all, pl.ds(0, half), *tiles[0:4],
-              lambda u: g_qkv.at[:, pl.ds(pl.multiple_of(u * wide, 128), half)]),
-        Share(links, norm_all, d_qkv_all, pl.ds(half, half), *tiles[4:8],
-              lambda u: g_qkv.at[:, pl.ds(pl.multiple_of(u * wide + half, 128), half)]),
-        Share(links, joined_all, d_resid_all, pl.ds(0, narrow), *tiles[8:12],
-              lambda u: g_skip.at[:, pl.ds(pl.multiple_of(u * narrow, narrow), narrow)]),
-    ]
-    quarter_q.wait()
-    shares[0].start()
-    shares[1].start()
-    quarter_r.wait()
-    shares[2].start()
-    exchange[0].wait_recv()
-    small_sum[0] = small_ref[...] + small_got[0]
-    exchange.append(links.send(small_sum.at[0], small_got.at[1], links.peer(2)))
-    shares[0].after_y()
-    exchange[1].wait_recv()
-    small_sum[1] = small_sum[0] + small_got[1]
-    exchange.append(links.send(small_sum.at[1], small_got.at[2], links.peer(4)))
-    shares[1].after_y()
-    shares[0].after_z1()
-    exchange[2].wait_recv()
-    mine = smalls.at[links.utt]
-    mine[...] = small_sum[1] + small_got[2]
-    spread = [links.send(mine, mine, links.mate(r)) for r in (2, 3, 1)]
-    shares[2].after_y()
-    shares[1].after_z1()
-    shares[0].after_z2()
-    shares[2].after_z1()
-    shares[1].after_z2()
-    shares[0].relay()
-    shares[2].after_z2()
-    shares[1].relay()
-    shares[0].wait()
-    shares[2].relay()
-    shares[1].wait()
-    shares[2].wait()
-    for copy in spread:
-        copy.wait_recv()
-    links.leave()
-
-
-def last(norm_all, joined_all, d_qkv, d_resid, small):
-    rows, model = d_resid.shape
-    vmem, there = everywhere(pltpu.VMEM), everywhere(pl.ANY)
-    shape = jax.ShapeDtypeStruct
-    bf16 = lambda *dims: pltpu.VMEM(dims, jnp.bfloat16)
-    wide = d_qkv.shape[1] // 4
-    return pl.pallas_call(
-        last_kernel,
-        in_specs=[vmem, vmem, there, there, vmem],
-        out_specs=[vmem] * 3,
-        out_shape=[
-            shape((model // 8, 4 * wide), jnp.bfloat16),
-            shape((model // 4, model), jnp.bfloat16),
-            shape((4,) + small.shape, jnp.float32),
-        ],
-        scratch_shapes=[
-            bf16(4 * rows, wide),
-            bf16(4 * rows, model // 4),
-            pltpu.VMEM((3,) + small.shape, jnp.float32),
-            pltpu.VMEM((2,) + small.shape, jnp.float32),
-        ]
-        + share_scratch(model // 8, wide // 2) * 2
-        + share_scratch(model // 4, model // 4)
-        + semaphores(48),
-        compiler_params=comm_params(3),
-    )(norm_all, joined_all, d_qkv, d_resid, small)
+        norm_a_all, joined_all, w_qkv, w_skip,
+    )
 
 
 def wide_tables(position):
@@ -1000,7 +1029,23 @@
     d_attn = back_product(d_branch, w_out)
     if fused:
         act_quarters = jnp.transpose(act_b.reshape(local_rows, shards, 4, -1), (2, 0, 1, 3))
-        d_qkv, g_w_down, g_w_up, g_w_out = attend_back(
+        pieces = jnp.concatenate([d_gate_a, d_shift_f, d_scale_f, d_gate_f], axis=1)
+        sums = jnp.dot(jnp.transpose(member_f), pieces, precision=HIGHEST_PRECISION)
+        sums = jnp.pad(sums.reshape(-1, 4, model_width), ((0, 0), (2, 0), (0, 0)))
+        row = lambda vector: vector.reshape(-1, model_width)
+        small = jnp.concatenate(
+            [
+                jnp.zeros((4, model_width), jnp.float32),
+                row(g_b_out),
+                row(g_b_up),
+                row(g_b_down),
+                row(sums),
+            ],
+            axis=0,
+        )
+        used = small.shape[0]
+        small = jnp.pad(small, ((0, -used % 8), (0, 0)))
+        g_w_down, g_w_up, g_w_out, g_w_qkv, g_w_skip, smalls, g_frames, g_skip_in = backward(
             d_attn.astype(jnp.bfloat16),
             qkv_heads,
             seg_col,
@@ -1009,12 +1054,30 @@
             total,
             cos_all,
             sin_all,
+            residual,
+            1.0 + scale_a,
+            d_mid,
+            segment[:, None],
+            small,
             d_ff,
             act_quarters.reshape(4, local_rows, -1),
             norm_f,
             d_inner_b,
             attn_b,
             d_branch,
+            norm_all,
+            joined_all,
+            w_qkv,
+            w_skip,
+        )
+        smalls = smalls[:, :used].reshape(4, -1)
+        biases = w_up.shape[1] + 6 * model_width
+        bias_sum = jnp.sum(smalls[:, :biases], axis=0)
+        d_mod_all = smalls[:, biases:].reshape(-1, 6 * model_width)
+        flow_all = flows[:, 0, : flow_times.shape[1]].reshape(-1)
+        act_all = jax.nn.silu(time_embed(flow_all, model_width)).astype(jnp.bfloat16)
+        g_w_skip, g_w_qkv, g_w_out, g_w_up, g_w_down = (
+            grad.astype(jnp.float32) for grad in (g_w_skip, g_w_qkv, g_w_out, g_w_up, g_w_down)
         )
     else:
         g_w_down = weight_grad(gather_left(act_b), d_ff)
@@ -1055,40 +1118,29 @@
             d_key_value[0].reshape(local_rows, HEADS, HEAD_DIM), angle_cos, angle_sin
         ).reshape(local_rows, model_width)
         d_qkv = jnp.concatenate([d_query_pre, d_key_pre, d_key_value[1]], axis=1).astype(jnp.bfloat16)
-    g_b_qkv = jnp.sum(d_qkv.astype(jnp.float32), axis=0)
-    d_norm_a = back_product(d_qkv, w_qkv)
-    _, norm_a_pull = jax.vjp(modulate, residual, scale_a, shift_a)
-    d_resid_norm, d_scale_a, d_shift_a = norm_a_pull(d_norm_a)
-    d_resid = (d_mid + d_resid_norm).astype(jnp.bfloat16)
-    g_b_skip = jnp.sum(d_resid.astype(jnp.float32), axis=0)
-    d_joined = back_product(d_resid, w_skip)
-    d_mod_f = jnp.concatenate(
-        [d_shift_a, d_scale_a, d_gate_a, d_shift_f, d_scale_f, d_gate_f], axis=1
-    )
-    d_mod_u = jnp.dot(jnp.transpose(member_f), d_mod_f, precision=HIGHEST_PRECISION)
-    small = jnp.concatenate(
-        [g_b_skip, g_b_qkv, g_b_out, g_b_up, g_b_down, d_mod_u.reshape(-1)]
-    )
-    biases = small.shape[0] - d_mod_u.size
-    if fused:
-        g_w_qkv, g_w_skip, smalls = last(
-            norm_all, joined_all, d_qkv, d_resid, small.reshape(-1, 128)
-        )
-        smalls = smalls.reshape(4, -1)
-        bias_sum = jnp.sum(smalls[:, :biases], axis=0)
-        d_mod_all = smalls[:, biases:].reshape(-1, d_mod_u.shape[1])
-        flow_all = flows[:, 0, : flow_times.shape[1]].reshape(-1)
-        act_all = jax.nn.silu(time_embed(flow_all, model_width)).astype(jnp.bfloat16)
-        g_w_skip, g_w_qkv, g_w_out, g_w_up, g_w_down = (
-            grad.astype(jnp.float32) for grad in (g_w_skip, g_w_qkv, g_w_out, g_w_up, g_w_down)
-        )
-    else:
+        g_b_qkv = jnp.sum(d_qkv.astype(jnp.float32), axis=0)
+        d_norm_a = back_product(d_qkv, w_qkv)
+        _, norm_a_pull = jax.vjp(modulate, residual, scale_a, shift_a)
+        d_resid_norm, d_scale_a, d_shift_a = norm_a_pull(d_norm_a)
+        d_resid = (d_mid + d_resid_norm).astype(jnp.bfloat16)
+        g_b_skip = jnp.sum(d_resid.astype(jnp.float32), axis=0)
+        d_joined = back_product(d_resid, w_skip)
+        d_mod_f = jnp.concatenate(
+            [d_shift_a, d_scale_a, d_gate_a, d_shift_f, d_scale_f, d_gate_f], axis=1
+        )
+        d_mod_u = jnp.dot(jnp.transpose(member_f), d_mod_f, precision=HIGHEST_PRECISION)
+        small = jnp.concatenate(
+            [g_b_skip, g_b_qkv, g_b_out, g_b_up, g_b_down, d_mod_u.reshape(-1)]
+        )
+        biases = small.shape[0] - d_mod_u.size
         g_w_qkv = weight_grad(gather_left(norm_a), d_qkv)
         g_w_skip = weight_grad(gather_left(joined), d_resid)
         small = xor_sum(small.reshape(-1, 128), "seq").reshape(-1)
         bias_sum = xor_sum(small[:biases].reshape(-1, 128), "utt").reshape(-1)
         d_mod_all = gather_ordered(small[biases:].reshape(d_mod_u.shape), 0)
         act_all = gather_ordered(time_act, 0)
+        g_frames = d_joined[:, :model_width].astype(jnp.bfloat16)
+        g_skip_in = d_joined[:, model_width:].astype(jnp.bfloat16)
     act_all = act_all.astype(jnp.float32)
     own_width = model_width // shards
     act_own = lax.dynamic_slice_in_dim(act_all, seq_place * own_width, own_width, 1)
@@ -1098,16 +1150,16 @@
         lax.dynamic_slice_in_dim(d_mod_all, seq_place * mod_width, mod_width, 1), axis=0
     )
     own_biases, offset = [], 0
-    for vector in (g_b_skip, g_b_qkv, g_b_out, g_b_up, g_b_down):
-        width = vector.shape[0] // shards
+    for size in (b_skip.shape[0], b_qkv.shape[0], b_out.shape[0], b_up.shape[0], b_down.shape[0]):
+        width = size // shards
         own_biases.append(
             lax.dynamic_slice_in_dim(bias_sum, offset + seq_place * width, width, 0)
         )
-        offset += vector.shape[0]
+        offset += size
     return (
         out_state.astype(jnp.bfloat16)[None],
-        d_joined[:, :model_width].astype(jnp.bfloat16)[None],
-        d_joined[:, model_width:].astype(jnp.bfloat16)[None],
+        g_frames[None],
+        g_skip_in[None],
         g_w_skip,
         own_biases[0],
         g_w_mod,

time: 320 us -> 278 us (0.87)
  Pallas kernels: 226 us -> 192 us
  matrix products: 48.8 us -> 41.6 us
    pallas_call x2 -> x1, Pallas kernels: 173 us -> 138 us  [backward(): pl.pallas_call(backward_kernel, in_specs=[there] + [vmem] * 12 + [there]...]
    dot_general x5 -> x3, matrix products: 18 us -> 13.1 us  [back_product(): jnp.einsum('fo,io->fi', gradient_rows, matrix, preferred_element_type=jnp...]
where the time goes in v1:
time: 278 us; the launch traced here: 274 us
  Pallas kernels  192 us (69%)
  matrix products  41.6 us (15%)
  other arithmetic  20.9 us (8%)
  local copies, waits for them, and re-layouts  16.6 us (6%)
  between operations  3.76 us (1%)
    pallas_call x1, Pallas kernels, backward(): pl.pallas_call(backward_kernel, in_specs=[there] + [vmem] * 12 + [there]...  138 us
    pallas_call x1, Pallas kernels, attend(): pl.pallas_call(attend_kernel, in_specs=[there, vmem, vmem, vmem, vmem, th...  47.5 us
    dot_general x3, matrix products, back_product(): jnp.einsum('fo,io->fi', gradient_rows, matrix, preferred_element_type=jnp...  13.1 us
    convert_element_type x5, other arithmetic, local(): grad.astype(jnp.float32)  8.59 us
    dot_general x1, matrix products, local(): mod_u = jnp.dot(time_act, w_mod, preferred_element_type=jnp.float32) + b_mod  6.32 us
    pallas_call x1, Pallas kernels, rotate_pack(): pl.pallas_call(rotate_pack_kernel, grid=(blocks,), in_specs=[pl.BlockSpec...  5.92 us

profile of v1, /device:TPU:0, one launch (start us, length us, event | category | flops | bytes accessed | tf_op | source)
XLA Modules:
  0.0 274.5 jit_solution(10139072809066334674)
XLA Ops:
  1.6 6.3 %convolution_add_fusion = f32[3,6144]{1,0:T(4,128)S(1)} fusion(bf16[1024,6144]{1,0:T(8,128)(2,1)} %param.28, f32[6144]{0:T(1024)} %param.29, f32[3,512]{1,0:T(4,128)S(1)} %get-tuple-element.83, f32[3,512]{1,0:T(4,128)S(1)} %get-tuple-element.82), kind=kOutput, calls=%fused_computation | convolution fusion | flops 37785600 | bytes 12693504 | tf_op jit(solution)/shard_map/dot_general | solution.py:943
  8.3 1.5 fusion.35
  9.8 4.1 %add_reduce_fusion = (f32[128]{0:T(128)S(1)}, f32[128,1024]{1,0:T(8,128)S(1)}) fusion(f32[1024]{0:T(1024)S(1)} %copy-done.20, bf16[2048,1024]{1,0:T(8,128)(2,1)} %w_skip_ref.1, bf16[128,1024]{1,0:T(8,128)(2,1)S(1)} %bitcast.82, bf16[128,1024]{1,0:T(8,128)(2,1)S(1)} %bitcast.84), kind=kOutput, calls=%fused_computation.24 | convolution fusion | flops 538181504 | bytes 5247488 | tf_op jit(solution)/shard_map/dot_general | solution.py:947
  14.2 1.0 broadcast_add_fusion
  15.2 2.2 convolution_add_fusion.2.q_ref.k_ref.v_ref
  17.5 1.0 fusion.28
  18.5 5.9 %shard_map.298.packed_ref = bf16[8,128,384]{2,1,0:T(8,128)(2,1)} custom-call(f32[128,3072]{1,0:T(8,128)} %convolution_add_fusion.2.q_ref.k_ref.v_ref, f32[128,3072]{1,0:T(8,128)} %convolution_add_fusion.2.q_ref.k_ref.v_ref, f32[128,3072]{1,0:T(8,128)} %convolution_add_fusion.2.q_ref.k_ref.v_ref, f32[128,128]{1,0:T(8,128)} %get-tuple-element.85.cos_ref, ...), custom_call_target="tpu_custom_call" | custom-call | tf_op jit(solution)/shard_map/pallas_call | solution.py:239
  24.5 1.0 copy.40.segq_ref
  26.1 1.4 maximum_bitcast_fusion
  28.7 47.5 %shard_map.299 = (bf16[128,1024]{1,0:T(8,128)(2,1)}, bf16[1024,384]{1,0:T(8,128)(2,1)}, f32[1024,128]{1,0:T(8,128)}, f32[1024,128]{1,0:T(8,128)}, f32[8,128]{1,0...) custom-call(bf16[8,128,384]{2,1,0:T(8,128)(2,1)} %shard_map.298.packed_ref, ...), custom_call_target="tpu_custom_call" | custom-call | tf_op jit(solution)/shard_map/pallas_call | solution.py:565
  76.2 1.9 fusion.60
  78.1 1.8 fusion.62
  83.0 7.8 %fusion.63 = f32[128,4096]{1,0:T(8,128)} fusion(bf16[128,1024]{1,0:T(8,128)(2,1)S(1)} %get-tuple-element.54.d_ff_ref, bf16[4096,1024]{1,0:T(8,128)(2,1)} %param.36), kind=kOutput, calls=%fused_computation.134 | convolution fusion | flops 1073741824 | bytes 10747904 | tf_op jit(solution)/shard_map/fo,io->fi/dot_general | solution.py:145
  90.8 4.8 %convert_reduce_fusion = (f32[4096]{0:T(1024)S(1)}, bf16[128,4096]{1,0:T(8,128)(2,1)S(1)}, bf16[128,4096]{1,0:T(8,128)(2,1)S(1)}) fusion(f32[128,4096]{1,0:T(8,128)} %fusion.63, f32[4096]{0:T(1024)S(1)} %copy-done.28, bf16[128,1024]{1,0:T(8,128)(2,1)S(1)} %get-tuple-element.67.norm_ref, bf16[1024,4096]{1,0:T(8,128)(2,1)S(1)} %bitcast.77), kind=kOutput, calls=%fused_computation.20 | convolution fusion | flops 1086844928 | bytes 12877824 | tf_op jit(solution)/shard_map/dot_general | solution.py:1010
  95.6 3.8 %slice_add_fusion.3 = (f32[128,1024]{1,0:T(8,128)}, f32[128]{0:T(128)S(1)}, f32[128,1024]{1,0:T(8,128)S(1)}) fusion(f32[128,6144]{1,0:T(8,128)S(1)} %copy-done.2, f32[128,1024]{1,0:T(8,128)S(1)} %get-tuple-element.62, f32[128]{0:T(128)S(1)} %broadcast_multiply_fusion, bf16[128,4096]{1,0:T(8,128)(2,1)S(1)} %get-tuple-element.56.d_inner_ref, ...), kind=kOutput, calls=%fused_computation.37 | convolution fusion | flops 1074528128 | bytes 12059648 | tf_op jit(solution)/shard_map/fo,io->fi/dot_general | solution.py:145
  99.4 2.5 fusion.59
  101.9 1.0 fusion.55
  103.0 1.5 convolution_convert_fusion.d_attn_ref
  104.6 3.4 %fusion.15 = (f32[1024,128]{1,0:T(8,128)}, f32[1024,128]{1,0:T(8,128)}) fusion(f32[128]{0:T(128)S(1)} %get-tuple-element.90, f32[128]{0:T(128)S(1)} %get-tuple-element.91, f32[1024]{0:T(1024)S(1)} %subtract_convert_fusion), kind=kLoop, calls=%fused_computation.31 | loop fusion | flops 262144 | bytes 1053696 | tf_op jit(solution)/shard_map/mul | solution.py:894
  108.7 2.3 fusion.7
  112.1 1.5 reshape.212
  113.7 1.4 copy.41
  115.0 1.3 reshape.213.act_ref
  116.3 138.2 %shard_map.300 = (bf16[512,1024]{1,0:T(8,128)(2,1)}, bf16[128,4096]{1,0:T(8,128)(2,1)}, bf16[128,1024]{1,0:T(8,128)(2,1)}, bf16[128,3072]{1,0:T(8,128)(2,1)}, bf...) custom-call(bf16[128,1024]{1,0:T(8,128)(2,1)} %convolution_convert_fusi, ...), custom_call_target="tpu_custom_call" | custom-call | tf_op jit(solution)/shard_map/pallas_call | solution.py:835
  254.5 2.1 convert_element_type.132
  256.6 1.1 slice_bitcast_fusion
  260.0 3.1 %fusion.33 = f32[128,6144]{1,0:T(8,128)} fusion(f32[12,6144]{1,0:T(8,128)S(1)} %reshape.215, s32[]{:T(128)S(6)} %select_n.84, f32[12,512]{1,0:T(8,128)S(1)} %get-tuple-element.81, f32[12,512]{1,0:T(8,128)S(1)} %get-tuple-element.80), kind=kOutput, calls=%fused_computation.80 | convolution fusion | flops 113255424 | bytes 3489796 | tf_op jit(solution)/shard_map/dot_general | solution.py:1147
  263.7 1.3 convert_element_type.134
  265.0 1.4 dynamic_slice.24
  267.3 2.8 %convert_element_type.136 = f32[128,4096]{1,0:T(8,128)} convert(bf16[128,4096]{1,0:T(8,128)(2,1)} %get-tuple-element.45) | non-fusion elementwise | flops 524288 | bytes 3145728 | tf_op jit(solution)/shard_map/convert_element_type | solution.py:1080
  270.1 1.4 dynamic_slice.26
  271.5 1.6 convert_element_type.137
  (122 shorter events, 11.2 us)
Async XLA Ops:
  0.6 75.5 %copy-start = (bf16[1024,1024]{1,0:T(8,128)(2,1)S(1)}, bf16[1024,1024]{1,0:T(8,128)(2,1)}, u32[]{:S(2)}) copy-start(bf16[1024,1024]{1,0:T(8,128)(2,1)} %param.32) | copy-start | bytes 6291460
  1.6 6.4 %copy-start.29 = (s32[1,3]{1,0:T(1,128)S(1)}, s32[1,3]{1,0:T(1,128)}, u32[]{:S(2)}) copy-start(s32[1,3]{1,0:T(1,128)} %param.22) | copy-start | bytes 40
  8.0 1.8 copy-start.13
  8.0 1.8 copy-start.20
  8.3 6.9 %slice-start.2 = ((s8[6291456]{0:T(1024)(128)(4,1)}), s8[4194304]{0:T(1024)(128)(4,1)S(1)}, s32[]{:S(2)}) async-start(s8[6291456]{0:T(1024)(128)(4,1)} %bitcast.74), calls=%async_computation.2 | async-start | bytes 8388608
  9.7 4.4 %copy-start.1 = (f32[128,6144]{1,0:T(8,128)}, f32[128,6144]{1,0:T(8,128)S(1)}, u32[]{:S(2)}) copy-start(f32[128,6144]{1,0:T(8,128)S(1)} %fusion.35) | copy-start | bytes 9437188
  9.8 5.4 %slice-start.3 = ((s8[6291456]{0:T(1024)(128)(4,1)}), s8[2097152]{0:T(1024)(128)(4,1)S(1)}, s32[]{:S(2)}) async-start(s8[6291456]{0:T(1024)(128)(4,1)} %bitcast.74), calls=%async_computation.3 | async-start | bytes 4194304
  15.2 2.2 copy-start.5
  15.2 2.2 copy-start.26
  18.5 7.1 %copy-start.25 = (s32[1,128]{1,0:T(1,128)S(1)}, s32[1,128]{1,0:T(1,128)}, u32[]{:S(2)}) copy-start(s32[1,128]{1,0:T(1,128)} %param.24) | copy-start | bytes 1540
  18.5 9.6 %copy-start.27 = (f32[1,3]{1,0:T(1,128)S(1)}, f32[1,3]{1,0:T(1,128)}, u32[]{:S(2)}) copy-start(f32[1,3]{1,0:T(1,128)} %param.21) | copy-start | bytes 40
  24.4 51.8 %copy-start.23 = (f32[1024]{0:T(1024)S(1)}, f32[1024]{0:T(1024)}, u32[]{:S(2)}) copy-start(f32[1024]{0:T(1024)} %param.33) | copy-start | bytes 12292
  24.5 4.2 %copy-start.18 = (s32[1024]{0:T(1024)}, s32[1024]{0:T(1024)S(1)}, u32[]{:S(2)}) copy-start(s32[1024]{0:T(1024)S(1)} %convert_reduce_fusion.3) | copy-start | bytes 12292
  28.7 53.9 %copy-start.6 = (bf16[1,128,1024]{2,1,0:T(8,128)(2,1)S(1)}, bf16[1,128,1024]{2,1,0:T(8,128)(2,1)}, u32[]{:S(2)}) copy-start(bf16[1,128,1024]{2,1,0:T(8,128)(2,1)} %param.25) | copy-start | bytes 786436
  76.2 6.5 %copy-start.2 = (f32[128,6144]{1,0:T(8,128)S(1)}, f32[128,6144]{1,0:T(8,128)}, u32[]{:S(2)}) copy-start(f32[128,6144]{1,0:T(8,128)} %copy-done.1) | copy-start | bytes 9437188
  76.2 14.6 %slice-start.4 = ((s8[8388608]{0:T(1024)(128)(4,1)}), s8[4194304]{0:T(1024)(128)(4,1)S(1)}, s32[]{:S(2)}) async-start(s8[8388608]{0:T(1024)(128)(4,1)} %bitcast.76), calls=%async_computation.4 | async-start | bytes 8388608
  82.9 7.8 %copy-start.8 = (bf16[128,1024]{1,0:T(8,128)(2,1)}, bf16[128,1024]{1,0:T(8,128)(2,1)S(1)}, u32[]{:S(2)}) copy-start(bf16[128,1024]{1,0:T(8,128)(2,1)S(1)} %get-tuple-element.54.d_ff_ref) | copy-start | bytes 786436
  82.9 7.8 %copy-start.10 = (bf16[128,1024]{1,0:T(8,128)(2,1)}, bf16[128,1024]{1,0:T(8,128)(2,1)S(1)}, u32[]{:S(2)}) copy-start(bf16[128,1024]{1,0:T(8,128)(2,1)S(1)} %get-tuple-element.67.norm_ref) | copy-start | bytes 786436
  82.9 7.8 %slice-start.5 = ((s8[8388608]{0:T(1024)(128)(4,1)}), s8[4194304]{0:T(1024)(128)(4,1)S(1)}, s32[]{:S(2)}) async-start(s8[8388608]{0:T(1024)(128)(4,1)} %bitcast.76), calls=%async_computation.5 | async-start | bytes 8388608
  83.0 7.8 %copy-start.28 = (f32[4096]{0:T(1024)S(1)}, f32[4096]{0:T(1024)}, u32[]{:S(2)}) copy-start(f32[4096]{0:T(1024)} %param.35) | copy-start | bytes 49156
  90.8 8.6 %slice-start = ((s8[8388608]{0:T(1024)(128)(4,1)}), s8[4194304]{0:T(1024)(128)(4,1)S(1)}, s32[]{:S(2)}) async-start(s8[8388608]{0:T(1024)(128)(4,1)} %bitcast.72), calls=%async_computation | async-start | bytes 8388608
  90.8 8.6 %slice-start.1 = ((s8[8388608]{0:T(1024)(128)(4,1)}), s8[4194304]{0:T(1024)(128)(4,1)S(1)}, s32[]{:S(2)}) async-start(s8[8388608]{0:T(1024)(128)(4,1)} %bitcast.72), calls=%async_computation.1 | async-start | bytes 8388608
  95.6 3.8 %copy-start.4 = (bf16[128,4096]{1,0:T(8,128)(2,1)}, bf16[128,4096]{1,0:T(8,128)(2,1)S(1)}, u32[]{:S(2)}) copy-start(bf16[128,4096]{1,0:T(8,128)(2,1)S(1)} %get-tuple-element.56.d_inner_ref) | copy-start | bytes 3145732
  95.6 3.8 %copy-start.24 = (f32[1024]{0:T(1024)S(1)}, f32[1024]{0:T(1024)}, u32[]{:S(2)}) copy-start(f32[1024]{0:T(1024)} %param.37) | copy-start | bytes 12292
  99.4 2.5 copy-start.9
  102.9 5.1 %copy-start.3 = (f32[128,1024]{1,0:T(8,128)}, f32[128,1024]{1,0:T(8,128)S(1)}, u32[]{:S(2)}) copy-start(f32[128,1024]{1,0:T(8,128)S(1)} %get-tuple-element.52.d_mid_ref) | copy-start | bytes 1572868
  102.9 8.1 %copy-start.7 = (bf16[128,1024]{1,0:T(8,128)(2,1)}, bf16[128,1024]{1,0:T(8,128)(2,1)S(1)}, u32[]{:S(2)}) copy-start(bf16[128,1024]{1,0:T(8,128)(2,1)S(1)} %get-tuple-element.58.d_branch_ref) | copy-start | bytes 786436
  258.9 4.8 %copy-start.14 = (bf16[128,3072]{1,0:T(8,128)(2,1)S(1)}, bf16[128,3072]{1,0:T(8,128)(2,1)}, u32[]{:S(2)}) copy-start(bf16[128,3072]{1,0:T(8,128)(2,1)} %get-tuple-element.43) | copy-start | bytes 2359300
  263.1 3.4 %copy-start.15 = (bf16[128,1024]{1,0:T(8,128)(2,1)S(1)}, bf16[128,1024]{1,0:T(8,128)(2,1)}, u32[]{:S(2)}) copy-start(bf16[128,1024]{1,0:T(8,128)(2,1)} %get-tuple-element.44) | copy-start | bytes 786436
  265.0 6.4 %copy-start.11 = (bf16[512,1024]{1,0:T(8,128)(2,1)S(1)}, bf16[512,1024]{1,0:T(8,128)(2,1)}, u32[]{:S(2)}) copy-start(bf16[512,1024]{1,0:T(8,128)(2,1)} %get-tuple-element.46) | copy-start | bytes 3145732
  270.1 3.7 %copy-start.16 = (bf16[128,1024]{1,0:T(8,128)(2,1)S(1)}, bf16[128,1024]{1,0:T(8,128)(2,1)}, u32[]{:S(2)}) copy-start(bf16[128,1024]{1,0:T(8,128)(2,1)} %get-tuple-element.39) | copy-start | bytes 786436
  270.1 3.0 %copy-start.17 = (bf16[128,1024]{1,0:T(8,128)(2,1)S(1)}, bf16[128,1024]{1,0:T(8,128)(2,1)}, u32[]{:S(2)}) copy-start(bf16[128,1024]{1,0:T(8,128)(2,1)} %get-tuple-element.38) | copy-start | bytes 786436
  (4 other events, 5.3 us)

commit v2 on v1

--- a/solution.py
+++ b/solution.py
@@ -257,7 +257,7 @@
 
 
 MESH = pl.DeviceIdType.MESH
-VMEM_LIMIT = 60 * 1024 * 1024
+VMEM_LIMIT = 62 * 1024 * 1024
 
 
 def flip(index, bit):
@@ -322,6 +322,8 @@
         return copy
 
     def leave(self):
+        assert len(self.sent) <= self.send_sems.shape[0]
+        assert self.held <= self.local_sems.shape[0]
         for copy in self.sent:
             copy.wait_send()
 
@@ -471,7 +473,7 @@
 
 
 def semaphores(count):
-    return [pltpu.SemaphoreType.DMA((count,))] * 2 + [pltpu.SemaphoreType.DMA((16,))]
+    return [pltpu.SemaphoreType.DMA((count,))] * 2 + [pltpu.SemaphoreType.DMA((32,))]
 
 
 def comm_params(collective_id):
@@ -585,51 +587,221 @@
     )(packed, seg_col, seg_row, counts, flow, norm_a, frames, skip)
 
 
+ALONG = (((1,), (1,)), ((), ()))
+DOWN = (((0,), (0,)), ((), ()))
+
+
+def normal_parts(values):
+    centred = values - jnp.mean(values, axis=1, keepdims=True)
+    scale = lax.rsqrt(jnp.mean(centred * centred, axis=1, keepdims=True) + EPSILON)
+    return centred * scale, scale
+
+
+def normal_back(inward, unit, scale):
+    return scale * (
+        inward
+        - jnp.mean(inward, axis=1, keepdims=True)
+        - unit * jnp.mean(inward * unit, axis=1, keepdims=True)
+    )
+
+
+def column_sum(values):
+    return jnp.sum(values.astype(jnp.float32), axis=0, keepdims=True)
+
+
 def backward_kernel(
-    d_attn_ref, heads_ref, segq_ref, segk_ref, exact_ref, total_ref, cos_ref, sin_ref,
-    resid_ref, gain_ref, d_mid_ref, segment_ref, small_ref,
-    d_ff_ref, act_ref, norm_ref, d_inner_ref, attn_ref, d_branch_ref,
-    norm_a_ref, joined_ref, w_qkv_ref, w_skip_ref,
-    g_down, g_up, g_out, g_qkv, g_skip, smalls, g_frames, g_skip_in,
+    utts, attn_ref, resid_ref, mod_ref, segment_ref, mask_ref, dropped_ref, counts_ref, out_grad_ref,
+    b_out_ref, b_up_ref, b_down_ref,
+    heads_ref, segq_ref, segk_ref, exact_ref, total_ref, cos_ref, sin_ref,
+    norm_a_ref, joined_ref, w_out_ref, w_up_ref, w_down_ref, w_qkv_ref, w_skip_ref,
+    mixed, g_down, g_up, g_out, g_qkv, g_skip, smalls, g_frames, g_skip_in,
+    d_ff, norm_f, act, d_inner, d_branch, d_attn, pieces, d_mid, ff_sum, d_norm,
     grad_heads, d_heads, dk_ref, dv_ref,
     d_ff_all, act_all, norm_all, d_inner_all, attn_all, d_branch_all,
     norm_a_all, joined_all, d_qkv, d_qkv_all, d_resid, d_resid_all,
-    w_qkv, w_skip, small_own, small_got, small_sum,
+    up_ring, down_ring, w_out, w_qkv, w_skip, small_own, small_got, small_sum,
     *rest,
 ):
-    tiles, (send_sems, recv_sems, local_sems) = rest[:-3], rest[-3:]
+    tiles, (send_sems, recv_sems, local_sems, ring_sems) = rest[:-4], rest[-4:]
     links = Links(send_sems, recv_sems, local_sems)
-    links.enter((1, 2, 3), range(1, 8))
-    rows, model = d_mid_ref.shape
-    far_first = (6, 7, 4, 5, 2, 3, 1)
-    own_rows = pl.ds(pl.multiple_of(links.seq * rows, rows), rows)
-    strip = lambda ref, place, size: ref.at[
-        :, pl.ds(pl.multiple_of(place * size, size), size)
-    ]
-    own = links.keep(strip(d_attn_ref, links.seq, 128), grad_heads.at[own_rows, :])
-    incoming = [
-        links.send(
-            strip(d_attn_ref, links.seq_of(r), 128), grad_heads.at[own_rows, :], links.peer(r)
-        )
-        for r in far_first
-    ]
-    gather_d = Gathered(links, d_ff_ref, d_ff_all)
-    quarter_a = Quarter(links, lambda u: act_ref.at[u], act_all)
-    gather_n = Gathered(links, norm_ref, norm_all)
-    width, narrow = d_inner_all.shape[1], d_branch_all.shape[1]
-    quarter_i = Quarter(links, lambda u: strip(d_inner_ref, u, width), d_inner_all)
-    gather_b = Gathered(links, attn_ref, attn_all)
-    quarter_b = Quarter(links, lambda u: strip(d_branch_ref, u, narrow), d_branch_all)
+    rows, model = resid_ref.shape
+    block_width = up_ring.shape[2]
+    steps = w_up_ref.shape[1] // block_width
+
+    def ring(c):
+        slot = c % 2
+        columns = pl.ds(pl.multiple_of(c * block_width, block_width), block_width)
+        return (
+            pltpu.make_async_copy(w_up_ref.at[:, columns], up_ring.at[slot], ring_sems.at[slot]),
+            pltpu.make_async_copy(
+                w_down_ref.at[columns, :], down_ring.at[slot], ring_sems.at[2 + slot]
+            ),
+        )
+
+    load_out = links.keep(w_out_ref, w_out)
+    for c in (0, 1):
+        for copy in ring(c):
+            copy.start()
     loads = [
         links.keep(w_qkv_ref, w_qkv),
         links.keep(w_skip_ref, w_skip),
         links.keep(norm_a_ref, norm_a_all),
         links.keep(joined_ref, joined_all),
     ]
-    small_own[...] = small_ref[...]
+    links.enter((1, 2, 3), range(1, 8))
+
+    def modulation(piece):
+        columns = slice(piece * model, (piece + 1) * model)
+        value = jnp.broadcast_to(mod_ref[0:1, columns], (rows, model))
+        for u in range(1, utts):
+            value = jnp.where(segment_ref[...] == u, mod_ref[u : u + 1, columns], value)
+        return value
+
+    n_drop, n_keep = counts_ref[0:1, 0:1], counts_ref[0:1, 1:2]
+    dropped = dropped_ref[...]
+    loss_weight = (
+        mask_ref[...]
+        * (n_drop + n_keep)
+        * 0.5
+        * (dropped / (n_drop + 1.0) + (1.0 - dropped) / (n_keep + 1.0))
+    )
+
+    def d_out():
+        return out_grad_ref[...].astype(jnp.float32) * loss_weight
+
+    d_ff[...] = (modulation(5) * d_out()).astype(jnp.bfloat16)
+    gather_d = Gathered(links, d_ff, d_ff_all)
+    load_out.wait()
+    branch = (
+        jnp.dot(attn_ref[...], w_out[...], preferred_element_type=jnp.float32) + b_out_ref[...]
+    )
+    pieces[0] = branch
+    mid = resid_ref[...] + modulation(2) * branch
+    d_mid[...] = mid
+    unit, _ = normal_parts(mid)
+    norm_f[...] = (unit * (1.0 + modulation(4)) + modulation(3)).astype(jnp.bfloat16)
+    gather_n = Gathered(links, norm_f, norm_all)
+    ff_sum[...] = jnp.zeros_like(ff_sum)
+    d_norm[...] = jnp.zeros_like(d_norm)
+    const = math.sqrt(2.0 / math.pi)
+
+    def feed(c, _):
+        slot = c % 2
+        columns = pl.ds(pl.multiple_of(c * block_width, block_width), block_width)
+        for copy in ring(c):
+            copy.wait()
+        inner = (
+            jnp.dot(norm_f[...], up_ring[slot], preferred_element_type=jnp.float32)
+            + b_up_ref[:, columns]
+        )
+        square = inner * inner
+        slope = jnp.tanh(const * inner * (1.0 + 0.044715 * square))
+        gate = 0.5 * (1.0 + slope)
+        act_b = (inner * gate).astype(jnp.bfloat16)
+        turn = gate + 0.5 * inner * (1.0 - slope * slope) * (
+            const * (1.0 + 3.0 * 0.044715 * square)
+        )
+        here = pl.ds(pl.multiple_of(c * 128, 128), 128)
+        for u in range(4):
+            act[u, :, here] = act_b[:, u * 128 : (u + 1) * 128]
+        d_act = lax.dot_general(
+            d_ff[...], down_ring[slot], ALONG, preferred_element_type=jnp.float32
+        )
+        d_inner_b = (turn * d_act).astype(jnp.bfloat16)
+        d_inner[:, columns] = d_inner_b
+        ff_sum[...] += jnp.dot(act_b, down_ring[slot], preferred_element_type=jnp.float32)
+        d_norm[...] += lax.dot_general(
+            d_inner_b, up_ring[slot], ALONG, preferred_element_type=jnp.float32
+        )
+
+        @pl.when(c + 2 < steps)
+        def _():
+            for copy in ring(c + 2):
+                copy.start()
+
+        return 0
+
+    lax.fori_loop(0, steps, feed, 0)
+    far_first = (6, 7, 4, 5, 2, 3, 1)
+    own_rows = pl.ds(pl.multiple_of(links.seq * rows, rows), rows)
+    strip = lambda ref, place, size: ref.at[
+        :, pl.ds(pl.multiple_of(place * size, size), size)
+    ]
+    width, narrow = d_inner_all.shape[1], d_branch_all.shape[1]
     gather_d.relay()
+    quarter_a = Quarter(links, lambda u: act.at[u], act_all)
+    quarter_i = Quarter(links, lambda u: strip(d_inner, u, width), d_inner_all)
+    gather_b = Gathered(links, attn_ref, attn_all)
+    mid = d_mid[...]
+    unit, scale = normal_parts(mid)
+    d_norm_f = d_norm[...]
+    pieces[2] = d_norm_f * unit
+    d_mid_f = d_out() + normal_back(d_norm_f * (1.0 + modulation(4)), unit, scale)
+    gate_a = modulation(2)
+    d_branch[...] = (gate_a * d_mid_f).astype(jnp.bfloat16)
+    pieces[0] = pieces[0] * d_mid_f
+    d_mid[...] = d_mid_f
+    d_attn[...] = lax.dot_general(
+        d_branch[...], w_out[...], ALONG, preferred_element_type=jnp.float32
+    ).astype(jnp.bfloat16)
+    own = links.keep(strip(d_attn, links.seq, 128), grad_heads.at[own_rows, :])
+    incoming_d = [
+        links.send(
+            strip(d_attn, links.seq_of(r), 128), grad_heads.at[own_rows, :], links.peer(r)
+        )
+        for r in far_first
+    ]
+    quarter_b = Quarter(links, lambda u: strip(d_branch, u, narrow), d_branch_all)
+    ff_out = ff_sum[...] + b_down_ref[...]
+    mixed[...] = (mid + modulation(5) * ff_out).astype(jnp.bfloat16)
+    pieces[1] = d_out() * ff_out
+    small_own[...] = jnp.zeros_like(small_own)
+    small_own[4:5, :] = column_sum(d_branch[...])
+    for c in range(4):
+        small_own[5 + c : 6 + c, :] = column_sum(d_inner[:, c * model : (c + 1) * model])
+    small_own[9:10, :] = column_sum(d_ff[...])
+
+    def utterance_sums(piece, values):
+        for u in range(utts):
+            row = 10 + 6 * u + piece
+            small_own[row : row + 1, :] = jnp.sum(
+                jnp.where(segment_ref[...] == u, values, 0.0), axis=0, keepdims=True
+            )
+
+    utterance_sums(2, pieces[0])
+    utterance_sums(3, d_norm[...])
+    utterance_sums(4, pieces[2])
+    utterance_sums(5, pieces[1])
+    half = width // 2
+    down_at = lambda h: lambda u: g_down.at[
+        pl.ds(pl.multiple_of(u * 128, 128), 128), pl.ds(h * half, half)
+    ]
+    column_at = lambda ref, step, offset, size: lambda u: ref.at[
+        :, pl.ds(pl.multiple_of(u * step + offset, 128), size)
+    ]
+    wide, thin = d_qkv_all.shape[1], d_resid_all.shape[1]
+    third = wide // 2
+    plans = [
+        (act_all, d_ff_all, pl.ds(0, half), down_at(0)),
+        (act_all, d_ff_all, pl.ds(half, half), down_at(1)),
+        (norm_all, d_inner_all, pl.ds(0, half), column_at(g_up, width, 0, half)),
+        (norm_all, d_inner_all, pl.ds(half, half), column_at(g_up, width, half, half)),
+        (attn_all, d_branch_all, pl.ds(0, narrow), column_at(g_out, narrow, 0, narrow)),
+        (norm_a_all, d_qkv_all, pl.ds(0, third), column_at(g_qkv, wide, 0, third)),
+        (norm_a_all, d_qkv_all, pl.ds(third, third), column_at(g_qkv, wide, third, third)),
+        (joined_all, d_resid_all, pl.ds(0, thin), column_at(g_skip, thin, 0, thin)),
+    ]
+    shares = [
+        Share(links, left, right, columns, *tiles[4 * i : 4 * i + 4], result)
+        for i, (left, right, columns, result) in enumerate(plans)
+    ]
+    gather_n.relay()
+    gather_d.wait()
+    quarter_a.wait()
+    shares[0].start()
+    shares[1].start()
     own.wait()
-    for copy in incoming:
+    for copy in incoming_d:
         copy.wait_recv()
     dk_ref[...] = jnp.zeros_like(dk_ref)
     dv_ref[...] = jnp.zeros_like(dv_ref)
@@ -638,8 +810,6 @@
     lower = lower_half((256, 128))
     k, v = heads_ref[:, 128:256], heads_ref[:, 256:384]
     seg_k = segk_ref[...]
-    along = (((1,), (1,)), ((), ()))
-    down = (((0,), (0,)), ((), ()))
 
     def turned(values, here):
         return (
@@ -658,14 +828,14 @@
             g_own = jnp.where(mine, grad_acc, zero)
             delta = jnp.sum(jnp.where(mine, product, 0.0), axis=1, keepdims=True)
             weights = head_scores(q_own, k, seg_q, seg_k)
-            dots = lax.dot_general(g_own, v, along, preferred_element_type=jnp.float32)
+            dots = lax.dot_general(g_own, v, ALONG, preferred_element_type=jnp.float32)
             d_scores = (weights * (dots - delta)).astype(jnp.bfloat16)
             d_query.append(jnp.dot(d_scores, k, preferred_element_type=jnp.float32))
             dk_ref[...] += lax.dot_general(
-                d_scores, q_own, down, preferred_element_type=jnp.float32
+                d_scores, q_own, DOWN, preferred_element_type=jnp.float32
             )
             dv_ref[...] += lax.dot_general(
-                weights.astype(jnp.bfloat16), g_own, down, preferred_element_type=jnp.float32
+                weights.astype(jnp.bfloat16), g_own, DOWN, preferred_element_type=jnp.float32
             )
         d_heads[here, 0:128] = turned(jnp.where(first, d_query[0], d_query[1]) * 0.125, here)
         return 0
@@ -692,39 +862,11 @@
         for r in far_first
         for c in range(3)
     ]
-    half = width // 2
-    down_at = lambda h: lambda u: g_down.at[
-        pl.ds(pl.multiple_of(u * 128, 128), 128), pl.ds(h * half, half)
-    ]
-    column_at = lambda ref, step, offset, size: lambda u: ref.at[
-        :, pl.ds(pl.multiple_of(u * step + offset, 128), size)
-    ]
-    wide, thin = d_qkv_all.shape[1], d_resid_all.shape[1]
-    third = wide // 2
-    plans = [
-        (act_all, d_ff_all, pl.ds(0, half), down_at(0)),
-        (act_all, d_ff_all, pl.ds(half, half), down_at(1)),
-        (norm_all, d_inner_all, pl.ds(0, half), column_at(g_up, width, 0, half)),
-        (norm_all, d_inner_all, pl.ds(half, half), column_at(g_up, width, half, half)),
-        (attn_all, d_branch_all, pl.ds(0, narrow), column_at(g_out, narrow, 0, narrow)),
-        (norm_a_all, d_qkv_all, pl.ds(0, third), column_at(g_qkv, wide, 0, third)),
-        (norm_a_all, d_qkv_all, pl.ds(third, third), column_at(g_qkv, wide, third, third)),
-        (joined_all, d_resid_all, pl.ds(0, thin), column_at(g_skip, thin, 0, thin)),
-    ]
-    shares = [
-        Share(links, left, right, columns, *tiles[4 * i : 4 * i + 4], result)
-        for i, (left, right, columns, result) in enumerate(plans)
-    ]
-    gather_n.relay()
-    gather_d.wait()
-    quarter_a.wait()
-    shares[0].start()
-    shares[1].start()
-    gather_b.relay()
     gather_n.wait()
     quarter_i.wait()
     shares[2].start()
     shares[3].start()
+    gather_b.relay()
     gather_b.wait()
     quarter_b.wait()
     shares[4].start()
@@ -738,37 +880,19 @@
         for copy in loads:
             copy.wait()
         state["qkv"] = Quarter(links, lambda u: strip(d_qkv, u, wide), d_qkv_all)
-        d_norm = lax.dot_general(
-            d_qkv[...], w_qkv[...], along, preferred_element_type=jnp.float32
-        )
-        resid = resid_ref[...]
-        centred = resid - jnp.mean(resid, axis=1, keepdims=True)
-        scale = lax.rsqrt(jnp.mean(centred * centred, axis=1, keepdims=True) + EPSILON)
-        unit = centred * scale
-        inward = d_norm * gain_ref[...]
-        d_resid_f = d_mid_ref[...] + scale * (
-            inward
-            - jnp.mean(inward, axis=1, keepdims=True)
-            - unit * jnp.mean(inward * unit, axis=1, keepdims=True)
-        )
+        d_norm_a = lax.dot_general(
+            d_qkv[...], w_qkv[...], ALONG, preferred_element_type=jnp.float32
+        )
+        unit, scale = normal_parts(resid_ref[...])
+        d_resid_f = d_mid[...] + normal_back(d_norm_a * (1.0 + modulation(1)), unit, scale)
         rounded = d_resid_f.astype(jnp.bfloat16)
         d_resid[...] = rounded
         state["resid"] = Quarter(links, lambda u: strip(d_resid, u, thin), d_resid_all)
-        small_own[0:1, :] = jnp.sum(rounded.astype(jnp.float32), axis=0, keepdims=True)
+        small_own[0:1, :] = column_sum(rounded)
         for c in range(3):
-            small_own[1 + c : 2 + c, :] = jnp.sum(
-                d_qkv[:, c * model : (c + 1) * model].astype(jnp.float32), axis=0, keepdims=True
-            )
-        d_scale = d_norm * unit
-        for u in range((small_own.shape[0] - 10) // 6):
-            inside = segment_ref[...] == u
-            row = 10 + 6 * u
-            small_own[row : row + 1, :] = jnp.sum(
-                jnp.where(inside, d_norm, 0.0), axis=0, keepdims=True
-            )
-            small_own[row + 1 : row + 2, :] = jnp.sum(
-                jnp.where(inside, d_scale, 0.0), axis=0, keepdims=True
-            )
+            small_own[1 + c : 2 + c, :] = column_sum(d_qkv[:, c * model : (c + 1) * model])
+        utterance_sums(0, d_norm_a)
+        utterance_sums(1, d_norm_a * unit)
         state["small"] = links.send(small_own, small_got.at[0], links.peer(1))
 
     def last_shares():
@@ -783,7 +907,7 @@
             out[...] = lax.dot_general(
                 d_resid[...],
                 w_skip[pl.ds(index * model, model), :],
-                along,
+                ALONG,
                 preferred_element_type=jnp.float32,
             ).astype(jnp.bfloat16)
 
@@ -819,34 +943,46 @@
 
 
 def backward(
-    d_attn, heads, seg_col, seg_row, exact, total, cos, sin,
-    resid, gain, d_mid, segment, small,
-    d_ff, act_quarters, norm_f, d_inner, attn_b, d_branch,
-    norm_a_all, joined_all, w_qkv, w_skip,
+    attn_b, resid, mod, segment, mask, dropped, counts, out_grad, b_out, b_up, b_down,
+    heads, seg_col, seg_row, exact, total, cos, sin,
+    norm_a_all, joined_all, w_out, w_up, w_down, w_qkv, w_skip,
 ):
-    rows, model = d_attn.shape
-    frames = heads.shape[0]
-    inner = d_inner.shape[1]
+    rows, model = resid.shape
+    frames, inner = heads.shape[0], w_up.shape[1]
+    utts = mod.shape[0]
+    small = (-(-(10 + 6 * utts) // 8) * 8, model)
+    mod = jnp.pad(mod, ((0, -utts % 8), (0, 0)))
     vmem, there = everywhere(pltpu.VMEM), everywhere(pl.ANY)
     shape = jax.ShapeDtypeStruct
     bf16 = lambda *dims: pltpu.VMEM(dims, jnp.bfloat16)
     f32 = lambda *dims: pltpu.VMEM(dims, jnp.float32)
-    part = model // 8
+    part, step = model // 8, inner // 8
     return pl.pallas_call(
-        backward_kernel,
-        in_specs=[there] + [vmem] * 12 + [there] * 10,
-        out_specs=[vmem] * 8,
+        partial(backward_kernel, utts),
+        in_specs=[vmem] * 18 + [there] * 7,
+        out_specs=[vmem] * 9,
         out_shape=[
+            shape((rows, model), jnp.bfloat16),
             shape((inner // 8, model), jnp.bfloat16),
             shape((part, inner), jnp.bfloat16),
             shape((part, model), jnp.bfloat16),
             shape((part, 3 * model), jnp.bfloat16),
             shape((2 * part, model), jnp.bfloat16),
-            shape((4,) + small.shape, jnp.float32),
+            shape((4,) + small, jnp.float32),
             shape((rows, model), jnp.bfloat16),
             shape((rows, model), jnp.bfloat16),
         ],
         scratch_shapes=[
+            bf16(rows, model),
+            bf16(rows, model),
+            bf16(4, rows, inner // 4),
+            bf16(rows, inner),
+            bf16(rows, model),
+            bf16(rows, model),
+            f32(3, rows, model),
+            f32(rows, model),
+            f32(rows, model),
+            f32(rows, model),
             bf16(frames, 128),
             bf16(frames, 384),
             f32(frames, 128),
@@ -863,23 +999,27 @@
             bf16(4 * rows, 3 * model // 4),
             bf16(rows, model),
             bf16(4 * rows, model // 4),
+            bf16(2, model, step),
+            bf16(2, step, model),
+            bf16(*w_out.shape),
             bf16(*w_qkv.shape),
             bf16(*w_skip.shape),
-            f32(*small.shape),
-            f32(3, *small.shape),
-            f32(2, *small.shape),
+            f32(*small),
+            f32(3, *small),
+            f32(2, *small),
         ]
         + share_scratch(part, inner // 8) * 4
         + share_scratch(part, model // 4)
         + share_scratch(part, 3 * model // 8) * 2
         + share_scratch(2 * part, model // 4)
-        + semaphores(112),
+        + semaphores(112)
+        + [pltpu.SemaphoreType.DMA((4,))],
         compiler_params=comm_params(2),
     )(
-        d_attn, heads, seg_col, seg_row, exact, total, cos, sin,
-        resid, gain, d_mid, segment, small,
-        d_ff, act_quarters, norm_f, d_inner, attn_b, d_branch,
-        norm_a_all, joined_all, w_qkv, w_skip,
+        attn_b, resid, mod, segment, mask, dropped, counts, out_grad,
+        b_out[None, :], b_up[None, :], b_down[None, :],
+        heads, seg_col, seg_row, exact, total, cos, sin,
+        norm_a_all, joined_all, w_out, w_up, w_down, w_qkv, w_skip,
     )
 
 
@@ -997,56 +1137,20 @@
         totals_rows = jnp.transpose(totals)
         attended = weighted / totals_rows[:, :, None]
         attn_b = attended.reshape(local_rows, model_width).astype(jnp.bfloat16)
-    n_drop, n_keep = counts[0, 0], counts[0, 1]
-    loss_weight = (
-        loss_mask
-        * (n_drop + n_keep)
-        * 0.5
-        * (dropped / (n_drop + 1.0) + (1.0 - dropped) / (n_keep + 1.0))
-    )
-    branch = jnp.dot(attn_b, w_out, preferred_element_type=jnp.float32) + b_out
-    mid_state = residual + gate_a * branch
-    norm_f = modulate(mid_state, scale_f, shift_f).astype(jnp.bfloat16)
-    ff_inner = jnp.dot(norm_f, w_up, preferred_element_type=jnp.float32) + b_up
-    ff_act, gelu_pull = jax.vjp(partial(jax.nn.gelu, approximate=True), ff_inner)
-    act_b = ff_act.astype(jnp.bfloat16)
-    ff_out = jnp.dot(act_b, w_down, preferred_element_type=jnp.float32) + b_down
-    out_state = mid_state + gate_f * ff_out
-    d_out = out_grad[0].astype(jnp.float32) * loss_weight[:, None]
-    d_ff = (gate_f * d_out).astype(jnp.bfloat16)
-    d_gate_f = d_out * ff_out
-    g_b_down = jnp.sum(d_ff.astype(jnp.float32), axis=0)
-    (d_inner,) = gelu_pull(back_product(d_ff, w_down))
-    d_inner_b = d_inner.astype(jnp.bfloat16)
-    g_b_up = jnp.sum(d_inner_b.astype(jnp.float32), axis=0)
-    d_norm_f = back_product(d_inner_b, w_up)
-    _, norm_f_pull = jax.vjp(modulate, mid_state, scale_f, shift_f)
-    d_mid_norm, d_scale_f, d_shift_f = norm_f_pull(d_norm_f)
-    d_mid = d_out + d_mid_norm
-    d_branch = (gate_a * d_mid).astype(jnp.bfloat16)
-    d_gate_a = d_mid * branch
-    g_b_out = jnp.sum(d_branch.astype(jnp.float32), axis=0)
-    d_attn = back_product(d_branch, w_out)
     if fused:
-        act_quarters = jnp.transpose(act_b.reshape(local_rows, shards, 4, -1), (2, 0, 1, 3))
-        pieces = jnp.concatenate([d_gate_a, d_shift_f, d_scale_f, d_gate_f], axis=1)
-        sums = jnp.dot(jnp.transpose(member_f), pieces, precision=HIGHEST_PRECISION)
-        sums = jnp.pad(sums.reshape(-1, 4, model_width), ((0, 0), (2, 0), (0, 0)))
-        row = lambda vector: vector.reshape(-1, model_width)
-        small = jnp.concatenate(
-            [
-                jnp.zeros((4, model_width), jnp.float32),
-                row(g_b_out),
-                row(g_b_up),
-                row(g_b_down),
-                row(sums),
-            ],
-            axis=0,
-        )
-        used = small.shape[0]
-        small = jnp.pad(small, ((0, -used % 8), (0, 0)))
-        g_w_down, g_w_up, g_w_out, g_w_qkv, g_w_skip, smalls, g_frames, g_skip_in = backward(
-            d_attn.astype(jnp.bfloat16),
+        column = lambda vector: vector[:, None]
+        mixed, g_w_down, g_w_up, g_w_out, g_w_qkv, g_w_skip, smalls, g_frames, g_skip_in = backward(
+            attn_b,
+            residual,
+            mod_u,
+            column(segment),
+            column(loss_mask),
+            column(dropped),
+            counts,
+            out_grad[0],
+            b_out,
+            b_up,
+            b_down,
             qkv_heads,
             seg_col,
             seg_row,
@@ -1054,22 +1158,15 @@
             total,
             cos_all,
             sin_all,
-            residual,
-            1.0 + scale_a,
-            d_mid,
-            segment[:, None],
-            small,
-            d_ff,
-            act_quarters.reshape(4, local_rows, -1),
-            norm_f,
-            d_inner_b,
-            attn_b,
-            d_branch,
             norm_all,
             joined_all,
+            w_out,
+            w_up,
+            w_down,
             w_qkv,
             w_skip,
         )
+        used = 10 + 6 * flow_times.shape[1]
         smalls = smalls[:, :used].reshape(4, -1)
         biases = w_up.shape[1] + 6 * model_width
         bias_sum = jnp.sum(smalls[:, :biases], axis=0)
@@ -1080,6 +1177,37 @@
             grad.astype(jnp.float32) for grad in (g_w_skip, g_w_qkv, g_w_out, g_w_up, g_w_down)
         )
     else:
+        n_drop, n_keep = counts[0, 0], counts[0, 1]
+        loss_weight = (
+            loss_mask
+            * (n_drop + n_keep)
+            * 0.5
+            * (dropped / (n_drop + 1.0) + (1.0 - dropped) / (n_keep + 1.0))
+        )
+        branch = jnp.dot(attn_b, w_out, preferred_element_type=jnp.float32) + b_out
+        mid_state = residual + gate_a * branch
+        norm_f = modulate(mid_state, scale_f, shift_f).astype(jnp.bfloat16)
+        ff_inner = jnp.dot(norm_f, w_up, preferred_element_type=jnp.float32) + b_up
+        ff_act, gelu_pull = jax.vjp(partial(jax.nn.gelu, approximate=True), ff_inner)
+        act_b = ff_act.astype(jnp.bfloat16)
+        ff_out = jnp.dot(act_b, w_down, preferred_element_type=jnp.float32) + b_down
+        out_state = mid_state + gate_f * ff_out
+        d_out = out_grad[0].astype(jnp.float32) * loss_weight[:, None]
+        d_ff = (gate_f * d_out).astype(jnp.bfloat16)
+        d_gate_f = d_out * ff_out
+        g_b_down = jnp.sum(d_ff.astype(jnp.float32), axis=0)
+        (d_inner,) = gelu_pull(back_product(d_ff, w_down))
+        d_inner_b = d_inner.astype(jnp.bfloat16)
+        g_b_up = jnp.sum(d_inner_b.astype(jnp.float32), axis=0)
+        d_norm_f = back_product(d_inner_b, w_up)
+        _, norm_f_pull = jax.vjp(modulate, mid_state, scale_f, shift_f)
+        d_mid_norm, d_scale_f, d_shift_f = norm_f_pull(d_norm_f)
+        d_mid = d_out + d_mid_norm
+        d_branch = (gate_a * d_mid).astype(jnp.bfloat16)
+        d_gate_a = d_mid * branch
+        g_b_out = jnp.sum(d_branch.astype(jnp.float32), axis=0)
+        d_attn = back_product(d_branch, w_out)
+        mixed = out_state.astype(jnp.bfloat16)
         g_w_down = weight_grad(gather_left(act_b), d_ff)
         g_w_up = weight_grad(gather_left(norm_f), d_inner_b)
         g_w_out = weight_grad(gather_left(attn_b), d_branch)
@@ -1157,7 +1285,7 @@
         )
         offset += size
     return (
-        out_state.astype(jnp.bfloat16)[None],
+        mixed[None],
         g_frames[None],
         g_skip_in[None],
         g_w_skip,

time: 278 us -> 244 us (0.88); the launches traced: 274 us -> 243 us
  matrix products: 41.6 us -> 14 us
  local copies, waits for them, and re-layouts: 16.6 us -> 11.4 us
  Pallas kernels: 192 us -> 196 us
  between operations: 3.76 us -> 0.9 us
    dot_general x7 -> x0, matrix products: 24.5 us -> none  [the longest x3 13.1 us: back_product(): jnp.einsum('fo,io->fi', gradient_rows, matrix, preferred_element_type=jnp...]
    pallas_call x1, Pallas kernels: 138 us -> 142 us  [backward(): pl.pallas_call(partial(backward_kernel, utts), in_specs=[vmem] * 18 + [th...]
    dot_general x1, matrix products: 4.13 us -> 0.81 us  [local(): jnp.dot(joined, w_skip, preferred_element_type=jnp.float32) + b_skip]
    reshape x5 -> x0, local copies, waits for them, and re-layouts: 2.88 us -> none  [the longest x1 1.53 us: local(): act_b.reshape(local_rows, shards, 4, -1)]
where the time goes in v2:
time: 244 us; the launch traced here: 243 us
  Pallas kernels  196 us (80%)
  other arithmetic  21.1 us (9%)
  matrix products  14 us (6%)
  local copies, waits for them, and re-layouts  11.4 us (5%)
    pallas_call x1, Pallas kernels, backward(): pl.pallas_call(partial(backward_kernel, utts), in_specs=[vmem] * 18 + [th...  142 us
    pallas_call x1, Pallas kernels, attend(): pl.pallas_call(attend_kernel, in_specs=[there, vmem, vmem, vmem, vmem, th...  47.6 us
    convert_element_type x5, other arithmetic, local(): grad.astype(jnp.float32)  7.45 us
    dot_general x1, matrix products, local(): mod_u = jnp.dot(time_act, w_mod, preferred_element_type=jnp.float32) + b_mod  6.46 us
    pallas_call x1, Pallas kernels, rotate_pack(): pl.pallas_call(rotate_pack_kernel, grid=(blocks,), in_specs=[pl.BlockSpec...  5.92 us

profile of v2, /device:TPU:0, one launch (start us, length us, event | category | flops | bytes accessed | tf_op | source)
XLA Modules:
  0.0 243.3 jit_solution(6861703827432246155)
XLA Ops:
  0.7 0.8 reduce-window.4
  1.6 0.7 fusion.25
  2.2 0.7 select_reduce_fusion.1
  3.0 1.0 fusion.7
  4.0 0.7 multiply_bitcast_fusion
  4.8 6.5 %convolution_add_fusion = f32[3,6144]{1,0:T(4,128)S(1)} fusion(bf16[1024,6144]{1,0:T(8,128)(2,1)} %param.28, f32[6144]{0:T(1024)} %param.29, f32[3,512]{1,0:T(4,128)S(1)} %get-tuple-element.63, f32[3,512]{1,0:T(4,128)S(1)} %get-tuple-element.62), kind=kOutput, calls=%fused_computation | convolution fusion | flops 37785600 | bytes 12693504 | tf_op jit(solution)/shard_map/dot_general | solution.py:1083
  11.3 1.5 fusion.15
  12.8 0.8 add_reduce_fusion
  13.9 1.0 broadcast_add_fusion
  14.9 2.2 convolution_add_fusion.1.q_ref.k_ref.v_ref
  17.1 5.9 %shard_map.298.packed_ref = bf16[8,128,384]{2,1,0:T(8,128)(2,1)} custom-call(f32[128,3072]{1,0:T(8,128)} %convolution_add_fusion.1.q_ref.k_ref.v_ref, f32[128,3072]{1,0:T(8,128)} %convolution_add_fusion.1.q_ref.k_ref.v_ref, f32[128,3072]{1,0:T(8,128)} %convolution_add_fusion.1.q_ref.k_ref.v_ref, f32[128,128]{1,0:T(8,128)} %get-tuple-element.65.cos_ref, ...), custom_call_target="tpu_custom_call" | custom-call | tf_op jit(solution)/shard_map/pallas_call | solution.py:239
  23.6 1.4 maximum_bitcast_fusion
  25.7 1.0 copy.50.segq_ref
  27.3 47.6 %shard_map.299 = (bf16[128,1024]{1,0:T(8,128)(2,1)}, bf16[1024,384]{1,0:T(8,128)(2,1)}, f32[1024,128]{1,0:T(8,128)}, f32[1024,128]{1,0:T(8,128)}, f32[8,128]{1,0...) custom-call(bf16[8,128,384]{2,1,0:T(8,128)(2,1)} %shard_map.298.packed_ref, ...), custom_call_target="tpu_custom_call" | custom-call | tf_op jit(solution)/shard_map/pallas_call | solution.py:567
  75.8 0.7 copy.54.segment_ref
  76.5 0.8 select_reduce_fusion
  77.3 3.1 %fusion = (f32[1024,128]{1,0:T(8,128)}, f32[1024,128]{1,0:T(8,128)}) fusion(f32[128]{0:T(128)S(1)} %get-tuple-element.68, f32[128]{0:T(128)S(1)} %get-tuple-element.69, f32[1024]{0:T(1024)S(1)} %subtract_convert_fusion), kind=kLoop, calls=%fused_computation.6 | loop fusion | flops 262144 | bytes 1053696 | tf_op jit(solution)/shard_map/mul | solution.py:1034
  80.4 0.7 pad.14.mod_ref
  81.1 0.7 copy.55.dropped_ref
  81.8 142.4 %shard_map.300 = (bf16[128,1024]{1,0:T(8,128)(2,1)}, bf16[512,1024]{1,0:T(8,128)(2,1)}, bf16[128,4096]{1,0:T(8,128)(2,1)}, bf16[128,1024]{1,0:T(8,128)(2,1)}, bf...) custom-call(bf16[128,1024]{1,0:T(8,128)(2,1)} %get-tuple-element.32., ...), custom_call_target="tpu_custom_call" | custom-call | tf_op jit(solution)/shard_map/pallas_call | solution.py:960
  224.2 1.2 slice_bitcast_fusion
  225.9 0.8 multiply_reduce_fusion.1
  227.0 3.1 %fusion.13 = f32[128,6144]{1,0:T(8,128)} fusion(f32[12,6144]{1,0:T(8,128)S(1)} %reshape.166, s32[]{:T(128)S(6)} %select_n.84, f32[12,512]{1,0:T(8,128)S(1)} %get-tuple-element.61, f32[12,512]{1,0:T(8,128)S(1)} %get-tuple-element.60), kind=kOutput, calls=%fused_computation.41 | convolution fusion | flops 113255424 | bytes 3489796 | tf_op jit(solution)/shard_map/dot_general | solution.py:1275
  230.1 1.5 convert_element_type.103
  231.7 1.6 convert_element_type.104
  233.9 2.4 convert_element_type.101
  237.0 1.1 convert_element_type.99
  238.1 0.7 dynamic_slice.24
  239.4 0.8 convert_element_type.102
  240.2 1.7 copy.70
  241.9 0.7 copy.71
  242.6 0.7 copy.72
  (62 shorter events, 6.0 us)
Async XLA Ops:
  4.8 8.0 %copy-start = (bf16[2048,1024]{1,0:T(8,128)(2,1)S(1)}, bf16[2048,1024]{1,0:T(8,128)(2,1)}, u32[]{:S(2)}) copy-start(bf16[2048,1024]{1,0:T(8,128)(2,1)} %w_skip_ref.1) | copy-start | bytes 12582916
  4.8 8.0 %copy-start.4 = (bf16[1,128,1024]{2,1,0:T(8,128)(2,1)S(1)}, bf16[1,128,1024]{2,1,0:T(8,128)(2,1)}, u32[]{:S(2)}) copy-start(bf16[1,128,1024]{2,1,0:T(8,128)(2,1)} %param.20) | copy-start | bytes 786436
  4.8 8.0 %copy-start.5 = (bf16[1,128,1024]{2,1,0:T(8,128)(2,1)S(1)}, bf16[1,128,1024]{2,1,0:T(8,128)(2,1)}, u32[]{:S(2)}) copy-start(bf16[1,128,1024]{2,1,0:T(8,128)(2,1)} %param.19) | copy-start | bytes 786436
  4.8 8.0 %copy-start.11 = (f32[1024]{0:T(1024)S(1)}, f32[1024]{0:T(1024)}, u32[]{:S(2)}) copy-start(f32[1024]{0:T(1024)} %param.27) | copy-start | bytes 12292
  11.3 3.6 %slice-start = ((s8[6291456]{0:T(1024)(128)(4,1)}), s8[4194304]{0:T(1024)(128)(4,1)S(1)}, s32[]{:S(2)}) async-start(s8[6291456]{0:T(1024)(128)(4,1)} %bitcast.49), calls=%async_computation | async-start | bytes 8388608
  12.8 2.1 copy-start.12
  12.8 2.1 slice-start.1
  14.9 2.2 copy-start.1
  17.1 5.9 %copy-start.14 = (s32[1,128]{1,0:T(1,128)S(1)}, s32[1,128]{1,0:T(1,128)}, u32[]{:S(2)}) copy-start(s32[1,128]{1,0:T(1,128)} %param.24) | copy-start | bytes 1540
  17.1 9.6 %copy-start.13 = (f32[1,3]{1,0:T(1,128)S(1)}, f32[1,3]{1,0:T(1,128)}, u32[]{:S(2)}) copy-start(f32[1,3]{1,0:T(1,128)} %param.21) | copy-start | bytes 40
  25.7 1.6 copy-start.10
  224.2 5.9 %copy-start.3 = (bf16[128,4096]{1,0:T(8,128)(2,1)S(1)}, bf16[128,4096]{1,0:T(8,128)(2,1)}, u32[]{:S(2)}) copy-start(bf16[128,4096]{1,0:T(8,128)(2,1)} %get-tuple-element.47) | copy-start | bytes 3145732
  225.7 6.0 %copy-start.2 = (bf16[512,1024]{1,0:T(8,128)(2,1)S(1)}, bf16[512,1024]{1,0:T(8,128)(2,1)}, u32[]{:S(2)}) copy-start(bf16[512,1024]{1,0:T(8,128)(2,1)} %get-tuple-element.48) | copy-start | bytes 3145732
  231.7 5.3 %copy-start.6 = (bf16[256,1024]{1,0:T(8,128)(2,1)S(1)}, bf16[256,1024]{1,0:T(8,128)(2,1)}, u32[]{:S(2)}) copy-start(bf16[256,1024]{1,0:T(8,128)(2,1)} %get-tuple-element.42) | copy-start | bytes 1572868
  231.7 7.7 %copy-start.7 = (bf16[128,1024]{1,0:T(8,128)(2,1)S(1)}, bf16[128,1024]{1,0:T(8,128)(2,1)}, u32[]{:S(2)}) copy-start(bf16[128,1024]{1,0:T(8,128)(2,1)} %get-tuple-element.46) | copy-start | bytes 786436
  231.7 10.2 %copy-start.9 = (bf16[128,1024]{1,0:T(8,128)(2,1)S(1)}, bf16[128,1024]{1,0:T(8,128)(2,1)}, u32[]{:S(2)}) copy-start(bf16[128,1024]{1,0:T(8,128)(2,1)} %get-tuple-element.40) | copy-start | bytes 786436
  231.7 10.9 %copy-start.8 = (bf16[128,1024]{1,0:T(8,128)(2,1)S(1)}, bf16[128,1024]{1,0:T(8,128)(2,1)}, u32[]{:S(2)}) copy-start(bf16[128,1024]{1,0:T(8,128)(2,1)} %get-tuple-element.41) | copy-start | bytes 786436

commit v3 on v2

--- a/solution.py
+++ b/solution.py
@@ -369,20 +369,29 @@
 
 
 class Share:
-    def __init__(self, links, left, right, columns, tile, got_y, got_z1, got_z2, result):
-        self.links = links
+    def __init__(self, links, y_first, left, right, columns, tile, got_a, got_b, got_z2, result):
+        self.links, self.y_first = links, y_first
         self.left, self.right, self.columns = left, right, columns
-        self.tile, self.got_y, self.got_z1, self.got_z2 = tile, got_y, got_z1, got_z2
+        self.tile, self.got_a, self.got_b, self.got_z2 = tile, got_a, got_b, got_z2
         self.result = result
         seq = links.seq
         self.y, self.zl, self.zh = seq % 2, (seq // 2) % 2, seq // 4
-
-    def product(self, y):
+        if y_first:
+            self.a, self.b, self.peers = self.y, self.zl, (1, 2)
+        else:
+            self.a, self.b, self.peers = self.zl, self.y, (2, 1)
+
+    def place(self, zh, a, b):
+        return (zh, b, a) if self.y_first else (zh, a, b)
+
+    def product(self, a):
         rows = self.tile.shape[3]
 
-        def block(z, _):
-            base = pl.multiple_of((2 * z + y) * rows, rows)
-            self.tile[z // 2, z % 2, y] = lax.dot_general(
+        def block(step, _):
+            zh, b = step // 2, step % 2
+            here = self.place(zh, a, b)
+            base = pl.multiple_of((4 * zh + 2 * here[1] + here[2]) * rows, rows)
+            self.tile[here] = lax.dot_general(
                 self.left[:, pl.ds(base, rows)],
                 self.right[:, self.columns],
                 (((0,), (0,)), ((), ())),
@@ -393,11 +402,12 @@
         lax.fori_loop(0, 4, block, 0)
 
     def start(self):
-        self.product(1 - self.y)
-        self.sent_y = self.links.send(
-            self.tile.at[:, :, 1 - self.y], self.got_y, self.links.peer(1)
-        )
-        self.product(self.y)
+        self.product(1 - self.a)
+        given = (
+            self.tile.at[:, :, 1 - self.a] if self.y_first else self.tile.at[:, 1 - self.a]
+        )
+        self.sent_a = self.links.send(given, self.got_a, self.links.peer(self.peers[0]))
+        self.product(self.a)
 
     def add(self, index, got):
         tile = self.tile
@@ -405,31 +415,32 @@
             jnp.bfloat16
         )
 
-    def after_y(self):
-        self.sent_y.wait_recv()
+    def after_a(self):
+        self.sent_a.wait_recv()
 
         def block(zh, _):
-            self.add((zh, 1 - self.zl, self.y), self.got_y[zh, 1 - self.zl])
+            self.add(self.place(zh, self.a, 1 - self.b), self.got_a[zh, 1 - self.b])
             return 0
 
         lax.fori_loop(0, 2, block, 0)
-        self.sent_z1 = self.links.send(
-            self.tile.at[:, 1 - self.zl, self.y], self.got_z1, self.links.peer(2)
+        _, low, y = self.place(0, self.a, 1 - self.b)
+        self.sent_b = self.links.send(
+            self.tile.at[:, low, y], self.got_b, self.links.peer(self.peers[1])
         )
 
         def rest(zh, _):
-            self.add((zh, self.zl, self.y), self.got_y[zh, self.zl])
+            self.add(self.place(zh, self.a, self.b), self.got_a[zh, self.b])
             return 0
 
         lax.fori_loop(0, 2, rest, 0)
 
-    def after_z1(self):
-        self.sent_z1.wait_recv()
-        self.add((1 - self.zh, self.zl, self.y), self.got_z1[1 - self.zh])
+    def after_b(self):
+        self.sent_b.wait_recv()
+        self.add((1 - self.zh, self.zl, self.y), self.got_b[1 - self.zh])
         self.sent_z2 = self.links.send(
             self.tile.at[1 - self.zh, self.zl, self.y], self.got_z2, self.links.peer(4)
         )
-        self.add((self.zh, self.zl, self.y), self.got_z1[self.zh])
+        self.add((self.zh, self.zl, self.y), self.got_b[self.zh])
 
     def after_z2(self):
         self.sent_z2.wait_recv()
@@ -463,7 +474,7 @@
 
 
 def run_shares(shares, hooks):
-    stages = ("after_y", "after_z1", "after_z2", "relay", "wait")
+    stages = ("after_a", "after_b", "after_z2", "relay", "wait")
     for turn in range(len(shares) + len(stages) - 1):
         for hook in hooks.get(turn, ()):
             hook()
@@ -780,7 +791,7 @@
         :, pl.ds(pl.multiple_of(u * step + offset, 128), size)
     ]
     wide, thin = d_qkv_all.shape[1], d_resid_all.shape[1]
-    third = wide // 2
+    third, slim = wide // 2, thin // 2
     plans = [
         (act_all, d_ff_all, pl.ds(0, half), down_at(0)),
         (act_all, d_ff_all, pl.ds(half, half), down_at(1)),
@@ -789,10 +800,12 @@
         (attn_all, d_branch_all, pl.ds(0, narrow), column_at(g_out, narrow, 0, narrow)),
         (norm_a_all, d_qkv_all, pl.ds(0, third), column_at(g_qkv, wide, 0, third)),
         (norm_a_all, d_qkv_all, pl.ds(third, third), column_at(g_qkv, wide, third, third)),
-        (joined_all, d_resid_all, pl.ds(0, thin), column_at(g_skip, thin, 0, thin)),
-    ]
+        (joined_all, d_resid_all, pl.ds(0, slim), column_at(g_skip, thin, 0, slim)),
+        (joined_all, d_resid_all, pl.ds(slim, slim), column_at(g_skip, thin, slim, slim)),
+    ]
+    y_first = (True, False, True, False, True, False, True, False, True)
     shares = [
-        Share(links, left, right, columns, *tiles[4 * i : 4 * i + 4], result)
+        Share(links, y_first[i], left, right, columns, *tiles[4 * i : 4 * i + 4], result)
         for i, (left, right, columns, result) in enumerate(plans)
     ]
     gather_n.relay()
@@ -901,6 +914,7 @@
         shares[6].start()
         state["resid"].wait()
         shares[7].start()
+        shares[8].start()
 
     def inputs():
         for index, out in enumerate((g_frames, g_skip_in)):
@@ -1011,8 +1025,8 @@
         + share_scratch(part, inner // 8) * 4
         + share_scratch(part, model // 4)
         + share_scratch(part, 3 * model // 8) * 2
-        + share_scratch(2 * part, model // 4)
-        + semaphores(112)
+        + share_scratch(2 * part, model // 8) * 2
+        + semaphores(128)
         + [pltpu.SemaphoreType.DMA((4,))],
         compiler_params=comm_params(2),
     )(

time: 244 us -> 245 us (level)
  no operation moved by 1% of the time
where the time goes in v3:
time: 245 us; the launch traced here: 244 us
  Pallas kernels  197 us (80%)
  other arithmetic  21.1 us (9%)
  matrix products  14 us (6%)
  local copies, waits for them, and re-layouts  11.4 us (5%)
    pallas_call x1, Pallas kernels, backward(): pl.pallas_call(partial(backward_kernel, utts), in_specs=[vmem] * 18 + [th...  143 us
    pallas_call x1, Pallas kernels, attend(): pl.pallas_call(attend_kernel, in_specs=[there, vmem, vmem, vmem, vmem, th...  47.6 us
    convert_element_type x5, other arithmetic, local(): grad.astype(jnp.float32)  7.45 us
    dot_general x1, matrix products, local(): mod_u = jnp.dot(time_act, w_mod, preferred_element_type=jnp.float32) + b_mod  6.46 us
    pallas_call x1, Pallas kernels, rotate_pack(): pl.pallas_call(rotate_pack_kernel, grid=(blocks,), in_specs=[pl.BlockSpec...  5.92 us

profile of v3, /device:TPU:0, one launch (start us, length us, event | category | flops | bytes accessed | tf_op | source)
XLA Modules:
  0.0 244.4 jit_solution(13584214560984014852)
XLA Ops:
  0.7 0.8 reduce-window.4
  1.6 0.7 fusion.25
  2.2 0.7 select_reduce_fusion.1
  3.0 1.0 fusion.7
  4.0 0.7 multiply_bitcast_fusion
  4.8 6.5 %convolution_add_fusion = f32[3,6144]{1,0:T(4,128)S(1)} fusion(bf16[1024,6144]{1,0:T(8,128)(2,1)} %param.28, f32[6144]{0:T(1024)} %param.29, f32[3,512]{1,0:T(4,128)S(1)} %get-tuple-element.63, f32[3,512]{1,0:T(4,128)S(1)} %get-tuple-element.62), kind=kOutput, calls=%fused_computation | convolution fusion | flops 37785600 | bytes 12693504 | tf_op jit(solution)/shard_map/dot_general | solution.py:1097
  11.3 1.5 fusion.15
  12.8 0.8 add_reduce_fusion
  13.9 1.0 broadcast_add_fusion
  14.9 2.2 convolution_add_fusion.1.q_ref.k_ref.v_ref
  17.1 5.9 %shard_map.298.packed_ref = bf16[8,128,384]{2,1,0:T(8,128)(2,1)} custom-call(f32[128,3072]{1,0:T(8,128)} %convolution_add_fusion.1.q_ref.k_ref.v_ref, f32[128,3072]{1,0:T(8,128)} %convolution_add_fusion.1.q_ref.k_ref.v_ref, f32[128,3072]{1,0:T(8,128)} %convolution_add_fusion.1.q_ref.k_ref.v_ref, f32[128,128]{1,0:T(8,128)} %get-tuple-element.65.cos_ref, ...), custom_call_target="tpu_custom_call" | custom-call | tf_op jit(solution)/shard_map/pallas_call | solution.py:239
  23.6 1.4 maximum_bitcast_fusion
  25.7 1.0 copy.50.segq_ref
  27.3 47.6 %shard_map.299 = (bf16[128,1024]{1,0:T(8,128)(2,1)}, bf16[1024,384]{1,0:T(8,128)(2,1)}, f32[1024,128]{1,0:T(8,128)}, f32[1024,128]{1,0:T(8,128)}, f32[8,128]{1,0...) custom-call(bf16[8,128,384]{2,1,0:T(8,128)(2,1)} %shard_map.298.packed_ref, ...), custom_call_target="tpu_custom_call" | custom-call | tf_op jit(solution)/shard_map/pallas_call | solution.py:578
  75.8 0.7 copy.54.segment_ref
  76.5 0.8 select_reduce_fusion
  77.3 3.1 %fusion = (f32[1024,128]{1,0:T(8,128)}, f32[1024,128]{1,0:T(8,128)}) fusion(f32[128]{0:T(128)S(1)} %get-tuple-element.68, f32[128]{0:T(128)S(1)} %get-tuple-element.69, f32[1024]{0:T(1024)S(1)} %subtract_convert_fusion), kind=kLoop, calls=%fused_computation.6 | loop fusion | flops 262144 | bytes 1053696 | tf_op jit(solution)/shard_map/mul | solution.py:1048
  80.4 0.7 pad.14.mod_ref
  81.1 0.7 copy.55.dropped_ref
  81.8 143.5 %shard_map.300 = (bf16[128,1024]{1,0:T(8,128)(2,1)}, bf16[512,1024]{1,0:T(8,128)(2,1)}, bf16[128,4096]{1,0:T(8,128)(2,1)}, bf16[128,1024]{1,0:T(8,128)(2,1)}, bf...) custom-call(bf16[128,1024]{1,0:T(8,128)(2,1)} %get-tuple-element.32., ...), custom_call_target="tpu_custom_call" | custom-call | tf_op jit(solution)/shard_map/pallas_call | solution.py:974
  225.3 1.2 slice_bitcast_fusion
  227.0 0.8 multiply_reduce_fusion.1
  228.1 3.1 %fusion.13 = f32[128,6144]{1,0:T(8,128)} fusion(f32[12,6144]{1,0:T(8,128)S(1)} %reshape.166, s32[]{:T(128)S(6)} %select_n.84, f32[12,512]{1,0:T(8,128)S(1)} %get-tuple-element.61, f32[12,512]{1,0:T(8,128)S(1)} %get-tuple-element.60), kind=kOutput, calls=%fused_computation.41 | convolution fusion | flops 113255424 | bytes 3489796 | tf_op jit(solution)/shard_map/dot_general | solution.py:1289
  231.2 1.5 convert_element_type.103
  232.8 1.6 convert_element_type.104
  234.9 2.4 convert_element_type.101
  238.1 1.1 convert_element_type.99
  239.1 0.7 dynamic_slice.24
  240.4 0.8 convert_element_type.102
  241.3 1.7 copy.70
  243.0 0.7 copy.71
  243.7 0.7 copy.72
  (62 shorter events, 6.0 us)
Async XLA Ops:
  4.8 8.0 %copy-start = (bf16[2048,1024]{1,0:T(8,128)(2,1)S(1)}, bf16[2048,1024]{1,0:T(8,128)(2,1)}, u32[]{:S(2)}) copy-start(bf16[2048,1024]{1,0:T(8,128)(2,1)} %w_skip_ref.1) | copy-start | bytes 12582916
  4.8 8.0 %copy-start.4 = (bf16[1,128,1024]{2,1,0:T(8,128)(2,1)S(1)}, bf16[1,128,1024]{2,1,0:T(8,128)(2,1)}, u32[]{:S(2)}) copy-start(bf16[1,128,1024]{2,1,0:T(8,128)(2,1)} %param.20) | copy-start | bytes 786436
  4.8 8.0 %copy-start.5 = (bf16[1,128,1024]{2,1,0:T(8,128)(2,1)S(1)}, bf16[1,128,1024]{2,1,0:T(8,128)(2,1)}, u32[]{:S(2)}) copy-start(bf16[1,128,1024]{2,1,0:T(8,128)(2,1)} %param.19) | copy-start | bytes 786436
  4.8 8.0 %copy-start.11 = (f32[1024]{0:T(1024)S(1)}, f32[1024]{0:T(1024)}, u32[]{:S(2)}) copy-start(f32[1024]{0:T(1024)} %param.27) | copy-start | bytes 12292
  11.3 3.6 %slice-start = ((s8[6291456]{0:T(1024)(128)(4,1)}), s8[4194304]{0:T(1024)(128)(4,1)S(1)}, s32[]{:S(2)}) async-start(s8[6291456]{0:T(1024)(128)(4,1)} %bitcast.49), calls=%async_computation | async-start | bytes 8388608
  12.8 2.1 copy-start.12
  12.8 2.1 slice-start.1
  14.9 2.2 copy-start.1
  17.1 5.9 %copy-start.14 = (s32[1,128]{1,0:T(1,128)S(1)}, s32[1,128]{1,0:T(1,128)}, u32[]{:S(2)}) copy-start(s32[1,128]{1,0:T(1,128)} %param.24) | copy-start | bytes 1540
  17.1 9.6 %copy-start.13 = (f32[1,3]{1,0:T(1,128)S(1)}, f32[1,3]{1,0:T(1,128)}, u32[]{:S(2)}) copy-start(f32[1,3]{1,0:T(1,128)} %param.21) | copy-start | bytes 40
  25.7 1.6 copy-start.10
  225.3 5.9 %copy-start.3 = (bf16[128,4096]{1,0:T(8,128)(2,1)S(1)}, bf16[128,4096]{1,0:T(8,128)(2,1)}, u32[]{:S(2)}) copy-start(bf16[128,4096]{1,0:T(8,128)(2,1)} %get-tuple-element.47) | copy-start | bytes 3145732
  226.8 6.0 %copy-start.2 = (bf16[512,1024]{1,0:T(8,128)(2,1)S(1)}, bf16[512,1024]{1,0:T(8,128)(2,1)}, u32[]{:S(2)}) copy-start(bf16[512,1024]{1,0:T(8,128)(2,1)} %get-tuple-element.48) | copy-start | bytes 3145732
  232.7 5.3 %copy-start.6 = (bf16[256,1024]{1,0:T(8,128)(2,1)S(1)}, bf16[256,1024]{1,0:T(8,128)(2,1)}, u32[]{:S(2)}) copy-start(bf16[256,1024]{1,0:T(8,128)(2,1)} %get-tuple-element.42) | copy-start | bytes 1572868
  232.7 7.7 %copy-start.7 = (bf16[128,1024]{1,0:T(8,128)(2,1)S(1)}, bf16[128,1024]{1,0:T(8,128)(2,1)}, u32[]{:S(2)}) copy-start(bf16[128,1024]{1,0:T(8,128)(2,1)} %get-tuple-element.46) | copy-start | bytes 786436
  232.7 10.2 %copy-start.9 = (bf16[128,1024]{1,0:T(8,128)(2,1)S(1)}, bf16[128,1024]{1,0:T(8,128)(2,1)}, u32[]{:S(2)}) copy-start(bf16[128,1024]{1,0:T(8,128)(2,1)} %get-tuple-element.40) | copy-start | bytes 786436
  232.7 10.9 %copy-start.8 = (bf16[128,1024]{1,0:T(8,128)(2,1)S(1)}, bf16[128,1024]{1,0:T(8,128)(2,1)}, u32[]{:S(2)}) copy-start(bf16[128,1024]{1,0:T(8,128)(2,1)} %get-tuple-element.41) | copy-start | bytes 786436

commit v4 on v3

--- a/solution.py
+++ b/solution.py
@@ -354,9 +354,10 @@
 
 
 class Quarter:
-    def __init__(self, links, piece_of, target):
+    def __init__(self, links, piece_of, target, columns=None):
         rows = target.shape[0] // 4
-        slot = lambda r: target.at[pl.ds(r * rows, rows), :]
+        columns = pl.ds(0, target.shape[1]) if columns is None else columns
+        slot = lambda r: target.at[pl.ds(r * rows, rows), columns]
         self.own = links.keep(piece_of(links.utt), slot(0))
         self.copies = [
             links.send(piece_of(links.utt_of(r)), slot(r), links.mate(r)) for r in (2, 3, 1)
@@ -691,10 +692,10 @@
     d_mid[...] = mid
     unit, _ = normal_parts(mid)
     norm_f[...] = (unit * (1.0 + modulation(4)) + modulation(3)).astype(jnp.bfloat16)
-    gather_n = Gathered(links, norm_f, norm_all)
     ff_sum[...] = jnp.zeros_like(ff_sum)
     d_norm[...] = jnp.zeros_like(d_norm)
     const = math.sqrt(2.0 / math.pi)
+    width = d_inner_all.shape[1]
 
     def feed(c, _):
         slot = c % 2
@@ -713,13 +714,13 @@
             const * (1.0 + 3.0 * 0.044715 * square)
         )
         here = pl.ds(pl.multiple_of(c * 128, 128), 128)
+        d_act = lax.dot_general(
+            d_ff[...], down_ring[slot], ALONG, preferred_element_type=jnp.float32
+        )
+        d_inner_b = (turn * d_act).astype(jnp.bfloat16)
         for u in range(4):
             act[u, :, here] = act_b[:, u * 128 : (u + 1) * 128]
-        d_act = lax.dot_general(
-            d_ff[...], down_ring[slot], ALONG, preferred_element_type=jnp.float32
-        )
-        d_inner_b = (turn * d_act).astype(jnp.bfloat16)
-        d_inner[:, columns] = d_inner_b
+            d_inner[u, :, here] = d_inner_b[:, u * 128 : (u + 1) * 128]
         ff_sum[...] += jnp.dot(act_b, down_ring[slot], preferred_element_type=jnp.float32)
         d_norm[...] += lax.dot_general(
             d_inner_b, up_ring[slot], ALONG, preferred_element_type=jnp.float32
@@ -732,17 +733,21 @@
 
         return 0
 
-    lax.fori_loop(0, steps, feed, 0)
+    middle = width // 2
+    left_half, right_half = pl.ds(0, middle), pl.ds(middle, middle)
+    lax.fori_loop(0, steps // 2, feed, 0)
+    quarters_a = [Quarter(links, lambda u: act.at[u, :, left_half], act_all, left_half)]
+    lax.fori_loop(steps // 2, steps, feed, 0)
+    gather_d.relay()
+    quarters_a.append(Quarter(links, lambda u: act.at[u, :, right_half], act_all, right_half))
+    gather_n = Gathered(links, norm_f, norm_all)
     far_first = (6, 7, 4, 5, 2, 3, 1)
     own_rows = pl.ds(pl.multiple_of(links.seq * rows, rows), rows)
     strip = lambda ref, place, size: ref.at[
         :, pl.ds(pl.multiple_of(place * size, size), size)
     ]
-    width, narrow = d_inner_all.shape[1], d_branch_all.shape[1]
-    gather_d.relay()
-    quarter_a = Quarter(links, lambda u: act.at[u], act_all)
-    quarter_i = Quarter(links, lambda u: strip(d_inner, u, width), d_inner_all)
-    gather_b = Gathered(links, attn_ref, attn_all)
+    narrow = d_branch_all.shape[1]
+    quarter_i = Quarter(links, lambda u: d_inner.at[u], d_inner_all)
     mid = d_mid[...]
     unit, scale = normal_parts(mid)
     d_norm_f = d_norm[...]
@@ -763,18 +768,19 @@
         for r in far_first
     ]
     quarter_b = Quarter(links, lambda u: strip(d_branch, u, narrow), d_branch_all)
+    gather_b = Gathered(links, attn_ref, attn_all)
     ff_out = ff_sum[...] + b_down_ref[...]
     mixed[...] = (mid + modulation(5) * ff_out).astype(jnp.bfloat16)
     pieces[1] = d_out() * ff_out
     small_own[...] = jnp.zeros_like(small_own)
     small_own[4:5, :] = column_sum(d_branch[...])
     for c in range(4):
-        small_own[5 + c : 6 + c, :] = column_sum(d_inner[:, c * model : (c + 1) * model])
+        small_own[5 + c : 6 + c, :] = column_sum(d_inner[c])
     small_own[9:10, :] = column_sum(d_ff[...])
 
     def utterance_sums(piece, values):
         for u in range(utts):
-            row = 10 + 6 * u + piece
+            row = 10 + utts * piece + u
             small_own[row : row + 1, :] = jnp.sum(
                 jnp.where(segment_ref[...] == u, values, 0.0), axis=0, keepdims=True
             )
@@ -803,14 +809,15 @@
         (joined_all, d_resid_all, pl.ds(0, slim), column_at(g_skip, thin, 0, slim)),
         (joined_all, d_resid_all, pl.ds(slim, slim), column_at(g_skip, thin, slim, slim)),
     ]
-    y_first = (True, False, True, False, True, False, True, False, True)
+    y_first = (True, False, True, True, True, False, True, True, True)
     shares = [
         Share(links, y_first[i], left, right, columns, *tiles[4 * i : 4 * i + 4], result)
         for i, (left, right, columns, result) in enumerate(plans)
     ]
     gather_n.relay()
     gather_d.wait()
-    quarter_a.wait()
+    for quarter in quarters_a:
+        quarter.wait()
     shares[0].start()
     shares[1].start()
     own.wait()
@@ -990,7 +997,7 @@
             bf16(rows, model),
             bf16(rows, model),
             bf16(4, rows, inner // 4),
-            bf16(rows, inner),
+            bf16(4, rows, inner // 4),
             bf16(rows, model),
             bf16(rows, model),
             f32(3, rows, model),
@@ -1037,6 +1044,121 @@
     )
 
 
+UP = 3
+
+
+def finish_kernel(utts, shards, act_ref, *rest):
+    kept_in, wide_in, smalls_in = rest[:3], rest[3:8], rest[8]
+    kept_out, wide_out, mod_out, bias_out = rest[9:12], rest[12:17], rest[17], rest[18:24]
+    kept, wide, staged = rest[24:27], rest[27:32], rest[32:37]
+    smalls_ref, mod_stage, bias_stage, d_mod, totals, sems, load_sems = rest[37:]
+    seq = lax.axis_index("seq")
+    loads, copies = [], []
+    for source, target in zip((*wide_in, smalls_in, *kept_in), (*wide, smalls_ref, *kept)):
+        copy = pltpu.make_async_copy(source, target, load_sems.at[len(loads)])
+        copy.start()
+        loads.append(copy)
+
+    def put(source, target):
+        copy = pltpu.make_async_copy(source, target, sems.at[len(copies)])
+        copy.start()
+        copies.append(copy)
+
+    model = smalls_ref.shape[2]
+    lanes = 128
+    for place, (source, stage, target) in enumerate(zip(wide, staged, wide_out)):
+        loads[place].wait()
+        if place == UP:
+            for u in range(4):
+                for c in range(shards):
+                    stage[:, (4 * c + u) * lanes : (4 * c + u + 1) * lanes] = source[
+                        :, u * model + c * lanes : u * model + (c + 1) * lanes
+                    ].astype(jnp.float32)
+        else:
+            stage[...] = source[...].astype(jnp.float32)
+        put(stage, target)
+    groups = smalls_ref.shape[0]
+    loads[5].wait()
+    bias_sum = (
+        smalls_ref[0, 0:10] + smalls_ref[1, 0:10] + smalls_ref[2, 0:10] + smalls_ref[3, 0:10]
+    )
+    for row in range(10):
+        totals[row, 0:1] = bias_sum[row : row + 1]
+    d_mod[...] = jnp.zeros_like(d_mod)
+    for piece in range(6):
+        first = 10 + utts * piece
+        for g in range(groups):
+            d_mod[piece, g * utts : (g + 1) * utts, :] = smalls_ref[g, first : first + utts, :]
+        rows = d_mod[piece]
+        totals[10 + piece, 0:1] = jnp.sum(rows, axis=0, keepdims=True)
+        columns = slice(piece * model, (piece + 1) * model)
+        mod_stage[:, columns] = jnp.dot(
+            act_ref[...], rows, precision=HIGHEST_PRECISION, preferred_element_type=jnp.float32
+        )
+    put(mod_stage, mod_out)
+    for load, source, target in zip(loads[6:], kept, kept_out):
+        load.wait()
+        put(source, target)
+    line = model // lanes
+    first = 0
+    for place, target in enumerate(bias_out):
+        count = target.shape[1] // lanes
+        for i in range(count):
+            unit = i * line + seq if place == UP else seq * count + i
+            column = pl.multiple_of((unit % line) * lanes, lanes)
+            bias_stage[place, 0:1, i * lanes : (i + 1) * lanes] = totals[
+                first + unit // line, 0:1, pl.ds(column, lanes)
+            ]
+        first += count * shards // line
+        put(bias_stage.at[place, pl.ds(0, 1), pl.ds(0, count * lanes)], target)
+    for copy in copies:
+        copy.wait()
+
+
+def finish(shards, utts, act_own, smalls, mixed, frames, skip, grads):
+    vmem, there = everywhere(pltpu.VMEM), everywhere(pl.ANY)
+    shape = jax.ShapeDtypeStruct
+    model = smalls.shape[2]
+    own = model // shards
+    depth = act_own.shape[1]
+    mod_shape = (own, 6 * model)
+    widths = [own, 3 * own, own, 4 * own, own, 6 * own]
+    kept = (mixed, frames, skip)
+    outs = pl.pallas_call(
+        partial(finish_kernel, utts, shards),
+        in_specs=[vmem] + [there] * 9,
+        out_specs=[there] * 15,
+        out_shape=[shape(v.shape, v.dtype) for v in kept]
+        + [shape(g.shape, jnp.float32) for g in grads]
+        + [shape(mod_shape, jnp.float32)]
+        + [shape((1, w), jnp.float32) for w in widths],
+        scratch_shapes=[pltpu.VMEM(v.shape, v.dtype) for v in (*kept, *grads)]
+        + [pltpu.VMEM(g.shape, jnp.float32) for g in grads]
+        + [
+            pltpu.VMEM(smalls.shape, jnp.float32),
+            pltpu.VMEM(mod_shape, jnp.float32),
+            pltpu.VMEM((6, 8, max(widths)), jnp.float32),
+            pltpu.VMEM((6, depth, model), jnp.float32),
+            pltpu.VMEM((16, 8, model), jnp.float32),
+            pltpu.SemaphoreType.DMA((15,)),
+            pltpu.SemaphoreType.DMA((9,)),
+        ],
+        compiler_params=pltpu.CompilerParams(vmem_limit_bytes=VMEM_LIMIT),
+    )(act_own, *kept, *grads, smalls)
+    return outs[:9], [v.reshape(-1) for v in outs[9:]]
+
+
+def own_time_act(flows, seq_place, shards, model):
+    half_dim, own = model // 2, model // shards
+    column = seq_place * own + jnp.arange(own, dtype=jnp.int32)
+    inverse = jnp.exp(
+        -math.log(10000.0) * (column % half_dim).astype(jnp.float32) / half_dim
+    )
+    angles = 1000.0 * flows[None, :] * inverse[:, None]
+    wave = jnp.where((column < half_dim)[:, None], jnp.sin(angles), jnp.cos(angles))
+    return jax.nn.silu(wave).astype(jnp.bfloat16).astype(jnp.float32)
+
+
 def wide_tables(position):
     half_dim = HEAD_DIM // 2
     lane = jnp.arange(128, dtype=jnp.int32) % HEAD_DIM
@@ -1180,16 +1302,21 @@
             w_qkv,
             w_skip,
         )
-        used = 10 + 6 * flow_times.shape[1]
-        smalls = smalls[:, :used].reshape(4, -1)
-        biases = w_up.shape[1] + 6 * model_width
-        bias_sum = jnp.sum(smalls[:, :biases], axis=0)
-        d_mod_all = smalls[:, biases:].reshape(-1, 6 * model_width)
-        flow_all = flows[:, 0, : flow_times.shape[1]].reshape(-1)
-        act_all = jax.nn.silu(time_embed(flow_all, model_width)).astype(jnp.bfloat16)
-        g_w_skip, g_w_qkv, g_w_out, g_w_up, g_w_down = (
-            grad.astype(jnp.float32) for grad in (g_w_skip, g_w_qkv, g_w_out, g_w_up, g_w_down)
-        )
+        utts = flow_times.shape[1]
+        act_own = own_time_act(flows[:, 0, :utts].reshape(-1), seq_place, shards, model_width)
+        act_own = jnp.pad(act_own, ((0, 0), (0, -act_own.shape[1] % 8)))
+        wide, biases = finish(
+            shards,
+            utts,
+            act_own,
+            smalls,
+            mixed,
+            g_frames,
+            g_skip_in,
+            (g_w_skip, g_w_qkv, g_w_out, g_w_up, g_w_down),
+        )
+        mixed, g_frames, g_skip_in, g_w_skip, g_w_qkv, g_w_out, g_w_up, g_w_down, g_w_mod = wide
+        own_biases, g_b_mod = biases[:5], biases[5]
     else:
         n_drop, n_keep = counts[0, 0], counts[0, 1]
         loss_weight = (
@@ -1283,21 +1410,21 @@
         act_all = gather_ordered(time_act, 0)
         g_frames = d_joined[:, :model_width].astype(jnp.bfloat16)
         g_skip_in = d_joined[:, model_width:].astype(jnp.bfloat16)
-    act_all = act_all.astype(jnp.float32)
-    own_width = model_width // shards
-    act_own = lax.dynamic_slice_in_dim(act_all, seq_place * own_width, own_width, 1)
-    g_w_mod = jnp.dot(jnp.transpose(act_own), d_mod_all, precision=HIGHEST_PRECISION)
-    mod_width = d_mod_all.shape[1] // shards
-    g_b_mod = jnp.sum(
-        lax.dynamic_slice_in_dim(d_mod_all, seq_place * mod_width, mod_width, 1), axis=0
-    )
-    own_biases, offset = [], 0
-    for size in (b_skip.shape[0], b_qkv.shape[0], b_out.shape[0], b_up.shape[0], b_down.shape[0]):
-        width = size // shards
-        own_biases.append(
-            lax.dynamic_slice_in_dim(bias_sum, offset + seq_place * width, width, 0)
-        )
-        offset += size
+        act_all = act_all.astype(jnp.float32)
+        own_width = model_width // shards
+        act_own = lax.dynamic_slice_in_dim(act_all, seq_place * own_width, own_width, 1)
+        g_w_mod = jnp.dot(jnp.transpose(act_own), d_mod_all, precision=HIGHEST_PRECISION)
+        mod_width = d_mod_all.shape[1] // shards
+        g_b_mod = jnp.sum(
+            lax.dynamic_slice_in_dim(d_mod_all, seq_place * mod_width, mod_width, 1), axis=0
+        )
+        own_biases, offset = [], 0
+        for size in (b_skip.shape[0], b_qkv.shape[0], b_out.shape[0], b_up.shape[0], b_down.shape[0]):
+            width = size // shards
+            own_biases.append(
+                lax.dynamic_slice_in_dim(bias_sum, offset + seq_place * width, width, 0)
+            )
+            offset += size
     return (
         mixed[None],
         g_frames[None],

time: 245 us -> 244 us (level)
  Pallas kernels: 197 us -> 204 us
  local copies, waits for them, and re-layouts: 11.4 us -> 5.35 us
  other arithmetic: 21.1 us -> 16.9 us
    pallas_call x0 -> x1, Pallas kernels: none -> 8.12 us  [finish(): pl.pallas_call(partial(finish_kernel, utts, shards), in_specs=[vmem] + [t...]
    convert_element_type x5 -> x1, other arithmetic: 7.45 us -> 0.33 us  [own_time_act(): return jax.nn.silu(wave).astype(jnp.bfloat16).astype(jnp.float32)]
    unnamed x39 -> x12, local copies, waits for them, and re-layouts: 4.62 us -> 0.03 us
    dot_general x1 -> x0, matrix products: 3.12 us -> none  [local(): jnp.dot(jnp.transpose(act_own), d_mod_all, precision=HIGHEST_PRECISION)]
    dot_general x1, matrix products: 2.16 us -> 5.01 us  [local(): jnp.dot(norm_a, w_qkv, preferred_element_type=jnp.float32) + b_qkv]
    pallas_call x0 -> x2, other arithmetic: none -> 2.56 us  [finish(): pl.pallas_call(partial(finish_kernel, utts, shards), in_specs=[vmem] + [t...]
where the time goes in v4:
time: 244 us; the launch traced here: 243 us
  Pallas kernels  204 us (84%)
  other arithmetic  16.9 us (7%)
  matrix products  15.8 us (6%)
  local copies, waits for them, and re-layouts  5.35 us (2%)
    pallas_call x1, Pallas kernels, backward(): pl.pallas_call(partial(backward_kernel, utts), in_specs=[vmem] * 18 + [th...  143 us
    pallas_call x1, Pallas kernels, attend(): pl.pallas_call(attend_kernel, in_specs=[there, vmem, vmem, vmem, vmem, th...  47.6 us
    pallas_call x1, Pallas kernels, finish(): pl.pallas_call(partial(finish_kernel, utts, shards), in_specs=[vmem] + [t...  8.12 us
    dot_general x1, matrix products, local(): mod_u = jnp.dot(time_act, w_mod, preferred_element_type=jnp.float32) + b_mod  6.37 us
    pallas_call x1, Pallas kernels, rotate_pack(): pl.pallas_call(rotate_pack_kernel, grid=(blocks,), in_specs=[pl.BlockSpec...  5.73 us
    dot_general x1, matrix products, local(): jnp.dot(norm_a, w_qkv, preferred_element_type=jnp.float32) + b_qkv  5.01 us

profile of v4, /device:TPU:0, one launch (start us, length us, event | category | flops | bytes accessed | tf_op | source)
XLA Modules:
  0.0 242.9 jit_solution(8620503094304439829)
XLA Ops:
  0.6 0.8 reduce-window.4
  1.5 0.7 fusion.32
  2.1 0.7 multiply_bitcast_fusion
  2.8 0.7 convert_bitcast_fusion
  3.5 0.7 select_reduce_fusion.1
  4.3 1.3 fusion.29
  5.6 1.4 maximum_bitcast_fusion
  7.2 0.6 pad.18.counts_ref
  7.8 1.2 pad.19.flow_ref
  9.0 0.1 multiply_sine_fusion.3
  9.1 0.7 copy.57.dropped_ref
  10.1 0.6 fusion.15.mask_ref
  10.7 0.7 copy.56.segment_ref
  11.5 6.4 %convolution_add_fusion = f32[3,6144]{1,0:T(4,128)S(1)} fusion(bf16[1024,6144]{1,0:T(8,128)(2,1)} %param.28, f32[6144]{0:T(1024)} %param.29, f32[3,512]{1,0:T(4,128)S(1)} %get-tuple-element.88, f32[3,512]{1,0:T(4,128)S(1)} %get-tuple-element.87), kind=kOutput, calls=%fused_computation | convolution fusion | flops 37785600 | bytes 12693504 | tf_op jit(solution)/shard_map/dot_general | solution.py:1219
  17.8 1.0 fusion.7
  18.8 0.7 pad.22.mod_ref
  19.5 1.0 copy.50.segq_ref
  20.5 3.0 %add_reduce_fusion = (f32[128]{0:T(128)S(1)}, f32[128,1024]{1,0:T(8,128)S(1)}) fusion(f32[1024]{0:T(1024)S(1)} %copy-done.4, bf16[2048,1024]{1,0:T(8,128)(2,1)} %w_skip_ref.1, bf16[128,1024]{1,0:T(8,128)(2,1)S(1)} %bitcast.50, bf16[128,1024]{1,0:T(8,128)(2,1)S(1)} %bitcast.52), kind=kOutput, calls=%fused_computation.3 | convolution fusion | flops 538181504 | bytes 5247488 | tf_op jit(solution)/shard_map/dot_general | solution.py:1223
  23.5 0.2 multiply_reduce_fusion
  23.8 3.2 %fusion = (f32[1024,128]{1,0:T(8,128)}, f32[1024,128]{1,0:T(8,128)}) fusion(f32[128]{0:T(128)S(1)} %get-tuple-element.94, f32[128]{0:T(128)S(1)} %get-tuple-element.95, f32[1024]{0:T(1024)S(1)} %subtract_convert_fusion), kind=kLoop, calls=%fused_computation.6 | loop fusion | flops 262144 | bytes 1053696 | tf_op jit(solution)/shard_map/mul | solution.py:1170
  27.0 1.5 fusion.19
  28.5 1.0 broadcast_add_fusion
  29.5 5.0 %convolution_add_fusion.1.q_ref.k_ref.v_ref = f32[128,3072]{1,0:T(8,128)} fusion(bf16[128,1024]{1,0:T(8,128)(2,1)S(1)} %get-tuple-element.84.norm_ref, bf16[1024,3072]{1,0:T(8,128)(2,1)} %w_qkv_ref.1, f32[3072]{0:T(1024)S(1)} %copy-done.5), kind=kOutput, calls=%fused_computation.1 | convolution fusion | flops 805699584 | bytes 8138752 | tf_op jit(solution)/shard_map/dot_general | solution.py:1225
  34.5 5.7 %shard_map.298.packed_ref = bf16[8,128,384]{2,1,0:T(8,128)(2,1)} custom-call(f32[128,3072]{1,0:T(8,128)} %convolution_add_fusion.1.q_ref.k_ref.v_ref, f32[128,3072]{1,0:T(8,128)} %convolution_add_fusion.1.q_ref.k_ref.v_ref, f32[128,3072]{1,0:T(8,128)} %convolution_add_fusion.1.q_ref.k_ref.v_ref, f32[128,128]{1,0:T(8,128)} %get-tuple-element.90.cos_ref, ...), custom_call_target="tpu_custom_call" | custom-call | tf_op jit(solution)/shard_map/pallas_call | solution.py:239
  40.2 47.6 %shard_map.299 = (bf16[128,1024]{1,0:T(8,128)(2,1)}, bf16[1024,384]{1,0:T(8,128)(2,1)}, f32[1024,128]{1,0:T(8,128)}, f32[1024,128]{1,0:T(8,128)}, f32[8,128]{1,0...) custom-call(bf16[8,128,384]{2,1,0:T(8,128)(2,1)} %shard_map.298.packed_ref, ...), custom_call_target="tpu_custom_call" | custom-call | tf_op jit(solution)/shard_map/pallas_call | solution.py:579
  87.8 0.7 multiply_reduce_fusion.1
  88.6 0.3 fusion.14
  89.0 0.6 pad_convert_fusion.act_ref
  89.6 142.6 %shard_map.300 = (bf16[128,1024]{1,0:T(8,128)(2,1)}, bf16[512,1024]{1,0:T(8,128)(2,1)}, bf16[128,4096]{1,0:T(8,128)(2,1)}, bf16[128,1024]{1,0:T(8,128)(2,1)}, bf...) custom-call(bf16[128,1024]{1,0:T(8,128)(2,1)} %get-tuple-element.48., ...), custom_call_target="tpu_custom_call" | custom-call | tf_op jit(solution)/shard_map/pallas_call | solution.py:981
  232.2 8.1 %shard_map.301 = (bf16[128,1024]{1,0:T(8,128)(2,1)}, bf16[128,1024]{1,0:T(8,128)(2,1)}, bf16[128,1024]{1,0:T(8,128)(2,1)}, f32[256,1024]{1,0:T(8,128)}, f32[128,...) custom-call(f32[128,16]{1,0:T(8,128)} %pad_convert_fusion.act_ref, ...), custom_call_target="tpu_custom_call" | custom-call | tf_op jit(solution)/shard_map/pallas_call | solution.py:1127
  240.3 1.3 reduce.2
  241.6 1.3 reduce.1
  (26 shorter events, 0.6 us)
Async XLA Ops:
  7.1 12.4 %copy-start.3 = (s32[1024]{0:T(1024)}, s32[1024]{0:T(1024)S(1)}, u32[]{:S(2)}) copy-start(s32[1024]{0:T(1024)S(1)} %convert_reduce_fusion) | copy-start | bytes 12292
  11.5 9.1 %copy-start.1 = (bf16[1,128,1024]{2,1,0:T(8,128)(2,1)S(1)}, bf16[1,128,1024]{2,1,0:T(8,128)(2,1)}, u32[]{:S(2)}) copy-start(bf16[1,128,1024]{2,1,0:T(8,128)(2,1)} %param.20) | copy-start | bytes 786436
  11.5 9.1 %copy-start.2 = (bf16[1,128,1024]{2,1,0:T(8,128)(2,1)S(1)}, bf16[1,128,1024]{2,1,0:T(8,128)(2,1)}, u32[]{:S(2)}) copy-start(bf16[1,128,1024]{2,1,0:T(8,128)(2,1)} %param.19) | copy-start | bytes 786436
  11.5 9.1 %copy-start.4 = (f32[1024]{0:T(1024)S(1)}, f32[1024]{0:T(1024)}, u32[]{:S(2)}) copy-start(f32[1024]{0:T(1024)} %param.27) | copy-start | bytes 12292
  23.5 5.9 %copy-start.5 = (f32[3072]{0:T(1024)S(1)}, f32[3072]{0:T(1024)}, u32[]{:S(2)}) copy-start(f32[3072]{0:T(1024)} %param.31) | copy-start | bytes 36868
  29.5 5.0 %copy-start = (bf16[128,1024]{1,0:T(8,128)(2,1)}, bf16[128,1024]{1,0:T(8,128)(2,1)S(1)}, u32[]{:S(2)}) copy-start(bf16[128,1024]{1,0:T(8,128)(2,1)S(1)} %get-tuple-element.84.norm_ref) | copy-start | bytes 786436

commit v5 on v4

--- a/solution.py
+++ b/solution.py
@@ -221,34 +221,6 @@
 
 def lower_half(shape):
     return lax.broadcasted_iota(jnp.int32, shape, 1) % HEAD_DIM < HEAD_DIM // 2
-
-
-def rotate_pack_kernel(q_ref, k_ref, v_ref, cos_ref, sin_ref, out_ref):
-    lower = lower_half(q_ref.shape)
-    cos, sin = cos_ref[...], sin_ref[...]
-    q, k = q_ref[...], k_ref[...]
-    out_ref[0, :, 0:128] = (q * cos + swap_halves(q, lower) * sin).astype(jnp.bfloat16)
-    out_ref[0, :, 128:256] = (k * cos + swap_halves(k, lower) * sin).astype(jnp.bfloat16)
-    out_ref[0, :, 256:384] = v_ref[...].astype(jnp.bfloat16)
-
-
-def rotate_pack(qkv_full, cos, sin):
-    rows = qkv_full.shape[0]
-    blocks = qkv_full.shape[1] // 384
-    table = pl.BlockSpec((rows, 128), lambda i: (0, 0))
-    return pl.pallas_call(
-        rotate_pack_kernel,
-        grid=(blocks,),
-        in_specs=[
-            pl.BlockSpec((rows, 128), lambda i: (0, i)),
-            pl.BlockSpec((rows, 128), lambda i: (0, blocks + i)),
-            pl.BlockSpec((rows, 128), lambda i: (0, 2 * blocks + i)),
-            table,
-            table,
-        ],
-        out_specs=pl.BlockSpec((1, rows, 384), lambda i: (i, 0, 0)),
-        out_shape=jax.ShapeDtypeStruct((blocks, rows, 384), jnp.bfloat16),
-    )(qkv_full, qkv_full, qkv_full, cos, sin)
 
 
 def head_scores(q, k, seg_q, seg_k):
@@ -494,51 +466,183 @@
     )
 
 
+class Frames:
+    def __init__(self, utts, lengths_ref):
+        self.starts, self.ends, end = [], [], 0
+        for u in range(utts):
+            self.starts.append(end)
+            end = end + lengths_ref[0, u]
+            self.ends.append(end)
+
+    def segment(self, frame):
+        return sum((frame >= end).astype(jnp.int32) for end in self.ends)
+
+    def of(self, segment, values):
+        total = jnp.zeros_like(segment)
+        for u, value in enumerate(values):
+            total = jnp.where(segment == u, value, total)
+        return total
+
+
+def frame_column(first, count):
+    return first + lax.broadcasted_iota(jnp.int32, (count, 1), 0)
+
+
+def per_frame(mod_ref, segment, utts, piece, model):
+    columns = slice(piece * model, (piece + 1) * model)
+    value = jnp.broadcast_to(mod_ref[0:1, columns], (segment.shape[0], model))
+    for u in range(1, utts):
+        value = jnp.where(segment == u, mod_ref[u : u + 1, columns], value)
+    return value
+
+
+FAR_FIRST = (6, 7, 4, 5, 2, 3, 1)
+
+
 def attend_kernel(
-    packed_ref, segq_ref, segk_ref, counts_ref, flow_ref, norm_ref, frames_ref, skip_ref,
-    attn_ref, heads_ref, exact_ref, total_ref, sums_ref, flows_ref, norm_all, joined_all,
-    attn_heads, counts_got, send_sems, recv_sems, local_sems,
+    utts, lengths_ref, chars_ref, drop_ref, flow_ref, act_ref, table_ref, frames_ref, skip_ref,
+    b_skip_ref, b_mod_ref, b_qkv_ref, w_skip_ref, w_mod_ref, w_qkv_ref,
+    attn_ref, heads_ref, exact_ref, total_ref, loss_ref, flows_ref, norm_all, joined_all,
+    resid_ref, mod_ref, cos_ref, sin_ref,
+    attn_heads, counts_got, sums_ref, flow_own, packed, norm_ref, w_skip, w_mod, w_qkv,
+    send_sems, recv_sems, local_sems,
 ):
     links = Links(send_sems, recv_sems, local_sems)
+    rows, model = frames_ref.shape
+    total_rows = heads_ref.shape[0]
+    early, late = pl.ds(0, 2 * model), pl.ds(2 * model, 4 * model)
+    load_skip = links.keep(w_skip_ref, w_skip)
+    load_early = links.keep(w_mod_ref.at[:, early], w_mod.at[:, early])
+    load_qkv = links.keep(w_qkv_ref, w_qkv)
+    load_late = links.keep(w_mod_ref.at[:, late], w_mod.at[:, late])
     links.enter((1, 2, 3), range(1, 8))
-    rows = packed_ref.shape[1]
-    width = frames_ref.shape[1]
-    own_rows = pl.ds(pl.multiple_of(links.seq * rows, rows), rows)
-    own = links.keep(packed_ref.at[links.seq], heads_ref.at[own_rows, :])
-    incoming = [
-        links.send(packed_ref.at[links.seq_of(r)], heads_ref.at[own_rows, :], links.peer(r))
-        for r in (6, 7, 4, 5, 2, 3, 1)
+    gathers = [
+        Gathered(links, frames_ref, joined_all, pl.ds(0, model)),
+        Gathered(links, skip_ref, joined_all, pl.ds(model, model)),
     ]
-    flows_ref[links.utt] = flow_ref[...]
+    flow_own[...] = jnp.zeros_like(flow_own)
+    flow_own[0:1, 0:utts] = flow_ref[...]
+    flows_ref[links.utt] = flow_own[...]
     flow_copies = [
-        links.send(flow_ref, flows_ref.at[links.utt], links.mate(r)) for r in (1, 2, 3)
+        links.send(flow_own, flows_ref.at[links.utt], links.mate(r)) for r in (1, 2, 3)
     ]
-    gathers = [
-        Gathered(links, norm_ref, norm_all),
-        Gathered(links, frames_ref, joined_all, pl.ds(0, width)),
-        Gathered(links, skip_ref, joined_all, pl.ds(width, width)),
-    ]
-    sums_ref[...] = counts_ref[...]
-    for place, (target, source) in enumerate(
-        ((links.mate(1), 0), (links.mate(2), 1), (links.peer(1), 2), (links.peer(2), 3),
-         (links.peer(4), 4))
-    ):
-        counts_got[5 + place] = sums_ref[...]
-        copy = links.send(counts_got.at[5 + place], counts_got.at[source], target)
-        copy.wait_recv()
-        sums_ref[...] = sums_ref[...] + counts_got[source]
+    tables = Frames(utts, lengths_ref)
+    first_row = pl.multiple_of(links.seq * rows, rows)
+    own_rows = pl.ds(first_row, rows)
+    frame = frame_column(links.seq * rows, rows)
+    segment = tables.segment(frame)
+    position = frame - tables.of(segment, tables.starts)
+    prompt = tables.of(segment, [chars_ref[0, u] for u in range(utts)])
+    in_loss = jnp.where(position >= prompt, 1.0, 0.0)
+    across = lax.broadcasted_iota(jnp.int32, (rows, rows), 1)
+    down = lax.broadcasted_iota(jnp.int32, (rows, rows), 0)
+    dropped = jnp.sum(
+        jnp.where(across == down, drop_ref[...].astype(jnp.float32), 0.0), axis=1, keepdims=True
+    )
+    lane = lax.broadcasted_iota(jnp.int32, sums_ref.shape, 1)
+    n_drop = jnp.sum(in_loss * dropped, axis=0, keepdims=True)
+    n_keep = jnp.sum(in_loss * (1.0 - dropped), axis=0, keepdims=True)
+    sums_ref[...] = jnp.where(lane == 0, n_drop, jnp.where(lane == 1, n_keep, 0.0))
+    targets = [links.mate(1), links.mate(2), links.peer(1), links.peer(2), links.peer(4)]
+    turn = []
+
+    def count_turn():
+        place = len(turn)
+        if place > 0:
+            turn[-1].wait_recv()
+            sums_ref[...] = sums_ref[...] + counts_got[place - 1]
+        if place < 5:
+            counts_got[5 + place] = sums_ref[...]
+            turn.append(
+                links.send(counts_got.at[5 + place], counts_got.at[place], targets[place])
+            )
+
+    count_turn()
+    quarter = total_rows // 4
+    for out, kind in ((cos_ref, 0), (sin_ref, 1)):
+        for j in range(4):
+            block = table_ref[kind, :, 32 * j : 32 * (j + 1)]
+            if kind == 0:
+                wide = jnp.concatenate([block] * 4, axis=1)
+            else:
+                wide = jnp.concatenate([-block, block] * 2, axis=1)
+            out[j * quarter : (j + 1) * quarter, :] = wide
+    load_skip.wait()
+    residual = (
+        jnp.dot(frames_ref[...], w_skip[0:model, :], preferred_element_type=jnp.float32)
+        + jnp.dot(skip_ref[...], w_skip[model:, :], preferred_element_type=jnp.float32)
+        + b_skip_ref[...]
+    )
+    resid_ref[...] = residual
+    count_turn()
+
+    def modulate_columns(columns):
+        mod_ref[:, columns] = (
+            jnp.dot(act_ref[...], w_mod[:, columns], preferred_element_type=jnp.float32)
+            + b_mod_ref[:, columns]
+        )
+
+    load_early.wait()
+    modulate_columns(slice(0, 2 * model))
+    unit, _ = normal_parts(residual)
+    norm_ref[...] = (
+        unit * (1.0 + per_frame(mod_ref, segment, utts, 1, model))
+        + per_frame(mod_ref, segment, utts, 0, model)
+    ).astype(jnp.bfloat16)
+    gathers.append(Gathered(links, norm_ref, norm_all))
+    count_turn()
+    load_qkv.wait()
+    cos, sin = cos_ref[own_rows, :], sin_ref[own_rows, :]
+    lower = lower_half((rows, 128))
+
+    def project(place, base):
+        columns = pl.ds(pl.multiple_of(base + place * 128, 128), 128)
+        return (
+            jnp.dot(norm_ref[...], w_qkv[:, columns], preferred_element_type=jnp.float32)
+            + b_qkv_ref[:, columns]
+        )
+
+    def pack(place):
+        q, k = project(place, 0), project(place, model)
+        packed[place, :, 0:128] = (q * cos + swap_halves(q, lower) * sin).astype(jnp.bfloat16)
+        packed[place, :, 128:256] = (k * cos + swap_halves(k, lower) * sin).astype(jnp.bfloat16)
+        packed[place, :, 256:384] = project(place, 2 * model).astype(jnp.bfloat16)
+
+    incoming = []
+    for r in FAR_FIRST:
+        place = links.seq_of(r)
+        pack(place)
+        incoming.append(
+            links.send(packed.at[place], heads_ref.at[own_rows, :], links.peer(r))
+        )
+    pack(links.seq)
+    own = links.keep(packed.at[links.seq], heads_ref.at[own_rows, :])
+    count_turn()
+    load_late.wait()
+    modulate_columns(slice(2 * model, 6 * model))
+    count_turn()
     gathers[0].relay()
+    gathers[1].relay()
+    count_turn()
+    n_drop, n_keep = sums_ref[0:1, 0:1], sums_ref[0:1, 1:2]
+    loss_weight = (
+        in_loss
+        * (n_drop + n_keep)
+        * 0.5
+        * (dropped / (n_drop + 1.0) + (1.0 - dropped) / (n_keep + 1.0))
+    )
+    loss_ref[...] = jnp.broadcast_to(loss_weight, loss_ref.shape)
     own.wait()
     for copy in incoming:
         copy.wait_recv()
     first = lax.broadcasted_iota(jnp.int32, (256, 128), 1) < HEAD_DIM
     zero = jnp.zeros((256, 128), jnp.bfloat16)
     k, v = heads_ref[:, 128:256], heads_ref[:, 256:384]
-    seg_k = segk_ref[...]
+    seg_k = tables.segment(lax.broadcasted_iota(jnp.int32, (1, total_rows), 1))
 
     def block(step, _):
         here = pl.ds(pl.multiple_of(step * 256, 256), 256)
-        q, seg_q = heads_ref[here, 0:128], segq_ref[here, :]
+        q, seg_q = heads_ref[here, 0:128], tables.segment(frame_column(step * 256, 256))
         results = []
         for mine in (first, jnp.logical_not(first)):
             weights = head_scores(jnp.where(mine, q, zero), k, seg_q, seg_k)
@@ -552,15 +656,14 @@
         total_ref[here, :] = total
         return 0
 
-    lax.fori_loop(0, heads_ref.shape[0] // 256, block, 0)
+    lax.fori_loop(0, total_rows // 256, block, 0)
     column = attn_ref.at[:, pl.ds(pl.multiple_of(links.seq * 128, 128), 128)]
     part = lambda place: attn_heads.at[pl.ds(pl.multiple_of(place * rows, rows), rows), :]
     own = links.keep(part(links.seq), column)
     incoming = [
-        links.send(part(links.seq_of(r)), column, links.peer(r)) for r in (6, 7, 4, 5, 2, 3, 1)
+        links.send(part(links.seq_of(r)), column, links.peer(r)) for r in FAR_FIRST
     ]
-    for gather in gathers[1:]:
-        gather.relay()
+    gathers[2].relay()
     for copy in flow_copies:
         copy.wait_recv()
     own.wait()
@@ -571,32 +674,51 @@
     links.leave()
 
 
-def attend(packed, seg_col, seg_row, counts, flow, norm_a, frames, skip):
-    shards, rows, _ = packed.shape
-    total_rows, width = shards * rows, norm_a.shape[1]
-    vmem, there = everywhere(pltpu.VMEM), everywhere(pl.ANY)
+def attend(
+    lengths, chars, drop, flow, act, table, frames, skip, b_skip, b_mod, b_qkv, w_skip, w_mod,
+    w_qkv, shards,
+):
+    rows, width = frames.shape
+    total_rows = shards * rows
+    utts = flow.shape[1]
+    vmem, there, scalar = everywhere(pltpu.VMEM), everywhere(pl.ANY), everywhere(pltpu.SMEM)
     shape = jax.ShapeDtypeStruct
+    bf16 = lambda *dims: pltpu.VMEM(dims, jnp.bfloat16)
     return pl.pallas_call(
-        attend_kernel,
-        in_specs=[there, vmem, vmem, vmem, vmem, there, there, there],
-        out_specs=[vmem] * 8,
+        partial(attend_kernel, utts),
+        in_specs=[scalar] * 2 + [vmem] * 9 + [there] * 3,
+        out_specs=[vmem] * 12,
         out_shape=[
             shape((rows, width), jnp.bfloat16),
             shape((total_rows, 384), jnp.bfloat16),
             shape((total_rows, 128), jnp.float32),
             shape((total_rows, 128), jnp.float32),
-            shape(counts.shape, jnp.float32),
-            shape((4,) + flow.shape, jnp.float32),
+            shape((rows, 128), jnp.float32),
+            shape((4, 8, 128), jnp.float32),
             shape((4 * rows, width), jnp.bfloat16),
             shape((4 * rows, 2 * width), jnp.bfloat16),
+            shape((rows, width), jnp.float32),
+            shape((8, 6 * width), jnp.float32),
+            shape((total_rows, 128), jnp.float32),
+            shape((total_rows, 128), jnp.float32),
         ],
         scratch_shapes=[
-            pltpu.VMEM((total_rows, 128), jnp.bfloat16),
-            pltpu.VMEM((10,) + counts.shape, jnp.float32),
+            bf16(total_rows, 128),
+            pltpu.VMEM((10, 8, 128), jnp.float32),
+            pltpu.VMEM((8, 128), jnp.float32),
+            pltpu.VMEM((8, 128), jnp.float32),
+            bf16(shards, rows, 384),
+            bf16(rows, width),
+            bf16(*w_skip.shape),
+            bf16(*w_mod.shape),
+            bf16(*w_qkv.shape),
         ]
         + semaphores(40),
         compiler_params=comm_params(1),
-    )(packed, seg_col, seg_row, counts, flow, norm_a, frames, skip)
+    )(
+        lengths, chars, drop, flow, act, table, frames, skip,
+        b_skip[None, :], b_mod[None, :], b_qkv[None, :], w_skip, w_mod, w_qkv,
+    )
 
 
 ALONG = (((1,), (1,)), ((), ()))
@@ -622,9 +744,9 @@
 
 
 def backward_kernel(
-    utts, attn_ref, resid_ref, mod_ref, segment_ref, mask_ref, dropped_ref, counts_ref, out_grad_ref,
+    utts, lengths_ref, attn_ref, resid_ref, mod_ref, loss_ref, out_grad_ref,
     b_out_ref, b_up_ref, b_down_ref,
-    heads_ref, segq_ref, segk_ref, exact_ref, total_ref, cos_ref, sin_ref,
+    heads_ref, exact_ref, total_ref, cos_ref, sin_ref,
     norm_a_ref, joined_ref, w_out_ref, w_up_ref, w_down_ref, w_qkv_ref, w_skip_ref,
     mixed, g_down, g_up, g_out, g_qkv, g_skip, smalls, g_frames, g_skip_in,
     d_ff, norm_f, act, d_inner, d_branch, d_attn, pieces, d_mid, ff_sum, d_norm,
@@ -662,24 +784,14 @@
     ]
     links.enter((1, 2, 3), range(1, 8))
 
+    tables = Frames(utts, lengths_ref)
+    segment = tables.segment(frame_column(links.seq * rows, rows))
+
     def modulation(piece):
-        columns = slice(piece * model, (piece + 1) * model)
-        value = jnp.broadcast_to(mod_ref[0:1, columns], (rows, model))
-        for u in range(1, utts):
-            value = jnp.where(segment_ref[...] == u, mod_ref[u : u + 1, columns], value)
-        return value
-
-    n_drop, n_keep = counts_ref[0:1, 0:1], counts_ref[0:1, 1:2]
-    dropped = dropped_ref[...]
-    loss_weight = (
-        mask_ref[...]
-        * (n_drop + n_keep)
-        * 0.5
-        * (dropped / (n_drop + 1.0) + (1.0 - dropped) / (n_keep + 1.0))
-    )
+        return per_frame(mod_ref, segment, utts, piece, model)
 
     def d_out():
-        return out_grad_ref[...].astype(jnp.float32) * loss_weight
+        return out_grad_ref[...].astype(jnp.float32) * loss_ref[:, 0:1]
 
     d_ff[...] = (modulation(5) * d_out()).astype(jnp.bfloat16)
     gather_d = Gathered(links, d_ff, d_ff_all)
@@ -741,7 +853,6 @@
     gather_d.relay()
     quarters_a.append(Quarter(links, lambda u: act.at[u, :, right_half], act_all, right_half))
     gather_n = Gathered(links, norm_f, norm_all)
-    far_first = (6, 7, 4, 5, 2, 3, 1)
     own_rows = pl.ds(pl.multiple_of(links.seq * rows, rows), rows)
     strip = lambda ref, place, size: ref.at[
         :, pl.ds(pl.multiple_of(place * size, size), size)
@@ -765,7 +876,7 @@
         links.send(
             strip(d_attn, links.seq_of(r), 128), grad_heads.at[own_rows, :], links.peer(r)
         )
-        for r in far_first
+        for r in FAR_FIRST
     ]
     quarter_b = Quarter(links, lambda u: strip(d_branch, u, narrow), d_branch_all)
     gather_b = Gathered(links, attn_ref, attn_all)
@@ -782,7 +893,7 @@
         for u in range(utts):
             row = 10 + utts * piece + u
             small_own[row : row + 1, :] = jnp.sum(
-                jnp.where(segment_ref[...] == u, values, 0.0), axis=0, keepdims=True
+                jnp.where(segment == u, values, 0.0), axis=0, keepdims=True
             )
 
     utterance_sums(2, pieces[0])
@@ -829,7 +940,7 @@
     zero = jnp.zeros((256, 128), jnp.bfloat16)
     lower = lower_half((256, 128))
     k, v = heads_ref[:, 128:256], heads_ref[:, 256:384]
-    seg_k = segk_ref[...]
+    seg_k = tables.segment(lax.broadcasted_iota(jnp.int32, (1, heads_ref.shape[0]), 1))
 
     def turned(values, here):
         return (
@@ -838,7 +949,7 @@
 
     def block(step, _):
         here = pl.ds(pl.multiple_of(step * 256, 256), 256)
-        q, seg_q = heads_ref[here, 0:128], segq_ref[here, :]
+        q, seg_q = heads_ref[here, 0:128], tables.segment(frame_column(step * 256, 256))
         scaled = grad_heads[here, :].astype(jnp.float32) / total_ref[here, :]
         grad_acc = scaled.astype(jnp.bfloat16)
         product = scaled * exact_ref[here, :]
@@ -879,7 +990,7 @@
     owns = [links.keep(part(links.seq, c), home(c)) for c in range(3)]
     incoming = [
         links.send(part(links.seq_of(r), c), home(c), links.peer(r))
-        for r in far_first
+        for r in FAR_FIRST
         for c in range(3)
     ]
     gather_n.wait()
@@ -964,15 +1075,14 @@
 
 
 def backward(
-    attn_b, resid, mod, segment, mask, dropped, counts, out_grad, b_out, b_up, b_down,
-    heads, seg_col, seg_row, exact, total, cos, sin,
+    lengths, attn_b, resid, mod, loss, out_grad, b_out, b_up, b_down,
+    heads, exact, total, cos, sin,
     norm_a_all, joined_all, w_out, w_up, w_down, w_qkv, w_skip,
 ):
     rows, model = resid.shape
     frames, inner = heads.shape[0], w_up.shape[1]
-    utts = mod.shape[0]
+    utts = lengths.shape[1]
     small = (-(-(10 + 6 * utts) // 8) * 8, model)
-    mod = jnp.pad(mod, ((0, -utts % 8), (0, 0)))
     vmem, there = everywhere(pltpu.VMEM), everywhere(pl.ANY)
     shape = jax.ShapeDtypeStruct
     bf16 = lambda *dims: pltpu.VMEM(dims, jnp.bfloat16)
@@ -980,7 +1090,7 @@
     part, step = model // 8, inner // 8
     return pl.pallas_call(
         partial(backward_kernel, utts),
-        in_specs=[vmem] * 18 + [there] * 7,
+        in_specs=[everywhere(pltpu.SMEM)] + [vmem] * 13 + [there] * 7,
         out_specs=[vmem] * 9,
         out_shape=[
             shape((rows, model), jnp.bfloat16),
@@ -1037,9 +1147,9 @@
         + [pltpu.SemaphoreType.DMA((4,))],
         compiler_params=comm_params(2),
     )(
-        attn_b, resid, mod, segment, mask, dropped, counts, out_grad,
+        lengths, attn_b, resid, mod, loss, out_grad,
         b_out[None, :], b_up[None, :], b_down[None, :],
-        heads, seg_col, seg_row, exact, total, cos, sin,
+        heads, exact, total, cos, sin,
         norm_a_all, joined_all, w_out, w_up, w_down, w_qkv, w_skip,
     )
 
@@ -1159,15 +1269,30 @@
     return jax.nn.silu(wave).astype(jnp.bfloat16).astype(jnp.float32)
 
 
-def wide_tables(position):
+def compact_tables(lengths, total_rows):
     half_dim = HEAD_DIM // 2
-    lane = jnp.arange(128, dtype=jnp.int32) % HEAD_DIM
+    shape = (total_rows // 4, 128)
+    lane = lax.broadcasted_iota(jnp.int32, shape, 1)
+    frame = lax.broadcasted_iota(jnp.int32, shape, 0) + (lane // half_dim) * shape[0]
+    start, end = jnp.zeros(shape, jnp.int32), jnp.int32(0)
+    for u in range(lengths.shape[0]):
+        end = end + lengths[u]
+        start = jnp.where(frame >= end, end, start)
     inverse = jnp.exp(
         -math.log(10000.0) * 2.0 * (lane % half_dim).astype(jnp.float32) / HEAD_DIM
     )
-    angles = position.astype(jnp.float32)[:, None] * inverse[None, :]
-    sign = jnp.where(lane < half_dim, -1.0, 1.0)
-    return jnp.cos(angles), jnp.sin(angles) * sign[None, :]
+    angles = (frame - start).astype(jnp.float32) * inverse
+    return jnp.stack([jnp.cos(angles), jnp.sin(angles)])
+
+
+def padded_time_act(flow_vals, model):
+    half_dim = model // 2
+    column = jnp.arange(model, dtype=jnp.int32)
+    inverse = jnp.exp(-math.log(10000.0) * (column % half_dim).astype(jnp.float32) / half_dim)
+    flow_vals = jnp.pad(flow_vals, (0, 8 - flow_vals.shape[0]))
+    angles = 1000.0 * flow_vals[:, None] * inverse[None, :]
+    wave = jnp.where((column < half_dim)[None, :], jnp.sin(angles), jnp.cos(angles))
+    return jax.nn.silu(wave).astype(jnp.bfloat16)
 
 
 def local(
@@ -1196,50 +1321,55 @@
     shards = lax.axis_size("seq")
     seq_place = lax.axis_index("seq")
     lengths = frame_lengths[0]
-    utt_ends = jnp.cumsum(lengths)
-    segment, position, in_loss, member = frame_tables(
-        lengths, char_lengths[0], seq_place * local_rows, local_rows
-    )
-    member_f = member.astype(jnp.float32)
-    loss_mask = in_loss.astype(jnp.float32)
-    dropped = drop_mask[0].astype(jnp.float32)
-    counts = jnp.stack([jnp.sum(loss_mask * dropped), jnp.sum(loss_mask * (1.0 - dropped))])
-    counts = jnp.pad(counts[None, :], ((0, 7), (0, 126)))
     whole = model_width * 4
     fused = (
         lax.axis_size("utt") == 4
         and shards == 8
         and HEADS * HEAD_DIM == 1024
+        and model_width == 1024
         and w_up.shape[1] == whole
         and local_rows == 128
+        and flow_times.shape[1] <= 8
     )
     if not fused:
+        utt_ends = jnp.cumsum(lengths)
+        segment, position, in_loss, member = frame_tables(
+            lengths, char_lengths[0], seq_place * local_rows, local_rows
+        )
+        member_f = member.astype(jnp.float32)
+        loss_mask = in_loss.astype(jnp.float32)
+        dropped = drop_mask[0].astype(jnp.float32)
+        counts = jnp.stack([jnp.sum(loss_mask * dropped), jnp.sum(loss_mask * (1.0 - dropped))])
+        counts = jnp.pad(counts[None, :], ((0, 7), (0, 126)))
         counts = xor_sum(xor_sum(counts, "utt"), "seq")
-    time_act = jax.nn.silu(time_embed(flow_times[0], model_width)).astype(jnp.bfloat16)
-    mod_u = jnp.dot(time_act, w_mod, preferred_element_type=jnp.float32) + b_mod
-    mod_f = jnp.dot(member_f, mod_u, precision=HIGHEST_PRECISION)
-    shift_a, scale_a, gate_a, shift_f, scale_f, gate_f = jnp.split(mod_f, 6, axis=1)
-    joined = jnp.concatenate([frames_in[0], skip_in[0]], axis=1)
-    residual = jnp.dot(joined, w_skip, preferred_element_type=jnp.float32) + b_skip
-    norm_a = modulate(residual, scale_a, shift_a).astype(jnp.bfloat16)
-    qkv_full = jnp.dot(norm_a, w_qkv, preferred_element_type=jnp.float32) + b_qkv
+        time_act = jax.nn.silu(time_embed(flow_times[0], model_width)).astype(jnp.bfloat16)
+        mod_u = jnp.dot(time_act, w_mod, preferred_element_type=jnp.float32) + b_mod
+        mod_f = jnp.dot(member_f, mod_u, precision=HIGHEST_PRECISION)
+        shift_a, scale_a, gate_a, shift_f, scale_f, gate_f = jnp.split(mod_f, 6, axis=1)
+        joined = jnp.concatenate([frames_in[0], skip_in[0]], axis=1)
+        residual = jnp.dot(joined, w_skip, preferred_element_type=jnp.float32) + b_skip
+        norm_a = modulate(residual, scale_a, shift_a).astype(jnp.bfloat16)
+        qkv_full = jnp.dot(norm_a, w_qkv, preferred_element_type=jnp.float32) + b_qkv
     if fused:
-        all_segment, all_position, _, _ = frame_tables(
-            lengths, char_lengths[0], 0, local_rows * shards
-        )
-        cos_all, sin_all = wide_tables(all_position)
-        cos_own, sin_own = wide_tables(position)
-        seg_col, seg_row = all_segment[:, None], all_segment[None, :]
-        flow = jnp.pad(flow_times, ((0, 7), (0, 128 - flow_times.shape[1])))
-        attn_b, qkv_heads, exact, total, counts, flows, norm_all, joined_all = attend(
-            rotate_pack(qkv_full, cos_own, sin_own),
-            seg_col,
-            seg_row,
-            counts,
-            flow,
-            norm_a,
+        (
+            attn_b, qkv_heads, exact, total, loss, flows, norm_all, joined_all,
+            residual, mod_u, cos_all, sin_all,
+        ) = attend(
+            frame_lengths,
+            char_lengths,
+            drop_mask,
+            flow_times,
+            padded_time_act(flow_times[0], model_width),
+            compact_tables(lengths, local_rows * shards),
             frames_in[0],
             skip_in[0],
+            b_skip,
+            b_mod,
+            b_qkv,
+            w_skip,
+            w_mod,
+            w_qkv,
+            shards,
         )
     else:
         angle_cos, angle_sin = rotary_tables(position, HEAD_DIM)
@@ -1274,22 +1404,17 @@
         attended = weighted / totals_rows[:, :, None]
         attn_b = attended.reshape(local_rows, model_width).astype(jnp.bfloat16)
     if fused:
-        column = lambda vector: vector[:, None]
         mixed, g_w_down, g_w_up, g_w_out, g_w_qkv, g_w_skip, smalls, g_frames, g_skip_in = backward(
+            frame_lengths,
             attn_b,
             residual,
             mod_u,
-            column(segment),
-            column(loss_mask),
-            column(dropped),
-            counts,
+            loss,
             out_grad[0],
             b_out,
             b_up,
             b_down,
             qkv_heads,
-            seg_col,
-            seg_row,
             exact,
             total,
             cos_all,

time: 244 us -> 220 us (0.902)
  matrix products: 15.8 us -> 0 us
  other arithmetic: 16.9 us -> 7.67 us
  local copies, waits for them, and re-layouts: 5.35 us -> 1.44 us
  Pallas kernels: 204 us -> 207 us
    dot_general x4 -> x0, matrix products: 15.8 us -> none  [the longest x1 6.37 us: local(): mod_u = jnp.dot(time_act, w_mod, preferred_element_type=jnp.float32) + b_mod]
    mul x3 -> x1, other arithmetic: 4.88 us -> 0.66 us  [padded_time_act(): angles = 1000.0 * flow_vals[:, None] * inverse[None, :]]
    pallas_call x3 -> x2, Pallas kernels: 196 us -> 199 us  [the longest x1 147 us: backward(): pl.pallas_call(partial(backward_kernel, utts), in_specs=[everywhere(pltpu...]
    pad x3 -> x0, local copies, waits for them, and re-layouts: 2.53 us -> none  [the longest x1 1.25 us: local(): flow = jnp.pad(flow_times, ((0, 7), (0, 128 - flow_times.shape[1])))]
    reduce_sum x6 -> x0, other arithmetic: 2.47 us -> none  [the longest x1 1.28 us: local(): jnp.sum(loss_mask * dropped)]
where the time goes in v5:
time: 220 us; the launch traced here: 219 us
  Pallas kernels  207 us (94%)
  other arithmetic  7.67 us (3%)
  between operations  2.67 us (1%)
    pallas_call x1, Pallas kernels, backward(): pl.pallas_call(partial(backward_kernel, utts), in_specs=[everywhere(pltpu...  147 us
    pallas_call x1, Pallas kernels, attend(): pl.pallas_call(partial(attend_kernel, utts), in_specs=[scalar] * 2 + [vme...  52.4 us
    pallas_call x1, Pallas kernels, finish(): pl.pallas_call(partial(finish_kernel, utts, shards), in_specs=[vmem] + [t...  8.12 us

profile of v5, /device:TPU:0, one launch (start us, length us, event | category | flops | bytes accessed | tf_op | source)
XLA Modules:
  0.0 219.2 jit_solution(3353184769155428878)
XLA Ops:
  0.6 0.7 pad_multiply_fusion
  1.4 1.4 fusion.30
  4.7 0.8 fusion.18.act_ref
  5.5 1.2 fusion.11
  6.7 0.7 pad_maximum_fusion.table_ref
  7.4 52.4 %shard_map.298 = (bf16[128,1024]{1,0:T(8,128)(2,1)}, bf16[1024,384]{1,0:T(8,128)(2,1)}, f32[1024,128]{1,0:T(8,128)}, f32[1024,128]{1,0:T(8,128)}, f32[128,128]{1...) custom-call(s32[1,3]{1,0:T(1,128)} %lengths_ref.3, ...), custom_call_target="tpu_custom_call" | custom-call | tf_op jit(solution)/shard_map/pallas_call | solution.py:687
  59.9 0.7 multiply_reduce_fusion
  60.6 0.1 mul.109
  60.7 0.3 fusion.9
  61.0 0.6 pad_convert_fusion.act_ref
  61.6 146.9 %shard_map.299 = (bf16[128,1024]{1,0:T(8,128)(2,1)}, bf16[512,1024]{1,0:T(8,128)(2,1)}, bf16[128,4096]{1,0:T(8,128)(2,1)}, bf16[128,1024]{1,0:T(8,128)(2,1)}, bf...) custom-call(s32[1,3]{1,0:T(1,128)} %lengths_ref.3, ...), custom_call_target="tpu_custom_call" | custom-call | tf_op jit(solution)/shard_map/pallas_call | solution.py:1091
  208.5 8.1 %shard_map.300 = (bf16[128,1024]{1,0:T(8,128)(2,1)}, bf16[128,1024]{1,0:T(8,128)(2,1)}, bf16[128,1024]{1,0:T(8,128)(2,1)}, f32[256,1024]{1,0:T(8,128)}, f32[128,...) custom-call(f32[128,16]{1,0:T(8,128)} %pad_convert_fusion.act_ref, ...), custom_call_target="tpu_custom_call" | custom-call | tf_op jit(solution)/shard_map/pallas_call | solution.py:1237
  216.7 1.3 reduce.2
  218.0 1.3 reduce.1
  (7 shorter events, 0.1 us)

commit v6 on v5

--- a/solution.py
+++ b/solution.py
@@ -446,16 +446,6 @@
     ]
 
 
-def run_shares(shares, hooks):
-    stages = ("after_a", "after_b", "after_z2", "relay", "wait")
-    for turn in range(len(shares) + len(stages) - 1):
-        for hook in hooks.get(turn, ()):
-            hook()
-        for place, stage in enumerate(stages):
-            if 0 <= turn - place < len(shares):
-                getattr(shares[turn - place], stage)()
-
-
 def semaphores(count):
     return [pltpu.SemaphoreType.DMA((count,))] * 2 + [pltpu.SemaphoreType.DMA((32,))]
 
@@ -501,9 +491,10 @@
 
 def attend_kernel(
     utts, lengths_ref, chars_ref, drop_ref, flow_ref, act_ref, table_ref, frames_ref, skip_ref,
+    out_grad_ref,
     b_skip_ref, b_mod_ref, b_qkv_ref, w_skip_ref, w_mod_ref, w_qkv_ref,
     attn_ref, heads_ref, exact_ref, total_ref, loss_ref, flows_ref, norm_all, joined_all,
-    resid_ref, mod_ref, cos_ref, sin_ref,
+    resid_ref, mod_ref, cos_ref, sin_ref, d_ff_ref, d_ff_all,
     attn_heads, counts_got, sums_ref, flow_own, packed, norm_ref, w_skip, w_mod, w_qkv,
     send_sems, recv_sems, local_sems,
 ):
@@ -632,17 +623,22 @@
         * (dropped / (n_drop + 1.0) + (1.0 - dropped) / (n_keep + 1.0))
     )
     loss_ref[...] = jnp.broadcast_to(loss_weight, loss_ref.shape)
+    d_out = out_grad_ref[...].astype(jnp.float32) * loss_weight
+    d_ff_ref[...] = (per_frame(mod_ref, segment, utts, 5, model) * d_out).astype(jnp.bfloat16)
+    gathers.append(Gathered(links, d_ff_ref, d_ff_all))
     own.wait()
     for copy in incoming:
         copy.wait_recv()
-    first = lax.broadcasted_iota(jnp.int32, (256, 128), 1) < HEAD_DIM
-    zero = jnp.zeros((256, 128), jnp.bfloat16)
+    first = lax.broadcasted_iota(jnp.int32, (rows, 128), 1) < HEAD_DIM
+    zero = jnp.zeros((rows, 128), jnp.bfloat16)
     k, v = heads_ref[:, 128:256], heads_ref[:, 256:384]
     seg_k = tables.segment(lax.broadcasted_iota(jnp.int32, (1, total_rows), 1))
-
-    def block(step, _):
-        here = pl.ds(pl.multiple_of(step * 256, 256), 256)
-        q, seg_q = heads_ref[here, 0:128], tables.segment(frame_column(step * 256, 256))
+    part = lambda place: pl.ds(pl.multiple_of(place * rows, rows), rows)
+    column = attn_ref.at[:, pl.ds(pl.multiple_of(links.seq * 128, 128), 128)]
+
+    def attend_rows(place):
+        here = part(place)
+        q, seg_q = heads_ref[here, 0:128], tables.segment(frame_column(place * rows, rows))
         results = []
         for mine in (first, jnp.logical_not(first)):
             weights = head_scores(jnp.where(mine, q, zero), k, seg_q, seg_k)
@@ -654,16 +650,16 @@
         attn_heads[here, :] = attended.astype(jnp.bfloat16)
         exact_ref[here, :] = attended
         total_ref[here, :] = total
-        return 0
-
-    lax.fori_loop(0, total_rows // 256, block, 0)
-    column = attn_ref.at[:, pl.ds(pl.multiple_of(links.seq * 128, 128), 128)]
-    part = lambda place: attn_heads.at[pl.ds(pl.multiple_of(place * rows, rows), rows), :]
-    own = links.keep(part(links.seq), column)
-    incoming = [
-        links.send(part(links.seq_of(r)), column, links.peer(r)) for r in FAR_FIRST
-    ]
+
+    incoming = []
+    for r in FAR_FIRST:
+        place = links.seq_of(r)
+        attend_rows(place)
+        incoming.append(links.send(attn_heads.at[part(place), :], column, links.peer(r)))
+    attend_rows(links.seq)
+    own = links.keep(attn_heads.at[part(links.seq), :], column)
     gathers[2].relay()
+    gathers[3].relay()
     for copy in flow_copies:
         copy.wait_recv()
     own.wait()
@@ -675,8 +671,8 @@
 
 
 def attend(
-    lengths, chars, drop, flow, act, table, frames, skip, b_skip, b_mod, b_qkv, w_skip, w_mod,
-    w_qkv, shards,
+    lengths, chars, drop, flow, act, table, frames, skip, out_grad, b_skip, b_mod, b_qkv, w_skip,
+    w_mod, w_qkv, shards,
 ):
     rows, width = frames.shape
     total_rows = shards * rows
@@ -686,8 +682,8 @@
     bf16 = lambda *dims: pltpu.VMEM(dims, jnp.bfloat16)
     return pl.pallas_call(
         partial(attend_kernel, utts),
-        in_specs=[scalar] * 2 + [vmem] * 9 + [there] * 3,
-        out_specs=[vmem] * 12,
+        in_specs=[scalar] * 2 + [vmem] * 10 + [there] * 3,
+        out_specs=[vmem] * 14,
         out_shape=[
             shape((rows, width), jnp.bfloat16),
             shape((total_rows, 384), jnp.bfloat16),
@@ -701,6 +697,8 @@
             shape((8, 6 * width), jnp.float32),
             shape((total_rows, 128), jnp.float32),
             shape((total_rows, 128), jnp.float32),
+            shape((rows, width), jnp.bfloat16),
+            shape((4 * rows, width), jnp.bfloat16),
         ],
         scratch_shapes=[
             bf16(total_rows, 128),
@@ -716,7 +714,7 @@
         + semaphores(40),
         compiler_params=comm_params(1),
     )(
-        lengths, chars, drop, flow, act, table, frames, skip,
+        lengths, chars, drop, flow, act, table, frames, skip, out_grad,
         b_skip[None, :], b_mod[None, :], b_qkv[None, :], w_skip, w_mod, w_qkv,
     )
 
@@ -744,12 +742,12 @@
 
 
 def backward_kernel(
-    utts, lengths_ref, attn_ref, resid_ref, mod_ref, loss_ref, out_grad_ref,
+    utts, lengths_ref, attn_ref, resid_ref, mod_ref, loss_ref, out_grad_ref, d_ff,
     b_out_ref, b_up_ref, b_down_ref,
     heads_ref, exact_ref, total_ref, cos_ref, sin_ref,
-    norm_a_ref, joined_ref, w_out_ref, w_up_ref, w_down_ref, w_qkv_ref, w_skip_ref,
+    norm_a_ref, joined_ref, d_ff_ref, w_out_ref, w_up_ref, w_down_ref, w_qkv_ref, w_skip_ref,
     mixed, g_down, g_up, g_out, g_qkv, g_skip, smalls, g_frames, g_skip_in,
-    d_ff, norm_f, act, d_inner, d_branch, d_attn, pieces, d_mid, ff_sum, d_norm,
+    norm_f, act, d_inner, d_branch, d_attn, pieces, d_mid, ff_sum, d_norm,
     grad_heads, d_heads, dk_ref, dv_ref,
     d_ff_all, act_all, norm_all, d_inner_all, attn_all, d_branch_all,
     norm_a_all, joined_all, d_qkv, d_qkv_all, d_resid, d_resid_all,
@@ -773,6 +771,7 @@
         )
 
     load_out = links.keep(w_out_ref, w_out)
+    load_d = links.keep(d_ff_ref, d_ff_all)
     for c in (0, 1):
         for copy in ring(c):
             copy.start()
@@ -793,8 +792,6 @@
     def d_out():
         return out_grad_ref[...].astype(jnp.float32) * loss_ref[:, 0:1]
 
-    d_ff[...] = (modulation(5) * d_out()).astype(jnp.bfloat16)
-    gather_d = Gathered(links, d_ff, d_ff_all)
     load_out.wait()
     branch = (
         jnp.dot(attn_ref[...], w_out[...], preferred_element_type=jnp.float32) + b_out_ref[...]
@@ -850,7 +847,6 @@
     lax.fori_loop(0, steps // 2, feed, 0)
     quarters_a = [Quarter(links, lambda u: act.at[u, :, left_half], act_all, left_half)]
     lax.fori_loop(steps // 2, steps, feed, 0)
-    gather_d.relay()
     quarters_a.append(Quarter(links, lambda u: act.at[u, :, right_half], act_all, right_half))
     gather_n = Gathered(links, norm_f, norm_all)
     own_rows = pl.ds(pl.multiple_of(links.seq * rows, rows), rows)
@@ -920,13 +916,13 @@
         (joined_all, d_resid_all, pl.ds(0, slim), column_at(g_skip, thin, 0, slim)),
         (joined_all, d_resid_all, pl.ds(slim, slim), column_at(g_skip, thin, slim, slim)),
     ]
-    y_first = (True, False, True, True, True, False, True, True, True)
+    y_first = (True, False, True, False, True, True, True, True, True)
     shares = [
         Share(links, y_first[i], left, right, columns, *tiles[4 * i : 4 * i + 4], result)
         for i, (left, right, columns, result) in enumerate(plans)
     ]
     gather_n.relay()
-    gather_d.wait()
+    load_d.wait()
     for quarter in quarters_a:
         quarter.wait()
     shares[0].start()
@@ -995,13 +991,13 @@
     ]
     gather_n.wait()
     quarter_i.wait()
-    shares[2].start()
-    shares[3].start()
-    gather_b.relay()
-    gather_b.wait()
-    quarter_b.wait()
-    shares[4].start()
     state = {}
+
+    def output_share():
+        gather_b.relay()
+        gather_b.wait()
+        quarter_b.wait()
+        shares[4].start()
 
     def projections():
         for copy in owns:
@@ -1026,10 +1022,12 @@
         utterance_sums(1, d_norm_a * unit)
         state["small"] = links.send(small_own, small_got.at[0], links.peer(1))
 
-    def last_shares():
+    def qkv_shares():
         state["qkv"].wait()
         shares[5].start()
         shares[6].start()
+
+    def skip_shares():
         state["resid"].wait()
         shares[7].start()
         shares[8].start()
@@ -1059,25 +1057,33 @@
         mine[...] = small_sum[1] + small_got[2]
         state["spread"] = [links.send(mine, mine, links.mate(r)) for r in (2, 3, 1)]
 
-    run_shares(
-        shares,
-        {
-            1: (projections,),
-            2: (last_shares,),
-            3: (inputs, small_y),
-            4: (small_z1,),
-            5: (small_z2,),
-        },
-    )
+    stages = ("start", "after_a", "after_b", "after_z2", "relay", "wait")
+    s, a, b, z, r, w = ([getattr(share, stage) for share in shares] for stage in stages)
+    for step in (
+        s[2], a[0], s[3], a[1],
+        output_share, projections,
+        a[2], b[0],
+        qkv_shares,
+        b[1], z[0],
+        small_y, inputs,
+        z[1], a[4], a[3],
+        skip_shares, small_z1,
+        b[2], a[5], r[0], r[1], b[4], z[2],
+        small_z2,
+        z[4], w[0], w[1], a[6], b[5], r[2], r[4], b[3], z[5], b[6], a[7], z[3], r[5], z[6],
+        a[8], b[7], r[3], r[6], w[2], w[4], w[5], z[7], b[8], w[3], w[6], r[7], z[8], w[7],
+        r[8], w[8],
+    ):
+        step()
     for copy in state["spread"]:
         copy.wait_recv()
     links.leave()
 
 
 def backward(
-    lengths, attn_b, resid, mod, loss, out_grad, b_out, b_up, b_down,
+    lengths, attn_b, resid, mod, loss, out_grad, d_ff, b_out, b_up, b_down,
     heads, exact, total, cos, sin,
-    norm_a_all, joined_all, w_out, w_up, w_down, w_qkv, w_skip,
+    norm_a_all, joined_all, d_ff_all, w_out, w_up, w_down, w_qkv, w_skip,
 ):
     rows, model = resid.shape
     frames, inner = heads.shape[0], w_up.shape[1]
@@ -1090,7 +1096,7 @@
     part, step = model // 8, inner // 8
     return pl.pallas_call(
         partial(backward_kernel, utts),
-        in_specs=[everywhere(pltpu.SMEM)] + [vmem] * 13 + [there] * 7,
+        in_specs=[everywhere(pltpu.SMEM)] + [vmem] * 14 + [there] * 8,
         out_specs=[vmem] * 9,
         out_shape=[
             shape((rows, model), jnp.bfloat16),
@@ -1104,7 +1110,6 @@
             shape((rows, model), jnp.bfloat16),
         ],
         scratch_shapes=[
-            bf16(rows, model),
             bf16(rows, model),
             bf16(4, rows, inner // 4),
             bf16(4, rows, inner // 4),
@@ -1147,10 +1152,10 @@
         + [pltpu.SemaphoreType.DMA((4,))],
         compiler_params=comm_params(2),
     )(
-        lengths, attn_b, resid, mod, loss, out_grad,
+        lengths, attn_b, resid, mod, loss, out_grad, d_ff,
         b_out[None, :], b_up[None, :], b_down[None, :],
         heads, exact, total, cos, sin,
-        norm_a_all, joined_all, w_out, w_up, w_down, w_qkv, w_skip,
+        norm_a_all, joined_all, d_ff_all, w_out, w_up, w_down, w_qkv, w_skip,
     )
 
 
@@ -1353,7 +1358,7 @@
     if fused:
         (
             attn_b, qkv_heads, exact, total, loss, flows, norm_all, joined_all,
-            residual, mod_u, cos_all, sin_all,
+            residual, mod_u, cos_all, sin_all, d_ff, d_ff_all,
         ) = attend(
             frame_lengths,
             char_lengths,
@@ -1363,6 +1368,7 @@
             compact_tables(lengths, local_rows * shards),
             frames_in[0],
             skip_in[0],
+            out_grad[0],
             b_skip,
             b_mod,
             b_qkv,
@@ -1411,6 +1417,7 @@
             mod_u,
             loss,
             out_grad[0],
+            d_ff,
             b_out,
             b_up,
             b_down,
@@ -1421,6 +1428,7 @@
             sin_all,
             norm_all,
             joined_all,
+            d_ff_all,
             w_out,
             w_up,
             w_down,

time: 220 us -> 218 us (level)
  no operation moved by 1% of the time
where the time goes in v6:
time: 218 us
  Pallas kernels  206 us (94%)
  other arithmetic  7.67 us (4%)
  between operations  2.67 us (1%)
    pallas_call x1, Pallas kernels, backward(): pl.pallas_call(partial(backward_kernel, utts), in_specs=[everywhere(pltpu...  147 us
    pallas_call x1, Pallas kernels, attend(): pl.pallas_call(partial(attend_kernel, utts), in_specs=[scalar] * 2 + [vme...  51.3 us
    pallas_call x1, Pallas kernels, finish(): pl.pallas_call(partial(finish_kernel, utts, shards), in_specs=[vmem] + [t...  8.12 us

profile of v6, /device:TPU:0, one launch (start us, length us, event | category | flops | bytes accessed | tf_op | source)
XLA Modules:
  0.0 217.9 jit_solution(3075517626261356244)
XLA Ops:
  0.6 0.7 pad_multiply_fusion
  1.4 1.4 fusion.30
  4.7 0.8 fusion.18.act_ref
  5.5 1.2 fusion.11
  6.7 0.7 pad_maximum_fusion.table_ref
  7.4 51.3 %shard_map.298 = (bf16[128,1024]{1,0:T(8,128)(2,1)}, bf16[1024,384]{1,0:T(8,128)(2,1)}, f32[1024,128]{1,0:T(8,128)}, f32[1024,128]{1,0:T(8,128)}, f32[128,128]{1...) custom-call(s32[1,3]{1,0:T(1,128)} %lengths_ref.3, ...), custom_call_target="tpu_custom_call" | custom-call | tf_op jit(solution)/shard_map/pallas_call | solution.py:683
  58.7 0.7 multiply_reduce_fusion
  59.4 0.1 mul.109
  59.5 0.3 fusion.9
  59.8 0.6 pad_convert_fusion.act_ref
  60.5 146.8 %shard_map.299 = (bf16[128,1024]{1,0:T(8,128)(2,1)}, bf16[512,1024]{1,0:T(8,128)(2,1)}, bf16[128,4096]{1,0:T(8,128)(2,1)}, bf16[128,1024]{1,0:T(8,128)(2,1)}, bf...) custom-call(s32[1,3]{1,0:T(1,128)} %lengths_ref.3, ...), custom_call_target="tpu_custom_call" | custom-call | tf_op jit(solution)/shard_map/pallas_call | solution.py:1097
  207.2 8.1 %shard_map.300 = (bf16[128,1024]{1,0:T(8,128)(2,1)}, bf16[128,1024]{1,0:T(8,128)(2,1)}, bf16[128,1024]{1,0:T(8,128)(2,1)}, f32[256,1024]{1,0:T(8,128)}, f32[128,...) custom-call(f32[128,16]{1,0:T(8,128)} %pad_convert_fusion.act_ref, ...), custom_call_target="tpu_custom_call" | custom-call | tf_op jit(solution)/shard_map/pallas_call | solution.py:1242
  215.4 1.3 reduce.2
  216.6 1.3 reduce.1
  (7 shorter events, 0.1 us)

commit v7 on v6

--- a/solution.py
+++ b/solution.py
@@ -357,11 +357,10 @@
     def place(self, zh, a, b):
         return (zh, b, a) if self.y_first else (zh, a, b)
 
-    def product(self, a):
+    def product(self, zh, a):
         rows = self.tile.shape[3]
 
-        def block(step, _):
-            zh, b = step // 2, step % 2
+        def block(b, _):
             here = self.place(zh, a, b)
             base = pl.multiple_of((4 * zh + 2 * here[1] + here[2]) * rows, rows)
             self.tile[here] = lax.dot_general(
@@ -372,15 +371,30 @@
             ).astype(jnp.bfloat16)
             return 0
 
-        lax.fori_loop(0, 4, block, 0)
+        lax.fori_loop(0, 2, block, 0)
+
+    def give(self, zh):
+        self.product(zh, 1 - self.a)
+        given = self.tile.at[zh, :, 1 - self.a] if self.y_first else self.tile.at[zh, 1 - self.a]
+        self.sent_a.append(
+            self.links.send(given, self.got_a.at[zh], self.links.peer(self.peers[0]))
+        )
+
+    def start_far(self):
+        self.sent_a, self.sent_b = [], []
+        self.give(1 - self.zh)
+        self.product(1 - self.zh, self.a)
+
+    def start_near(self):
+        self.give(self.zh)
+        self.product(self.zh, self.a)
 
     def start(self):
-        self.product(1 - self.a)
-        given = (
-            self.tile.at[:, :, 1 - self.a] if self.y_first else self.tile.at[:, 1 - self.a]
-        )
-        self.sent_a = self.links.send(given, self.got_a, self.links.peer(self.peers[0]))
-        self.product(self.a)
+        self.sent_a, self.sent_b = [], []
+        self.give(1 - self.zh)
+        self.give(self.zh)
+        self.product(1 - self.zh, self.a)
+        self.product(self.zh, self.a)
 
     def add(self, index, got):
         tile = self.tile
@@ -389,30 +403,26 @@
         )
 
     def after_a(self):
-        self.sent_a.wait_recv()
-
-        def block(zh, _):
-            self.add(self.place(zh, self.a, 1 - self.b), self.got_a[zh, 1 - self.b])
-            return 0
-
-        lax.fori_loop(0, 2, block, 0)
-        _, low, y = self.place(0, self.a, 1 - self.b)
-        self.sent_b = self.links.send(
-            self.tile.at[:, low, y], self.got_b, self.links.peer(self.peers[1])
-        )
-
-        def rest(zh, _):
+        halves = (1 - self.zh, self.zh)
+        for sent, zh in zip(self.sent_a, halves):
+            sent.wait_recv()
+            here = self.place(zh, self.a, 1 - self.b)
+            self.add(here, self.got_a[zh, 1 - self.b])
+            self.sent_b.append(
+                self.links.send(
+                    self.tile.at[here], self.got_b.at[zh], self.links.peer(self.peers[1])
+                )
+            )
+        for zh in halves:
             self.add(self.place(zh, self.a, self.b), self.got_a[zh, self.b])
-            return 0
-
-        lax.fori_loop(0, 2, rest, 0)
 
     def after_b(self):
-        self.sent_b.wait_recv()
+        self.sent_b[0].wait_recv()
         self.add((1 - self.zh, self.zl, self.y), self.got_b[1 - self.zh])
         self.sent_z2 = self.links.send(
             self.tile.at[1 - self.zh, self.zl, self.y], self.got_z2, self.links.peer(4)
         )
+        self.sent_b[1].wait_recv()
         self.add((self.zh, self.zl, self.y), self.got_b[self.zh])
 
     def after_z2(self):
@@ -751,7 +761,7 @@
     grad_heads, d_heads, dk_ref, dv_ref,
     d_ff_all, act_all, norm_all, d_inner_all, attn_all, d_branch_all,
     norm_a_all, joined_all, d_qkv, d_qkv_all, d_resid, d_resid_all,
-    up_ring, down_ring, w_out, w_qkv, w_skip, small_own, small_got, small_sum,
+    up_ring, down_ring, w_out, w_qkv, w_skip, small_own, small_got, small_out,
     *rest,
 ):
     tiles, (send_sems, recv_sems, local_sems, ring_sems) = rest[:-4], rest[-4:]
@@ -760,9 +770,14 @@
     block_width = up_ring.shape[2]
     steps = w_up_ref.shape[1] // block_width
 
+    zh = links.seq // 4
+
+    def chunk(c):
+        return (c + (1 - zh) * (steps // 2)) % steps
+
     def ring(c):
         slot = c % 2
-        columns = pl.ds(pl.multiple_of(c * block_width, block_width), block_width)
+        columns = pl.ds(pl.multiple_of(chunk(c) * block_width, block_width), block_width)
         return (
             pltpu.make_async_copy(w_up_ref.at[:, columns], up_ring.at[slot], ring_sems.at[slot]),
             pltpu.make_async_copy(
@@ -808,7 +823,7 @@
 
     def feed(c, _):
         slot = c % 2
-        columns = pl.ds(pl.multiple_of(c * block_width, block_width), block_width)
+        columns = pl.ds(pl.multiple_of(chunk(c) * block_width, block_width), block_width)
         for copy in ring(c):
             copy.wait()
         inner = (
@@ -822,7 +837,7 @@
         turn = gate + 0.5 * inner * (1.0 - slope * slope) * (
             const * (1.0 + 3.0 * 0.044715 * square)
         )
-        here = pl.ds(pl.multiple_of(c * 128, 128), 128)
+        here = pl.ds(pl.multiple_of(chunk(c) * 128, 128), 128)
         d_act = lax.dot_general(
             d_ff[...], down_ring[slot], ALONG, preferred_element_type=jnp.float32
         )
@@ -843,11 +858,12 @@
         return 0
 
     middle = width // 2
-    left_half, right_half = pl.ds(0, middle), pl.ds(middle, middle)
+    half_at = lambda place: pl.ds(pl.multiple_of(place * middle, middle), middle)
+    far_half, near_half = half_at(1 - zh), half_at(zh)
     lax.fori_loop(0, steps // 2, feed, 0)
-    quarters_a = [Quarter(links, lambda u: act.at[u, :, left_half], act_all, left_half)]
+    quarters_a = [Quarter(links, lambda u: act.at[u, :, far_half], act_all, far_half)]
     lax.fori_loop(steps // 2, steps, feed, 0)
-    quarters_a.append(Quarter(links, lambda u: act.at[u, :, right_half], act_all, right_half))
+    quarters_a.append(Quarter(links, lambda u: act.at[u, :, near_half], act_all, near_half))
     gather_n = Gathered(links, norm_f, norm_all)
     own_rows = pl.ds(pl.multiple_of(links.seq * rows, rows), rows)
     strip = lambda ref, place, size: ref.at[
@@ -876,26 +892,6 @@
     ]
     quarter_b = Quarter(links, lambda u: strip(d_branch, u, narrow), d_branch_all)
     gather_b = Gathered(links, attn_ref, attn_all)
-    ff_out = ff_sum[...] + b_down_ref[...]
-    mixed[...] = (mid + modulation(5) * ff_out).astype(jnp.bfloat16)
-    pieces[1] = d_out() * ff_out
-    small_own[...] = jnp.zeros_like(small_own)
-    small_own[4:5, :] = column_sum(d_branch[...])
-    for c in range(4):
-        small_own[5 + c : 6 + c, :] = column_sum(d_inner[c])
-    small_own[9:10, :] = column_sum(d_ff[...])
-
-    def utterance_sums(piece, values):
-        for u in range(utts):
-            row = 10 + utts * piece + u
-            small_own[row : row + 1, :] = jnp.sum(
-                jnp.where(segment == u, values, 0.0), axis=0, keepdims=True
-            )
-
-    utterance_sums(2, pieces[0])
-    utterance_sums(3, d_norm[...])
-    utterance_sums(4, pieces[2])
-    utterance_sums(5, pieces[1])
     half = width // 2
     down_at = lambda h: lambda u: g_down.at[
         pl.ds(pl.multiple_of(u * 128, 128), 128), pl.ds(h * half, half)
@@ -916,17 +912,39 @@
         (joined_all, d_resid_all, pl.ds(0, slim), column_at(g_skip, thin, 0, slim)),
         (joined_all, d_resid_all, pl.ds(slim, slim), column_at(g_skip, thin, slim, slim)),
     ]
-    y_first = (True, False, True, False, True, True, True, True, True)
+    y_first = (True, False, True, True, True, True, True, True, True)
     shares = [
         Share(links, y_first[i], left, right, columns, *tiles[4 * i : 4 * i + 4], result)
         for i, (left, right, columns, result) in enumerate(plans)
     ]
+    load_d.wait()
+    quarters_a[0].wait()
+    shares[0].start_far()
+    shares[1].start_far()
+    ff_out = ff_sum[...] + b_down_ref[...]
+    mixed[...] = (mid + modulation(5) * ff_out).astype(jnp.bfloat16)
+    pieces[1] = d_out() * ff_out
+    small_own[...] = jnp.zeros_like(small_own)
+    small_own[4:5, :] = column_sum(d_branch[...])
+    for c in range(4):
+        small_own[5 + c : 6 + c, :] = column_sum(d_inner[c])
+    small_own[9:10, :] = column_sum(d_ff[...])
+
+    def utterance_sums(piece, values):
+        for u in range(utts):
+            row = 10 + utts * piece + u
+            small_own[row : row + 1, :] = jnp.sum(
+                jnp.where(segment == u, values, 0.0), axis=0, keepdims=True
+            )
+
+    utterance_sums(2, pieces[0])
+    utterance_sums(3, d_norm[...])
+    utterance_sums(4, pieces[2])
+    utterance_sums(5, pieces[1])
     gather_n.relay()
-    load_d.wait()
-    for quarter in quarters_a:
-        quarter.wait()
-    shares[0].start()
-    shares[1].start()
+    quarters_a[1].wait()
+    shares[0].start_near()
+    shares[1].start_near()
     own.wait()
     for copy in incoming_d:
         copy.wait_recv()
@@ -1020,7 +1038,8 @@
             small_own[1 + c : 2 + c, :] = column_sum(d_qkv[:, c * model : (c + 1) * model])
         utterance_sums(0, d_norm_a)
         utterance_sums(1, d_norm_a * unit)
-        state["small"] = links.send(small_own, small_got.at[0], links.peer(1))
+        small_out[0] = small_own[...].astype(jnp.bfloat16)
+        state["small"] = links.send(small_out.at[0], small_got.at[0], links.peer(1))
 
     def qkv_shares():
         state["qkv"].wait()
@@ -1043,36 +1062,39 @@
 
     def small_y():
         state["small"].wait_recv()
-        small_sum[0] = small_own[...] + small_got[0]
-        state["small"] = links.send(small_sum.at[0], small_got.at[1], links.peer(2))
+        small_own[...] += small_got[0].astype(jnp.float32)
+        small_out[1] = small_own[...].astype(jnp.bfloat16)
+        state["small"] = links.send(small_out.at[1], small_got.at[1], links.peer(2))
 
     def small_z1():
         state["small"].wait_recv()
-        small_sum[1] = small_sum[0] + small_got[1]
-        state["small"] = links.send(small_sum.at[1], small_got.at[2], links.peer(4))
+        small_own[...] += small_got[1].astype(jnp.float32)
+        small_out[2] = small_own[...].astype(jnp.bfloat16)
+        state["small"] = links.send(small_out.at[2], small_got.at[2], links.peer(4))
 
     def small_z2():
         state["small"].wait_recv()
         mine = smalls.at[links.utt]
-        mine[...] = small_sum[1] + small_got[2]
+        mine[...] = (small_own[...] + small_got[2].astype(jnp.float32)).astype(jnp.bfloat16)
         state["spread"] = [links.send(mine, mine, links.mate(r)) for r in (2, 3, 1)]
 
     stages = ("start", "after_a", "after_b", "after_z2", "relay", "wait")
     s, a, b, z, r, w = ([getattr(share, stage) for share in shares] for stage in stages)
     for step in (
-        s[2], a[0], s[3], a[1],
+        s[2], a[0], a[1], s[3],
         output_share, projections,
-        a[2], b[0],
+        a[2], b[0], b[1],
         qkv_shares,
-        b[1], z[0],
+        z[0], b[2],
         small_y, inputs,
-        z[1], a[4], a[3],
-        skip_shares, small_z1,
-        b[2], a[5], r[0], r[1], b[4], z[2],
+        z[1], z[2],
+        skip_shares,
+        a[3], r[0], r[1],
+        small_z1,
+        a[4], b[3], r[2], z[3], b[4],
         small_z2,
-        z[4], w[0], w[1], a[6], b[5], r[2], r[4], b[3], z[5], b[6], a[7], z[3], r[5], z[6],
-        a[8], b[7], r[3], r[6], w[2], w[4], w[5], z[7], b[8], w[3], w[6], r[7], z[8], w[7],
-        r[8], w[8],
+        w[0], w[1], a[5], z[4], r[3], b[5], w[2], a[6], r[4], z[5], b[6], w[3], a[7], r[5],
+        z[6], b[7], w[4], a[8], b[8], z[7], r[6], w[5], z[8], r[7], w[6], r[8], w[7], w[8],
     ):
         step()
     for copy in state["spread"]:
@@ -1088,7 +1110,7 @@
     rows, model = resid.shape
     frames, inner = heads.shape[0], w_up.shape[1]
     utts = lengths.shape[1]
-    small = (-(-(10 + 6 * utts) // 8) * 8, model)
+    small = (-(-(10 + 6 * utts) // 16) * 16, model)
     vmem, there = everywhere(pltpu.VMEM), everywhere(pl.ANY)
     shape = jax.ShapeDtypeStruct
     bf16 = lambda *dims: pltpu.VMEM(dims, jnp.bfloat16)
@@ -1105,7 +1127,7 @@
             shape((part, model), jnp.bfloat16),
             shape((part, 3 * model), jnp.bfloat16),
             shape((2 * part, model), jnp.bfloat16),
-            shape((4,) + small, jnp.float32),
+            shape((4,) + small, jnp.bfloat16),
             shape((rows, model), jnp.bfloat16),
             shape((rows, model), jnp.bfloat16),
         ],
@@ -1141,14 +1163,14 @@
             bf16(*w_qkv.shape),
             bf16(*w_skip.shape),
             f32(*small),
-            f32(3, *small),
-            f32(2, *small),
+            bf16(3, *small),
+            bf16(3, *small),
         ]
         + share_scratch(part, inner // 8) * 4
         + share_scratch(part, model // 4)
         + share_scratch(part, 3 * model // 8) * 2
         + share_scratch(2 * part, model // 8) * 2
-        + semaphores(128)
+        + semaphores(160)
         + [pltpu.SemaphoreType.DMA((4,))],
         compiler_params=comm_params(2),
     )(
@@ -1166,10 +1188,10 @@
     kept_in, wide_in, smalls_in = rest[:3], rest[3:8], rest[8]
     kept_out, wide_out, mod_out, bias_out = rest[9:12], rest[12:17], rest[17], rest[18:24]
     kept, wide, staged = rest[24:27], rest[27:32], rest[32:37]
-    smalls_ref, mod_stage, bias_stage, d_mod, totals, sems, load_sems = rest[37:]
+    smalls_got, smalls_ref, mod_stage, bias_stage, d_mod, totals, sems, load_sems = rest[37:]
     seq = lax.axis_index("seq")
     loads, copies = [], []
-    for source, target in zip((*wide_in, smalls_in, *kept_in), (*wide, smalls_ref, *kept)):
+    for source, target in zip((*wide_in, smalls_in, *kept_in), (*wide, smalls_got, *kept)):
         copy = pltpu.make_async_copy(source, target, load_sems.at[len(loads)])
         copy.start()
         loads.append(copy)
@@ -1194,6 +1216,7 @@
         put(stage, target)
     groups = smalls_ref.shape[0]
     loads[5].wait()
+    smalls_ref[...] = smalls_got[...].astype(jnp.float32)
     bias_sum = (
         smalls_ref[0, 0:10] + smalls_ref[1, 0:10] + smalls_ref[2, 0:10] + smalls_ref[3, 0:10]
     )
@@ -1250,6 +1273,7 @@
         scratch_shapes=[pltpu.VMEM(v.shape, v.dtype) for v in (*kept, *grads)]
         + [pltpu.VMEM(g.shape, jnp.float32) for g in grads]
         + [
+            pltpu.VMEM(smalls.shape, smalls.dtype),
             pltpu.VMEM(smalls.shape, jnp.float32),
             pltpu.VMEM(mod_shape, jnp.float32),
             pltpu.VMEM((6, 8, max(widths)), jnp.float32),

time: 218 us -> 216 us (level)
    pallas_call x1, Pallas kernels: 147 us -> 144 us  [backward(): pl.pallas_call(partial(backward_kernel, utts), in_specs=[everywhere(pltpu...]
where the time goes in v7:
time: 216 us; the launch traced here: 215 us
  Pallas kernels  204 us (94%)
  other arithmetic  7.69 us (4%)
  between operations  2.67 us (1%)
    pallas_call x1, Pallas kernels, backward(): pl.pallas_call(partial(backward_kernel, utts), in_specs=[everywhere(pltpu...  144 us
    pallas_call x1, Pallas kernels, attend(): pl.pallas_call(partial(attend_kernel, utts), in_specs=[scalar] * 2 + [vme...  51.3 us
    pallas_call x1, Pallas kernels, finish(): pl.pallas_call(partial(finish_kernel, utts, shards), in_specs=[vmem] + [t...  7.86 us

profile of v7, /device:TPU:0, one launch (start us, length us, event | category | flops | bytes accessed | tf_op | source)
XLA Modules:
  0.0 215.3 jit_solution(5510205271035577925)
XLA Ops:
  0.6 0.7 pad_multiply_fusion
  1.4 1.4 fusion.30
  4.7 0.8 fusion.18.act_ref
  5.5 1.2 fusion.11
  6.7 0.7 pad_maximum_fusion.table_ref
  7.4 51.3 %shard_map.298 = (bf16[128,1024]{1,0:T(8,128)(2,1)}, bf16[1024,384]{1,0:T(8,128)(2,1)}, f32[1024,128]{1,0:T(8,128)}, f32[1024,128]{1,0:T(8,128)}, f32[128,128]{1...) custom-call(s32[1,3]{1,0:T(1,128)} %lengths_ref.3, ...), custom_call_target="tpu_custom_call" | custom-call | tf_op jit(solution)/shard_map/pallas_call | solution.py:693
  58.7 0.7 multiply_reduce_fusion
  59.5 0.1 mul.109
  59.6 0.3 fusion.9
  59.9 0.6 pad_convert_fusion.act_ref
  60.5 144.4 %shard_map.299 = (bf16[128,1024]{1,0:T(8,128)(2,1)}, bf16[512,1024]{1,0:T(8,128)(2,1)}, bf16[128,4096]{1,0:T(8,128)(2,1)}, bf16[128,1024]{1,0:T(8,128)(2,1)}, bf...) custom-call(s32[1,3]{1,0:T(1,128)} %lengths_ref.3, ...), custom_call_target="tpu_custom_call" | custom-call | tf_op jit(solution)/shard_map/pallas_call | solution.py:1119
  204.9 7.9 %shard_map.300 = (bf16[128,1024]{1,0:T(8,128)(2,1)}, bf16[128,1024]{1,0:T(8,128)(2,1)}, bf16[128,1024]{1,0:T(8,128)(2,1)}, f32[256,1024]{1,0:T(8,128)}, f32[128,...) custom-call(f32[128,16]{1,0:T(8,128)} %pad_convert_fusion.act_ref, ...), custom_call_target="tpu_custom_call" | custom-call | tf_op jit(solution)/shard_map/pallas_call | solution.py:1265
  212.8 1.3 reduce.2
  214.1 1.3 reduce.1
  (7 shorter events, 0.1 us)

commit v8 on v7

--- a/solution.py
+++ b/solution.py
@@ -457,7 +457,7 @@
 
 
 def semaphores(count):
-    return [pltpu.SemaphoreType.DMA((count,))] * 2 + [pltpu.SemaphoreType.DMA((32,))]
+    return [pltpu.SemaphoreType.DMA((count,))] * 2 + [pltpu.SemaphoreType.DMA((40,))]
 
 
 def comm_params(collective_id):
@@ -500,12 +500,12 @@
 
 
 def attend_kernel(
-    utts, lengths_ref, chars_ref, drop_ref, flow_ref, act_ref, table_ref, frames_ref, skip_ref,
+    utts, lengths_ref, chars_ref, drop_ref, act_ref, cos_in, sin_in, frames_ref, skip_ref,
     out_grad_ref,
     b_skip_ref, b_mod_ref, b_qkv_ref, w_skip_ref, w_mod_ref, w_qkv_ref,
-    attn_ref, heads_ref, exact_ref, total_ref, loss_ref, flows_ref, norm_all, joined_all,
+    attn_ref, heads_ref, exact_ref, total_ref, loss_ref, acts_ref, norm_all, joined_all,
     resid_ref, mod_ref, cos_ref, sin_ref, d_ff_ref, d_ff_all,
-    attn_heads, counts_got, sums_ref, flow_own, packed, norm_ref, w_skip, w_mod, w_qkv,
+    attn_heads, counts_got, sums_ref, packed, norm_ref, w_skip, w_mod, w_qkv,
     send_sems, recv_sems, local_sems,
 ):
     links = Links(send_sems, recv_sems, local_sems)
@@ -521,11 +521,9 @@
         Gathered(links, frames_ref, joined_all, pl.ds(0, model)),
         Gathered(links, skip_ref, joined_all, pl.ds(model, model)),
     ]
-    flow_own[...] = jnp.zeros_like(flow_own)
-    flow_own[0:1, 0:utts] = flow_ref[...]
-    flows_ref[links.utt] = flow_own[...]
-    flow_copies = [
-        links.send(flow_own, flows_ref.at[links.utt], links.mate(r)) for r in (1, 2, 3)
+    act_own = links.keep(act_ref, acts_ref.at[links.utt])
+    act_copies = [
+        links.send(act_ref, acts_ref.at[links.utt], links.mate(r)) for r in (1, 2, 3)
     ]
     tables = Frames(utts, lengths_ref)
     first_row = pl.multiple_of(links.seq * rows, rows)
@@ -560,14 +558,11 @@
 
     count_turn()
     quarter = total_rows // 4
-    for out, kind in ((cos_ref, 0), (sin_ref, 1)):
-        for j in range(4):
-            block = table_ref[kind, :, 32 * j : 32 * (j + 1)]
-            if kind == 0:
-                wide = jnp.concatenate([block] * 4, axis=1)
-            else:
-                wide = jnp.concatenate([-block, block] * 2, axis=1)
-            out[j * quarter : (j + 1) * quarter, :] = wide
+    for j in range(4):
+        here, lanes = slice(j * quarter, (j + 1) * quarter), slice(32 * j, 32 * (j + 1))
+        cosines, sines = cos_in[:, lanes], sin_in[:, lanes]
+        cos_ref[here, :] = jnp.concatenate([cosines] * 4, axis=1)
+        sin_ref[here, :] = jnp.concatenate([-sines, sines] * 2, axis=1)
     load_skip.wait()
     residual = (
         jnp.dot(frames_ref[...], w_skip[0:model, :], preferred_element_type=jnp.float32)
@@ -670,7 +665,8 @@
     own = links.keep(attn_heads.at[part(links.seq), :], column)
     gathers[2].relay()
     gathers[3].relay()
-    for copy in flow_copies:
+    act_own.wait()
+    for copy in act_copies:
         copy.wait_recv()
     own.wait()
     for copy in incoming:
@@ -681,26 +677,26 @@
 
 
 def attend(
-    lengths, chars, drop, flow, act, table, frames, skip, out_grad, b_skip, b_mod, b_qkv, w_skip,
+    lengths, chars, drop, act, cos, sin, frames, skip, out_grad, b_skip, b_mod, b_qkv, w_skip,
     w_mod, w_qkv, shards,
 ):
     rows, width = frames.shape
     total_rows = shards * rows
-    utts = flow.shape[1]
+    utts = lengths.shape[1]
     vmem, there, scalar = everywhere(pltpu.VMEM), everywhere(pl.ANY), everywhere(pltpu.SMEM)
     shape = jax.ShapeDtypeStruct
     bf16 = lambda *dims: pltpu.VMEM(dims, jnp.bfloat16)
     return pl.pallas_call(
         partial(attend_kernel, utts),
         in_specs=[scalar] * 2 + [vmem] * 10 + [there] * 3,
-        out_specs=[vmem] * 14,
+        out_specs=[vmem] * 5 + [there] * 3 + [vmem] * 5 + [there],
         out_shape=[
             shape((rows, width), jnp.bfloat16),
             shape((total_rows, 384), jnp.bfloat16),
             shape((total_rows, 128), jnp.float32),
             shape((total_rows, 128), jnp.float32),
             shape((rows, 128), jnp.float32),
-            shape((4, 8, 128), jnp.float32),
+            shape((4,) + act.shape, act.dtype),
             shape((4 * rows, width), jnp.bfloat16),
             shape((4 * rows, 2 * width), jnp.bfloat16),
             shape((rows, width), jnp.float32),
@@ -714,7 +710,6 @@
             bf16(total_rows, 128),
             pltpu.VMEM((10, 8, 128), jnp.float32),
             pltpu.VMEM((8, 128), jnp.float32),
-            pltpu.VMEM((8, 128), jnp.float32),
             bf16(shards, rows, 384),
             bf16(rows, width),
             bf16(*w_skip.shape),
@@ -724,7 +719,7 @@
         + semaphores(40),
         compiler_params=comm_params(1),
     )(
-        lengths, chars, drop, flow, act, table, frames, skip, out_grad,
+        lengths, chars, drop, act, cos, sin, frames, skip, out_grad,
         b_skip[None, :], b_mod[None, :], b_qkv[None, :], w_skip, w_mod, w_qkv,
     )
 
@@ -754,13 +749,15 @@
 def backward_kernel(
     utts, lengths_ref, attn_ref, resid_ref, mod_ref, loss_ref, out_grad_ref, d_ff,
     b_out_ref, b_up_ref, b_down_ref,
-    heads_ref, exact_ref, total_ref, cos_ref, sin_ref,
+    heads_in, exact_in, total_in, cos_in, sin_in,
     norm_a_ref, joined_ref, d_ff_ref, w_out_ref, w_up_ref, w_down_ref, w_qkv_ref, w_skip_ref,
+    mixed_out, down_out, up_out, out_out, qkv_out, skip_out, smalls_out, frames_out, skip_in_out,
     mixed, g_down, g_up, g_out, g_qkv, g_skip, smalls, g_frames, g_skip_in,
     norm_f, act, d_inner, d_branch, d_attn, pieces, d_mid, ff_sum, d_norm,
     grad_heads, d_heads, dk_ref, dv_ref,
     d_ff_all, act_all, norm_all, d_inner_all, attn_all, d_branch_all,
     norm_a_all, joined_all, d_qkv, d_qkv_all, d_resid, d_resid_all,
+    heads_ref, exact_ref, total_ref, cos_ref, sin_ref,
     up_ring, down_ring, w_out, w_qkv, w_skip, small_own, small_got, small_out,
     *rest,
 ):
@@ -790,6 +787,13 @@
     for c in (0, 1):
         for copy in ring(c):
             copy.start()
+    head_loads = [
+        links.keep(source, target)
+        for source, target in (
+            (heads_in, heads_ref), (exact_in, exact_ref), (total_in, total_ref),
+            (cos_in, cos_ref), (sin_in, sin_ref),
+        )
+    ]
     loads = [
         links.keep(w_qkv_ref, w_qkv),
         links.keep(w_skip_ref, w_skip),
@@ -923,6 +927,7 @@
     shares[1].start_far()
     ff_out = ff_sum[...] + b_down_ref[...]
     mixed[...] = (mid + modulation(5) * ff_out).astype(jnp.bfloat16)
+    saved = [links.keep(mixed, mixed_out)]
     pieces[1] = d_out() * ff_out
     small_own[...] = jnp.zeros_like(small_own)
     small_own[4:5, :] = column_sum(d_branch[...])
@@ -948,6 +953,8 @@
     own.wait()
     for copy in incoming_d:
         copy.wait_recv()
+    for copy in head_loads:
+        copy.wait()
     dk_ref[...] = jnp.zeros_like(dk_ref)
     dv_ref[...] = jnp.zeros_like(dv_ref)
     first = lax.broadcasted_iota(jnp.int32, (256, 128), 1) < HEAD_DIM
@@ -1078,6 +1085,9 @@
         mine[...] = (small_own[...] + small_got[2].astype(jnp.float32)).astype(jnp.bfloat16)
         state["spread"] = [links.send(mine, mine, links.mate(r)) for r in (2, 3, 1)]
 
+    def save(*pairs):
+        return lambda: saved.extend(links.keep(source, target) for source, target in pairs)
+
     stages = ("start", "after_a", "after_b", "after_z2", "relay", "wait")
     s, a, b, z, r, w = ([getattr(share, stage) for share in shares] for stage in stages)
     for step in (
@@ -1086,19 +1096,22 @@
         a[2], b[0], b[1],
         qkv_shares,
         z[0], b[2],
-        small_y, inputs,
+        small_y, inputs, save((g_frames, frames_out), (g_skip_in, skip_in_out)),
         z[1], z[2],
         skip_shares,
         a[3], r[0], r[1],
         small_z1,
         a[4], b[3], r[2], z[3], b[4],
         small_z2,
-        w[0], w[1], a[5], z[4], r[3], b[5], w[2], a[6], r[4], z[5], b[6], w[3], a[7], r[5],
-        z[6], b[7], w[4], a[8], b[8], z[7], r[6], w[5], z[8], r[7], w[6], r[8], w[7], w[8],
+        w[0], w[1], save((g_down, down_out)), a[5], z[4], r[3], b[5], w[2], a[6], r[4], z[5], b[6], w[3], save((g_up, up_out)), a[7], r[5],
+        z[6], b[7], w[4], save((g_out, out_out)), a[8], b[8], z[7], r[6], w[5], z[8], r[7], w[6], save((g_qkv, qkv_out)), r[8], w[7], w[8], save((g_skip, skip_out)),
     ):
         step()
     for copy in state["spread"]:
         copy.wait_recv()
+    save((smalls, smalls_out))()
+    for copy in saved:
+        copy.wait()
     links.leave()
 
 
@@ -1116,22 +1129,24 @@
     bf16 = lambda *dims: pltpu.VMEM(dims, jnp.bfloat16)
     f32 = lambda *dims: pltpu.VMEM(dims, jnp.float32)
     part, step = model // 8, inner // 8
+    outs = [
+        shape((rows, model), jnp.bfloat16),
+        shape((inner // 8, model), jnp.bfloat16),
+        shape((part, inner), jnp.bfloat16),
+        shape((part, model), jnp.bfloat16),
+        shape((part, 3 * model), jnp.bfloat16),
+        shape((2 * part, model), jnp.bfloat16),
+        shape((4,) + small, jnp.bfloat16),
+        shape((rows, model), jnp.bfloat16),
+        shape((rows, model), jnp.bfloat16),
+    ]
     return pl.pallas_call(
         partial(backward_kernel, utts),
-        in_specs=[everywhere(pltpu.SMEM)] + [vmem] * 14 + [there] * 8,
-        out_specs=[vmem] * 9,
-        out_shape=[
-            shape((rows, model), jnp.bfloat16),
-            shape((inner // 8, model), jnp.bfloat16),
-            shape((part, inner), jnp.bfloat16),
-            shape((part, model), jnp.bfloat16),
-            shape((part, 3 * model), jnp.bfloat16),
-            shape((2 * part, model), jnp.bfloat16),
-            shape((4,) + small, jnp.bfloat16),
-            shape((rows, model), jnp.bfloat16),
-            shape((rows, model), jnp.bfloat16),
-        ],
-        scratch_shapes=[
+        in_specs=[everywhere(pltpu.SMEM)] + [vmem] * 9 + [there] * 13,
+        out_specs=[there] * 9,
+        out_shape=outs,
+        scratch_shapes=[pltpu.VMEM(out.shape, out.dtype) for out in outs]
+        + [
             bf16(rows, model),
             bf16(4, rows, inner // 4),
             bf16(4, rows, inner // 4),
@@ -1157,6 +1172,11 @@
             bf16(4 * rows, 3 * model // 4),
             bf16(rows, model),
             bf16(4 * rows, model // 4),
+            bf16(frames, 384),
+            f32(frames, 128),
+            f32(frames, 128),
+            f32(frames, 128),
+            f32(frames, 128),
             bf16(2, model, step),
             bf16(2, step, model),
             bf16(*w_out.shape),
@@ -1184,14 +1204,18 @@
 UP = 3
 
 
-def finish_kernel(utts, shards, act_ref, *rest):
-    kept_in, wide_in, smalls_in = rest[:3], rest[3:8], rest[8]
+def finish_kernel(utts, shards, *rest):
+    kept_in, wide_in, smalls_in, act_in = rest[:3], rest[3:8], rest[8], rest[9]
+    rest = rest[1:]
     kept_out, wide_out, mod_out, bias_out = rest[9:12], rest[12:17], rest[17], rest[18:24]
     kept, wide, staged = rest[24:27], rest[27:32], rest[32:37]
-    smalls_got, smalls_ref, mod_stage, bias_stage, d_mod, totals, sems, load_sems = rest[37:]
+    smalls_got, act_got, bias_stage = rest[37], rest[38], rest[39:45]
+    smalls_ref, act_rows, mod_stage, d_mod, totals, sems, load_sems = rest[45:]
     seq = lax.axis_index("seq")
     loads, copies = [], []
-    for source, target in zip((*wide_in, smalls_in, *kept_in), (*wide, smalls_got, *kept)):
+    for source, target in zip(
+        (*wide_in, smalls_in, act_in, *kept_in), (*wide, smalls_got, act_got, *kept)
+    ):
         copy = pltpu.make_async_copy(source, target, load_sems.at[len(loads)])
         copy.start()
         loads.append(copy)
@@ -1217,6 +1241,14 @@
     groups = smalls_ref.shape[0]
     loads[5].wait()
     smalls_ref[...] = smalls_got[...].astype(jnp.float32)
+    loads[6].wait()
+    act_rows[...] = jnp.zeros_like(act_rows)
+    own = act_rows.shape[1]
+    own_columns = pl.ds(pl.multiple_of(seq * own, own), own)
+    for g in range(groups):
+        act_rows[g * utts : (g + 1) * utts, :] = act_got[g, :, own_columns].astype(jnp.float32)[
+            0:utts
+        ]
     bias_sum = (
         smalls_ref[0, 0:10] + smalls_ref[1, 0:10] + smalls_ref[2, 0:10] + smalls_ref[3, 0:10]
     )
@@ -1230,72 +1262,69 @@
         rows = d_mod[piece]
         totals[10 + piece, 0:1] = jnp.sum(rows, axis=0, keepdims=True)
         columns = slice(piece * model, (piece + 1) * model)
-        mod_stage[:, columns] = jnp.dot(
-            act_ref[...], rows, precision=HIGHEST_PRECISION, preferred_element_type=jnp.float32
+        mod_stage[:, columns] = lax.dot_general(
+            act_rows[...],
+            rows,
+            DOWN,
+            precision=HIGHEST_PRECISION,
+            preferred_element_type=jnp.float32,
         )
     put(mod_stage, mod_out)
-    for load, source, target in zip(loads[6:], kept, kept_out):
+    for load, source, target in zip(loads[7:], kept, kept_out):
         load.wait()
         put(source, target)
     line = model // lanes
     first = 0
     for place, target in enumerate(bias_out):
-        count = target.shape[1] // lanes
+        count = target.shape[0] // lanes
         for i in range(count):
             unit = i * line + seq if place == UP else seq * count + i
             column = pl.multiple_of((unit % line) * lanes, lanes)
-            bias_stage[place, 0:1, i * lanes : (i + 1) * lanes] = totals[
-                first + unit // line, 0:1, pl.ds(column, lanes)
+            bias_stage[place][i * lanes : (i + 1) * lanes] = totals[
+                first + unit // line, 0, pl.ds(column, lanes)
             ]
         first += count * shards // line
-        put(bias_stage.at[place, pl.ds(0, 1), pl.ds(0, count * lanes)], target)
+        put(bias_stage[place], target)
     for copy in copies:
         copy.wait()
 
 
-def finish(shards, utts, act_own, smalls, mixed, frames, skip, grads):
-    vmem, there = everywhere(pltpu.VMEM), everywhere(pl.ANY)
+def finish(shards, utts, acts, smalls, mixed, frames, skip, grads):
+    there = everywhere(pl.ANY)
     shape = jax.ShapeDtypeStruct
     model = smalls.shape[2]
     own = model // shards
-    depth = act_own.shape[1]
+    depth = -(-acts.shape[0] * utts // 8) * 8
     mod_shape = (own, 6 * model)
     widths = [own, 3 * own, own, 4 * own, own, 6 * own]
     kept = (mixed, frames, skip)
     outs = pl.pallas_call(
         partial(finish_kernel, utts, shards),
-        in_specs=[vmem] + [there] * 9,
+        in_specs=[there] * 10,
         out_specs=[there] * 15,
         out_shape=[shape(v.shape, v.dtype) for v in kept]
         + [shape(g.shape, jnp.float32) for g in grads]
         + [shape(mod_shape, jnp.float32)]
-        + [shape((1, w), jnp.float32) for w in widths],
+        + [shape((w,), jnp.float32) for w in widths],
         scratch_shapes=[pltpu.VMEM(v.shape, v.dtype) for v in (*kept, *grads)]
         + [pltpu.VMEM(g.shape, jnp.float32) for g in grads]
         + [
             pltpu.VMEM(smalls.shape, smalls.dtype),
+            pltpu.VMEM(acts.shape, acts.dtype),
+        ]
+        + [pltpu.VMEM((w,), jnp.float32) for w in widths]
+        + [
             pltpu.VMEM(smalls.shape, jnp.float32),
+            pltpu.VMEM((depth, own), jnp.float32),
             pltpu.VMEM(mod_shape, jnp.float32),
-            pltpu.VMEM((6, 8, max(widths)), jnp.float32),
             pltpu.VMEM((6, depth, model), jnp.float32),
             pltpu.VMEM((16, 8, model), jnp.float32),
             pltpu.SemaphoreType.DMA((15,)),
-            pltpu.SemaphoreType.DMA((9,)),
+            pltpu.SemaphoreType.DMA((10,)),
         ],
         compiler_params=pltpu.CompilerParams(vmem_limit_bytes=VMEM_LIMIT),
-    )(act_own, *kept, *grads, smalls)
-    return outs[:9], [v.reshape(-1) for v in outs[9:]]
-
-
-def own_time_act(flows, seq_place, shards, model):
-    half_dim, own = model // 2, model // shards
-    column = seq_place * own + jnp.arange(own, dtype=jnp.int32)
-    inverse = jnp.exp(
-        -math.log(10000.0) * (column % half_dim).astype(jnp.float32) / half_dim
-    )
-    angles = 1000.0 * flows[None, :] * inverse[:, None]
-    wave = jnp.where((column < half_dim)[:, None], jnp.sin(angles), jnp.cos(angles))
-    return jax.nn.silu(wave).astype(jnp.bfloat16).astype(jnp.float32)
+    )(*kept, *grads, smalls, acts)
+    return outs[:9], outs[9:]
 
 
 def compact_tables(lengths, total_rows):
@@ -1311,7 +1340,7 @@
         -math.log(10000.0) * 2.0 * (lane % half_dim).astype(jnp.float32) / HEAD_DIM
     )
     angles = (frame - start).astype(jnp.float32) * inverse
-    return jnp.stack([jnp.cos(angles), jnp.sin(angles)])
+    return jnp.cos(angles), jnp.sin(angles)
 
 
 def padded_time_act(flow_vals, model):
@@ -1381,15 +1410,14 @@
         qkv_full = jnp.dot(norm_a, w_qkv, preferred_element_type=jnp.float32) + b_qkv
     if fused:
         (
-            attn_b, qkv_heads, exact, total, loss, flows, norm_all, joined_all,
+            attn_b, qkv_heads, exact, total, loss, acts, norm_all, joined_all,
             residual, mod_u, cos_all, sin_all, d_ff, d_ff_all,
         ) = attend(
             frame_lengths,
             char_lengths,
             drop_mask,
-            flow_times,
             padded_time_act(flow_times[0], model_width),
-            compact_tables(lengths, local_rows * shards),
+            *compact_tables(lengths, local_rows * shards),
             frames_in[0],
             skip_in[0],
             out_grad[0],
@@ -1460,12 +1488,10 @@
             w_skip,
         )
         utts = flow_times.shape[1]
-        act_own = own_time_act(flows[:, 0, :utts].reshape(-1), seq_place, shards, model_width)
-        act_own = jnp.pad(act_own, ((0, 0), (0, -act_own.shape[1] % 8)))
         wide, biases = finish(
             shards,
             utts,
-            act_own,
+            acts,
             smalls,
             mixed,
             g_frames,

time: 216 us -> 214 us (level)
  other arithmetic: 7.69 us -> 3.38 us
    pallas_call x1, Pallas kernels: 144 us -> 147 us  [backward(): pl.pallas_call(partial(backward_kernel, utts), in_specs=[everywhere(pltpu...]
    pallas_call x2 -> x0, other arithmetic: 2.56 us -> none  [finish(): pl.pallas_call(partial(finish_kernel, utts, shards), in_specs=[vmem] + [t...]
where the time goes in v8:
time: 214 us; the launch traced here: 213 us
  Pallas kernels  205 us (96%)
  other arithmetic  3.38 us (2%)
  between operations  2.83 us (1%)
    pallas_call x1, Pallas kernels, backward(): pl.pallas_call(partial(backward_kernel, utts), in_specs=[everywhere(pltpu...  147 us
    pallas_call x1, Pallas kernels, attend(): pl.pallas_call(partial(attend_kernel, utts), in_specs=[scalar] * 2 + [vme...  50.7 us
    pallas_call x1, Pallas kernels, finish(): pl.pallas_call(partial(finish_kernel, utts, shards), in_specs=[there] * 1...  7.11 us

profile of v8, /device:TPU:0, one launch (start us, length us, event | category | flops | bytes accessed | tf_op | source)
XLA Modules:
  0.0 212.6 jit_solution(7851554865414863119)
XLA Ops:
  0.6 0.7 pad_multiply_fusion
  1.3 1.4 fusion.18
  4.7 0.8 fusion.11.act_ref
  5.5 1.9 fusion.3
  7.3 50.7 %shard_map.298 = (bf16[128,1024]{1,0:T(8,128)(2,1)}, bf16[1024,384]{1,0:T(8,128)(2,1)}, f32[1024,128]{1,0:T(8,128)}, f32[1024,128]{1,0:T(8,128)}, f32[128,128]{1...) custom-call(s32[1,3]{1,0:T(1,128)} %lengths_ref.3, ...), custom_call_target="tpu_custom_call" | custom-call | tf_op jit(solution)/shard_map/pallas_call | solution.py:689
  58.1 147.2 %shard_map.299 = (bf16[128,1024]{1,0:T(8,128)(2,1)}, bf16[512,1024]{1,0:T(8,128)(2,1)}, bf16[128,4096]{1,0:T(8,128)(2,1)}, bf16[128,1024]{1,0:T(8,128)(2,1)}, bf...) custom-call(s32[1,3]{1,0:T(1,128)} %lengths_ref.3, ...), custom_call_target="tpu_custom_call" | custom-call | tf_op jit(solution)/shard_map/pallas_call | solution.py:1143
  205.3 7.1 %shard_map.300 = (bf16[128,1024]{1,0:T(8,128)(2,1)}, bf16[128,1024]{1,0:T(8,128)(2,1)}, bf16[128,1024]{1,0:T(8,128)(2,1)}, f32[256,1024]{1,0:T(8,128)}, f32[128,...) custom-call(bf16[128,1024]{1,0:T(8,128)(2,1)} %get-tuple-element.66., ...), custom_call_target="tpu_custom_call" | custom-call | tf_op jit(solution)/shard_map/pallas_call | solution.py:1301
  (5 shorter events, 0.0 us)

commit v9 on v8

--- a/solution.py
+++ b/solution.py
@@ -916,7 +916,7 @@
         (joined_all, d_resid_all, pl.ds(0, slim), column_at(g_skip, thin, 0, slim)),
         (joined_all, d_resid_all, pl.ds(slim, slim), column_at(g_skip, thin, slim, slim)),
     ]
-    y_first = (True, False, True, True, True, True, True, True, True)
+    y_first = (True,) * 9
     shares = [
         Share(links, y_first[i], left, right, columns, *tiles[4 * i : 4 * i + 4], result)
         for i, (left, right, columns, result) in enumerate(plans)

time: 214 us -> 209 us (0.977)
  Pallas kernels: 205 us -> 201 us
    pallas_call x1, Pallas kernels: 147 us -> 143 us  [backward(): pl.pallas_call(partial(backward_kernel, utts), in_specs=[everywhere(pltpu...]
where the time goes in v9:
time: 209 us; the launch traced here: 208 us
  Pallas kernels  201 us (96%)
  other arithmetic  3.38 us (2%)
  between operations  2.83 us (1%)
    pallas_call x1, Pallas kernels, backward(): pl.pallas_call(partial(backward_kernel, utts), in_specs=[everywhere(pltpu...  143 us
    pallas_call x1, Pallas kernels, attend(): pl.pallas_call(partial(attend_kernel, utts), in_specs=[scalar] * 2 + [vme...  50.7 us
    pallas_call x1, Pallas kernels, finish(): pl.pallas_call(partial(finish_kernel, utts, shards), in_specs=[there] * 1...  7.11 us

profile of v9, /device:TPU:0, one launch (start us, length us, event | category | flops | bytes accessed | tf_op | source)
XLA Modules:
  0.0 208.1 jit_solution(6068656921120238156)
XLA Ops:
  0.6 0.7 pad_multiply_fusion
  1.3 1.4 fusion.18
  4.7 0.8 fusion.11.act_ref
  5.5 1.9 fusion.3
  7.3 50.7 %shard_map.298 = (bf16[128,1024]{1,0:T(8,128)(2,1)}, bf16[1024,384]{1,0:T(8,128)(2,1)}, f32[1024,128]{1,0:T(8,128)}, f32[1024,128]{1,0:T(8,128)}, f32[128,128]{1...) custom-call(s32[1,3]{1,0:T(1,128)} %lengths_ref.3, ...), custom_call_target="tpu_custom_call" | custom-call | tf_op jit(solution)/shard_map/pallas_call | solution.py:689
  58.1 142.7 %shard_map.299 = (bf16[128,1024]{1,0:T(8,128)(2,1)}, bf16[512,1024]{1,0:T(8,128)(2,1)}, bf16[128,4096]{1,0:T(8,128)(2,1)}, bf16[128,1024]{1,0:T(8,128)(2,1)}, bf...) custom-call(s32[1,3]{1,0:T(1,128)} %lengths_ref.3, ...), custom_call_target="tpu_custom_call" | custom-call | tf_op jit(solution)/shard_map/pallas_call | solution.py:1143
  200.8 7.1 %shard_map.300 = (bf16[128,1024]{1,0:T(8,128)(2,1)}, bf16[128,1024]{1,0:T(8,128)(2,1)}, bf16[128,1024]{1,0:T(8,128)(2,1)}, f32[256,1024]{1,0:T(8,128)}, f32[128,...) custom-call(bf16[128,1024]{1,0:T(8,128)(2,1)} %get-tuple-element.66., ...), custom_call_target="tpu_custom_call" | custom-call | tf_op jit(solution)/shard_map/pallas_call | solution.py:1301
  (5 shorter events, 0.0 us)

commit v10 on v9

--- a/solution.py
+++ b/solution.py
@@ -514,8 +514,6 @@
     early, late = pl.ds(0, 2 * model), pl.ds(2 * model, 4 * model)
     load_skip = links.keep(w_skip_ref, w_skip)
     load_early = links.keep(w_mod_ref.at[:, early], w_mod.at[:, early])
-    load_qkv = links.keep(w_qkv_ref, w_qkv)
-    load_late = links.keep(w_mod_ref.at[:, late], w_mod.at[:, late])
     links.enter((1, 2, 3), range(1, 8))
     gathers = [
         Gathered(links, frames_ref, joined_all, pl.ds(0, model)),
@@ -564,6 +562,7 @@
         cos_ref[here, :] = jnp.concatenate([cosines] * 4, axis=1)
         sin_ref[here, :] = jnp.concatenate([-sines, sines] * 2, axis=1)
     load_skip.wait()
+    load_qkv = links.keep(w_qkv_ref, w_qkv)
     residual = (
         jnp.dot(frames_ref[...], w_skip[0:model, :], preferred_element_type=jnp.float32)
         + jnp.dot(skip_ref[...], w_skip[model:, :], preferred_element_type=jnp.float32)
@@ -579,6 +578,7 @@
         )
 
     load_early.wait()
+    load_late = links.keep(w_mod_ref.at[:, late], w_mod.at[:, late])
     modulate_columns(slice(0, 2 * model))
     unit, _ = normal_parts(residual)
     norm_ref[...] = (

time: 209 us -> 209 us (level)
  no operation moved by 1% of the time
where the time goes in v10:
time: 209 us; the launch traced here: 208 us
  Pallas kernels  201 us (96%)
  other arithmetic  3.38 us (2%)
  between operations  2.83 us (1%)
    pallas_call x1, Pallas kernels, backward(): pl.pallas_call(partial(backward_kernel, utts), in_specs=[everywhere(pltpu...  143 us
    pallas_call x1, Pallas kernels, attend(): pl.pallas_call(partial(attend_kernel, utts), in_specs=[scalar] * 2 + [vme...  50.7 us
    pallas_call x1, Pallas kernels, finish(): pl.pallas_call(partial(finish_kernel, utts, shards), in_specs=[there] * 1...  7.11 us

profile of v10, /device:TPU:0, one launch (start us, length us, event | category | flops | bytes accessed | tf_op | source)
XLA Modules:
  0.0 208.1 jit_solution(6711619547908414431)
XLA Ops:
  0.6 0.7 pad_multiply_fusion
  1.3 1.4 fusion.18
  4.7 0.8 fusion.11.act_ref
  5.5 1.9 fusion.3
  7.3 50.7 %shard_map.298 = (bf16[128,1024]{1,0:T(8,128)(2,1)}, bf16[1024,384]{1,0:T(8,128)(2,1)}, f32[1024,128]{1,0:T(8,128)}, f32[1024,128]{1,0:T(8,128)}, f32[128,128]{1...) custom-call(s32[1,3]{1,0:T(1,128)} %lengths_ref.3, ...), custom_call_target="tpu_custom_call" | custom-call | tf_op jit(solution)/shard_map/pallas_call | solution.py:689
  58.1 142.7 %shard_map.299 = (bf16[128,1024]{1,0:T(8,128)(2,1)}, bf16[512,1024]{1,0:T(8,128)(2,1)}, bf16[128,4096]{1,0:T(8,128)(2,1)}, bf16[128,1024]{1,0:T(8,128)(2,1)}, bf...) custom-call(s32[1,3]{1,0:T(1,128)} %lengths_ref.3, ...), custom_call_target="tpu_custom_call" | custom-call | tf_op jit(solution)/shard_map/pallas_call | solution.py:1143
  200.8 7.1 %shard_map.300 = (bf16[128,1024]{1,0:T(8,128)(2,1)}, bf16[128,1024]{1,0:T(8,128)(2,1)}, bf16[128,1024]{1,0:T(8,128)(2,1)}, f32[256,1024]{1,0:T(8,128)}, f32[128,...) custom-call(bf16[128,1024]{1,0:T(8,128)(2,1)} %get-tuple-element.66., ...), custom_call_target="tpu_custom_call" | custom-call | tf_op jit(solution)/shard_map/pallas_call | solution.py:1301
  (5 shorter events, 0.0 us)
